TPU v7x, 32 devices: a whole 2x2x4 slice. The times are simulated.
32 devices in a mesh: member: 2 (over x), wave: 8 (over z, y), lev: 2 (over core).
Axes of the slice: x: 2, y: 2, z: 4, core: 2. Of those that a mesh axis runs over, the one named last changes fastest.
Arguments:
- grid: bfloat16 [128, 320, 2, 1280], P(('member', 'lev'), 'wave'), parts along dimension 0, may hold values from -6 to 6
- lat_order: int32 [320], replicated, may hold values from 0 to 319, each once
- wave_order: int32 [640], replicated, may hold values from 0 to 639, as said below
- trim: int32 [640], replicated, may hold values from 0 to 4, as said below
- legendre: bfloat16 [640, 640, 320], P('wave'), may hold values from -0.3125 to 0.3125
- modes_in: bfloat16 [64, 64], replicated, may hold values from -0.75 to 0.75
- modes_out: bfloat16 [64, 64], replicated, may hold values from -0.75 to 0.75
- implicit: float32 [64], replicated, may hold values from 0.3 to 30
Outputs:
- fourier_out: bfloat16 [128, 320, 2, 1280], P(('member', 'lev'), 'wave'), parts along dimension 0
There are 2 independent parts, one for each index of `member`. A program takes and returns all parts, laid end to end along the dimension named above; an argument that names none is the same for every part. Nothing has to cross between parts.
Inputs may be any that keep to these rules, and one draw needn't show every extreme that they name: `wave_order`: a permutation of 0 to 639 in which entries 2i and 2i+1 are k and 639-k for some k. `trim`: for wavenumber m, how many blocks of 64 latitudes nearest each pole take no part in its products.
All inputs are finite; a program needn't handle non-finite values.
Results may differ from a plain program's by a relative error of at most 0.015.
Values may be sent and summed in bfloat16 or wider, within the bound.
No kernel may reach another device: no remote copies, remote signals or barrier semaphores. Data moves between devices by JAX's collectives and lax.ppermute only.
A program may use at most 192 MiB of HBM per device.

v0:
```python
import math

import jax
import jax.numpy as jnp
from jax import lax
from jax.sharding import PartitionSpec as P

LBLK = 64


def fourier_table(wave_order, lon_count):
    longitude = jnp.arange(lon_count, dtype=jnp.int32)
    phase_int = longitude[:, None] * wave_order[None, :] % lon_count
    angles = phase_int.astype(jnp.float32) * (2.0 * math.pi / lon_count)
    dft_table = jnp.stack([jnp.cos(angles), -jnp.sin(angles)], 2) * (1.0 / math.sqrt(lon_count))
    return dft_table.reshape(lon_count, 2 * wave_order.shape[0])


def keep_masks(wavenum, trim, row_count, lat_count):
    row_index = jnp.arange(row_count, dtype=jnp.int32)
    latitude = jnp.arange(lat_count, dtype=jnp.int32)
    row_keep = wavenum[:, None] + row_index[None, :] < row_count
    lat_keep = latitude[None, :] >= LBLK * trim[wavenum][:, None]
    return (row_keep, lat_keep)


def forward(received, legendre_part, row_keep, lat_keep, fields):
    wave_count, row_count, lat_count = legendre_part.shape
    columns_in = received.reshape(fields, lat_count, 2, wave_count, 2).transpose(3, 2, 1, 4, 0)
    columns_in = columns_in.reshape(wave_count, 2, lat_count, 2 * fields)
    columns_in = jnp.where(lat_keep[:, None, :, None], columns_in, jnp.zeros((), jnp.bfloat16))
    paired = legendre_part.reshape(wave_count, row_count // 2, 2, lat_count)
    coeffs = jnp.einsum("wael,welx->waex", paired, columns_in, preferred_element_type=jnp.float32)
    rows_ok = row_keep.reshape(wave_count, row_count // 2, 2)[..., None]
    coeffs = jnp.where(rows_ok, coeffs, jnp.float32(0.0))
    return coeffs.astype(jnp.bfloat16).reshape(wave_count, row_count // 2, 2, 2, fields)


def vertical(coeffs, wavenum, modes_in, modes_out, implicit):
    wave_count = coeffs.shape[0]
    row_count = coeffs.shape[1] * 2
    degree = (wavenum[:, None] + jnp.arange(row_count, dtype=jnp.int32)[None, :]).astype(
        jnp.float32
    )
    factor = (degree * (degree + 1.0) / float(row_count * (row_count - 1))).reshape(
        wave_count, row_count // 2, 2
    )
    modal_part = jnp.einsum("waecl,kl->waeck", coeffs, modes_in, preferred_element_type=jnp.float32)
    scaled = (modal_part / (1.0 + factor[..., None, None] * implicit)).astype(jnp.bfloat16)
    solved = jnp.einsum("waeck,lk->waecl", scaled, modes_out, preferred_element_type=jnp.float32)
    return solved.astype(jnp.bfloat16)


def inverse(solved, legendre_part, lat_keep, fields):
    wave_count, half_rows = (solved.shape[0], solved.shape[1])
    lat_count = legendre_part.shape[2]
    paired = legendre_part.reshape(wave_count, half_rows, 2, lat_count)
    flattened = solved.reshape(wave_count, half_rows, 2, 2 * fields)
    parity_sums = jnp.einsum(
        "wael,waex->welx", paired, flattened, preferred_element_type=jnp.float32
    )
    parity_sums = jnp.where(lat_keep[:, None, :, None], parity_sums, jnp.float32(0.0))
    north_side = parity_sums[:, 0] + parity_sums[:, 1]
    south_side = parity_sums[:, 0] - parity_sums[:, 1]
    hemispheres = jnp.stack([north_side, south_side], 2).astype(jnp.bfloat16)
    hemispheres = hemispheres.reshape(wave_count, lat_count, 2, 2, fields).transpose(4, 1, 2, 0, 3)
    return hemispheres.reshape(fields, lat_count, 2, 2 * wave_count)


def local(grid, lat_order, wave_order, trim, legendre, modes_in, modes_out, implicit):
    half_fields, lat_pairs, lon_count = (grid.shape[0], grid.shape[1], grid.shape[3])
    per_device = legendre.shape[0]
    row_count, lat_count = (legendre.shape[1], legendre.shape[2])
    inverse_order = (
        jnp.zeros((lat_count,), jnp.int32).at[lat_order].set(jnp.arange(lat_count, dtype=jnp.int32))
    )
    dft_table = fourier_table(wave_order, lon_count)
    upper_part = dft_table.astype(jnp.bfloat16)
    lower_part = (dft_table - upper_part.astype(jnp.float32)).astype(jnp.bfloat16)
    grid_rows = grid.reshape(-1, lon_count)
    spectra = jnp.dot(grid_rows, upper_part, preferred_element_type=jnp.float32)
    spectra = (spectra + jnp.dot(grid_rows, lower_part, preferred_element_type=jnp.float32)).astype(
        jnp.bfloat16
    )
    spectra = (
        lax.optimization_barrier(spectra).astype(jnp.float32).reshape(half_fields, lat_pairs, 2, -1)
    )
    symmetric = jnp.stack(
        [spectra[:, :, 0] + spectra[:, :, 1], spectra[:, :, 0] - spectra[:, :, 1]], 2
    ).astype(jnp.bfloat16)
    first_slot = lax.axis_index("wave") * per_device
    my_waves = lax.dynamic_slice_in_dim(wave_order, first_slot, per_device)
    levels = lax.axis_size("lev")
    lev_share = per_device // levels
    offset = lax.axis_index("lev") * lev_share
    row_keep, lat_keep = keep_masks(my_waves, trim, row_count, lat_count)
    received = lax.all_to_all(symmetric, "wave", split_axis=3, concat_axis=1, tiled=True)
    received = jnp.take(received, inverse_order, axis=1)
    coeffs = forward(received, legendre, row_keep, lat_keep, half_fields)
    gathered = lax.all_to_all(coeffs, "lev", split_axis=0, concat_axis=4, tiled=True)
    wavenum = lax.dynamic_slice_in_dim(my_waves, offset, lev_share)
    solved = vertical(gathered, wavenum, modes_in, modes_out, implicit)
    returned = lax.all_to_all(solved, "lev", split_axis=4, concat_axis=0, tiled=True)
    result = inverse(returned, legendre, lat_keep, half_fields)
    result = jnp.take(result, lat_order, axis=1)
    fourier_out = lax.all_to_all(result, "wave", split_axis=1, concat_axis=3, tiled=True)
    return fourier_out


def solution(mesh):
    in_specs = (
        P(("member", "lev"), "wave", None, None),
        P(),
        P(),
        P(),
        P("wave", None, None),
        P(),
        P(),
        P(),
    )
    out_specs = P(("member", "lev"), "wave", None, None)
    return jax.shard_map(local, mesh=mesh, in_specs=in_specs, out_specs=out_specs, check_vma=False)
```

profile of v0, /device:TPU:0, one launch (start us, length us, event | category | flops | bytes accessed | tf_op | source)
XLA Modules:
  0.0 914.3 jit_solution(9252496254895439674)
XLA Ops:
  0.0 14.0 %fusion.18 = (f32[1280,640,1]{1,0,2:T(8,128)S(1)}, f32[1280,640,1]{1,0,2:T(8,128)S(1)}) fusion(s32[640]{0:T(1024)} %param.12), kind=kLoop, calls=%fused_computation.38 | loop fusion | flops 8192000 | bytes 6556160 | tf_op jit(solution)/shard_map/cos | solution.py:15
  34.5 14.2 %reshape.250 = bf16[2560,1280]{1,0:T(8,128)(2,1)} reshape(bf16[32,40,2,1280]{3,2,1,0:T(2,128)(2,1)} %param.10) | data formatting | bytes 13107200 | tf_op jit(solution)/shard_map/reshape | solution.py:80
  64.0 15.1 %fusion.27 = f32[1280,2560]{1,0:T(8,128)} fusion(bf16[1280,1280]{0,1:T(8,128)(2,1)} %convert_element_type.83, bf16[2560,1280]{1,0:T(8,128)(2,1)} %reshape.250), kind=kOutput, calls=%fused_computation.59 | convolution fusion | flops 8388608000 | bytes 22937600 | tf_op jit(solution)/shard_map/dot_general | solution.py:81
  79.1 14.5 %fusion.6 = bf16[2560,1280]{0,1:T(8,128)(2,1)} fusion(f32[1280,2560]{1,0:T(8,128)} %fusion.27, bf16[1280,1280]{0,1:T(8,128)(2,1)} %convert_element_type.86, bf16[2560,1280]{1,0:T(8,128)(2,1)S(1)} %bitcast.80), kind=kOutput, calls=%fused_computation.16 | convolution fusion | flops 8395161600 | bytes 29491200 | tf_op jit(solution)/shard_map/dot_general | solution.py:82
  104.2 15.7 %reshape.260 = f32[32,40,2,1280]{3,2,1,0:T(2,128)} reshape(f32[2560,1280]{1,0:T(8,128)} %copy.70) | data formatting | bytes 26214400 | tf_op jit(solution)/shard_map/reshape | solution.py:86
  119.9 17.0 %add_convert_fusion.1 = (bf16[32,40,1,1280]{3,2,1,0:T(2,128)(2,1)S(1)}, bf16[32,40,1,1280]{3,2,1,0:T(2,128)(2,1)S(1)}) fusion(f32[32,40,2,1280]{3,2,1,0:T(2,128)} %reshape.260), kind=kLoop, calls=%fused_computation.27 | loop fusion | flops 6553600 | bytes 19660800 | tf_op jit(solution)/shard_map/convert.5
  136.9 16.0 %pad_maximum_fusion.1 = bf16[32,40,2,1280]{3,2,1,0:T(2,128)(2,1)} fusion(bf16[32,40,1,1280]{3,2,1,0:T(2,128)(2,1)S(1)} %get-tuple-element.11, bf16[32,40,1,1280]{3,2,1,0:T(2,128)(2,1)S(1)} %get-tuple-element.10), kind=kLoop, calls=%fused_computation.25 | loop fusion | flops 13107200 | bytes 13107200 | tf_op jit(solution)/shard_map/stack | solution.py:88
  152.9 32.9 %copy.71 = bf16[32,40,2,1280]{1,0,2,3:T(8,128)(2,1)} copy(bf16[32,40,2,1280]{3,2,1,0:T(2,128)(2,1)} %pad_maximum_fusion.1) | data formatting | bytes 13107200 | tf_op jit(solution)/shard_map/stack | solution.py:88
  185.7 34.8 %reshape.306 = bf16[8,2,204800]{2,1,0:T(2,128)(2,1)} reshape(bf16[1280,2,32,40]{3,2,1,0:T(8,128)(2,1)} %bitcast.66) | data formatting | bytes 13107200
  227.9 47.9 %copy.76 = bf16[80,640,320]{2,0,1:T(8,128)(2,1)} copy(bf16[80,640,320]{1,2,0:T(8,128)(2,1)} %param.14) | data formatting | bytes 65536000 | tf_op args[4]
  286.6 85.1 %all-to-all-done = bf16[8,2,204800]{2,1,0:T(2,128)(2,1)} async-done(((bf16[8,2,204800]{2,1,0:T(2,128)(2,1)}), bf16[8,2,204800]{2,1,0:T(2,128)(2,1)}, u32[]{:S(2)}, u32[]{:S(2)}) %all-to-all-start) | async-done | bytes 6553632 | tf_op jit(solution)/shard_map/all_to_all | solution.py:97
  371.7 36.1 %reshape.307 = bf16[1280,2,32,40]{3,2,1,0:T(8,128)(2,1)} reshape(bf16[8,2,204800]{2,1,0:T(2,128)(2,1)} %all-to-all-done) | data formatting | bytes 13107200
  407.8 29.9 %copy.89 = bf16[32,40,2,8,160]{4,0,2,1,3:T(8,128)(2,1)} copy(bf16[32,40,2,8,160]{1,0,2,4,3:T(8,128)(2,1)} %bitcast.67) | data formatting | bytes 13107200 | tf_op jit(solution)/shard_map/all_to_all | solution.py:97
  437.7 14.6 %gather_fusion.1 = bf16[320,32,2,160]{3,1,2,0:T(8,128)(2,1)} fusion(bf16[32,320,2,160]{3,0,2,1:T(8,128)(2,1)} %bitcast.69, s32[1024]{0:T(1024)S(1)} %pad_clamp_fusion.1), kind=kCustom, calls=%fused_computation.clone | custom fusion | bytes 13108480 | tf_op jit(solution)/shard_map/jit(_take)/gather | solution.py:98
  462.6 17.0 %copy.74 = bf16[32,320,2,160]{1,0,3,2:T(8,128)(2,1)} copy(bf16[32,320,2,160]{3,0,2,1:T(8,128)(2,1)} %select_bitcast_fusion.2) | data formatting | bytes 13107200 | tf_op jit(solution)/shard_map/jit(_take)/select_n | solution.py:98
  479.7 28.6 %fusion.4 = bf16[80,320,2,64]{1,3,2,0:T(8,128)(2,1)} fusion(bf16[80,320,2,320]{3,0,2,1:T(8,128)(2,1)} %bitcast.64, bf16[80,2,320,64]{2,3,0,1:T(8,128)(2,1)} %bitcast.76, pred[80,320]{1,0:T(8,128)(4,1)S(1)} %iota_compare_fusion, pred[80,320,2]{1,2,0:T(4,128)(4,1)S(1)} %add_compare_fusion), kind=kOutput, calls=%fused_computation.9 | convolution fusion | flops 2106982400 | bytes 45952000 | tf_op jit(solution)/shard_map/wael,welx->waex/dot_general | solution.py:33
  508.3 11.6 %all_to_all.69 = bf16[80,320,2,2,32]{1,4,3,2,0:T(8,128)(2,1)S(1)} all-to-all(bf16[80,320,2,2,32]{1,4,3,2,0:T(8,128)(2,1)} %bitcast.77), channel_id=1, replica_groups=mesh['member'=2,'wave'=8,'lev'=2] {'lev'}, dimensions={0} | all-to-all | bytes 13107200 | tf_op jit(solution)/shard_map/all_to_all | solution.py:100
  534.1 13.6 %copy.80 = bf16[40,320,2,2,64]{1,3,2,0,4:T(2,128)(2,1)S(1)} copy(bf16[40,320,2,2,64]{1,4,3,2,0:T(8,128)(2,1)} %convolution_convert_fusion) | data formatting | bytes 13107200 | tf_op jit(solution)/shard_map/convert_element_type | solution.py:51
  567.2 29.8 %select_bitcast_fusion = f32[80,2,320,64]{2,3,1,0:T(8,128)} fusion(bf16[80,320,2,64]{1,3,2,0:T(8,128)(2,1)S(1)} %bitcast.70, bf16[80,320,2,320]{3,0,2,1:T(8,128)(2,1)} %bitcast.65, pred[80,320]{1,0:T(8,128)(4,1)S(1)} %iota_compare_fusion), kind=kOutput, calls=%fused_computation.10 | convolution fusion | flops 2100428800 | bytes 52454400 | tf_op jit(solution)/shard_map/wael,waex->welx/dot_general | solution.py:59
  608.7 17.3 %copy.83 = bf16[32,320,2,160]{3,0,2,1:T(8,128)(2,1)} copy(bf16[32,320,2,160]{1,0,3,2:T(8,128)(2,1)} %bitcast.71) | data formatting | bytes 13107200 | tf_op jit(solution)/shard_map/reshape | solution.py:67
  626.0 14.6 %gather_fusion.2 = bf16[320,32,2,160]{3,1,2,0:T(8,128)(2,1)} fusion(bf16[32,320,2,160]{3,0,2,1:T(8,128)(2,1)} %copy.83, s32[1024]{0:T(1024)S(1)} %pad_clamp_fusion), kind=kCustom, calls=%fused_computation.1.clone | custom fusion | bytes 13108480 | tf_op jit(solution)/shard_map/jit(_take)/gather | solution.py:105
  646.6 232.1 %all_to_all.71 = bf16[32,320,2,160]{3,0,2,1:T(8,128)(2,1)} all-to-all(bf16[32,320,2,160]{3,0,2,1:T(8,128)(2,1)S(1)} %select_bitcast_fusion.1), channel_id=1, replica_groups=mesh['member'=2,'wave'=8,'lev'=2] {'wave'}, dimensions={1} | all-to-all | bytes 13107200 | tf_op jit(solution)/shard_map/all_to_all | solution.py:106
  878.7 13.8 %copy.91 = bf16[32,40,2,8,160]{4,3,2,1,0:T(8,128)(2,1)} copy(bf16[32,40,2,8,160]{4,0,2,1,3:T(8,128)(2,1)} %bitcast.68) | data formatting | bytes 13107200 | tf_op jit(solution)/shard_map/all_to_all | solution.py:106
  892.5 21.4 %reshape.303 = bf16[32,40,2,1280]{3,2,1,0:T(2,128)(2,1)} reshape(bf16[32,40,2,8,160]{4,3,2,1,0:T(8,128)(2,1)} %copy.91) | data formatting | bytes 13107200 | tf_op jit(solution)/shard_map/all_to_all | solution.py:106
  (49 shorter events, 126.0 us)
Async XLA Ops:
  0.0 524.3 %copy-start = (bf16[64,64]{1,0:T(8,128)(2,1)S(1)}, bf16[64,64]{1,0:T(8,128)(2,1)}, u32[]{:S(2)}) copy-start(bf16[64,64]{1,0:T(8,128)(2,1)} %param.16) | copy-start | bytes 24580
  56.2 23.0 %slice-start = ((s8[6553600]{0:T(1024)(128)(4,1)}), s8[2359296]{0:T(1024)(128)(4,1)S(1)}, s32[]{:S(2)}) async-start(s8[6553600]{0:T(1024)(128)(4,1)} %bitcast.79), calls=%async_computation.4 | async-start | bytes 4718592
  64.0 15.1 %slice-start.1 = ((s8[6553600]{0:T(1024)(128)(4,1)}), s8[4194304]{0:T(1024)(128)(4,1)S(1)}, s32[]{:S(2)}) async-start(s8[6553600]{0:T(1024)(128)(4,1)} %bitcast.79), calls=%async_computation.5 | async-start | bytes 8388608
  220.6 151.1 %all-to-all-start = ((bf16[8,2,204800]{2,1,0:T(2,128)(2,1)}), bf16[8,2,204800]{2,1,0:T(2,128)(2,1)}, u32[]{:S(2)}, u32[]{:S(2)}) async-start(bf16[8,2,204800]{2,1,0:T(2,128)(2,1)} %reshape.306), calls=%async_computation | async-start | bytes 13107200 | tf_op jit(solution)/shard_map/all_to_all | solution.py:97
  227.9 48.9 %copy-start.2 = (s32[320]{0:T(512)S(1)}, s32[320]{0:T(512)}, u32[]{:S(2)}) copy-start(s32[320]{0:T(512)} %param.11) | copy-start | bytes 3844
  227.9 52.6 %copy-start.1 = (s32[640]{0:T(1024)S(1)}, s32[640]{0:T(1024)}, u32[]{:S(2)}) copy-start(s32[640]{0:T(1024)} %param.13) | copy-start | bytes 7684
  227.9 54.5 %copy-start.3 = (f32[64]{0:T(128)S(1)}, f32[64]{0:T(128)}, u32[]{:S(2)}) copy-start(f32[64]{0:T(128)} %param.17) | copy-start | bytes 772
  519.9 4.4 copy-start.4
where the time goes:
time: 928 us; the launch traced here: 914 us
  local copies, waits for them, and re-layouts  386 us (42%)
  blocking collectives  255 us (27%)
  matrix products  97.8 us (11%)
  waiting for transfers between devices  85.1 us (9%)
  other arithmetic  82.7 us (9%)
    all_to_all x1, blocking collectives, local(): lax.all_to_all(result, 'wave', split_axis=1, concat_axis=3, tiled=True)  232 us
    unnamed x17, local copies, waits for them, and re-layouts  119 us
    all_to_all x1, waiting for transfers between devices, local(): lax.all_to_all(symmetric, 'wave', split_axis=3, concat_axis=1, tiled=True)  85.1 us
    all_to_all x2, local copies, waits for them, and re-layouts, local(): lax.all_to_all(result, 'wave', split_axis=1, concat_axis=3, tiled=True)  35.2 us
    another operation x1, local copies, waits for them, and re-layouts, local(): jnp.stack([spectra[:, :, 0] + spectra[:, :, 1], spectra[:, :, 0] - spectr...  32.9 us
    all_to_all x1, local copies, waits for them, and re-layouts, local(): lax.all_to_all(symmetric, 'wave', split_axis=3, concat_axis=1, tiled=True)  29.9 us
    dot_general x1, matrix products, inverse(): jnp.einsum('wael,waex->welx', paired, flattened, preferred_element_type=j...  29.8 us
    dot_general x1, matrix products, forward(): jnp.einsum('wael,welx->waex', paired, columns_in, preferred_element_type=...  28.6 us
  transfers between devices with their start and end apart: 1, of which 1 were waited for; matrix products, arithmetic and copies ran while one was open for 6% of the time, Pallas kernels for 0%

commit v1 on v0

v1 whole, which is shorter than its diff:
```python
import functools
import math

import jax
import jax.numpy as jnp
from jax import lax
from jax.experimental import pallas as pl
from jax.experimental.pallas import tpu as pltpu
from jax.sharding import PartitionSpec as P

LBLK = 64
LANES = 128
TILE = 8
AXES = ("wave", "lev")
NT = (((1,), (1,)), ((), ()))
NN = (((1,), (0,)), ((), ()))


def dot(a, b, dims=NN):
    return lax.dot_general(a, b, dims, preferred_element_type=jnp.float32)


def cosine_rows(freq_ref, first, count, width, lon_count):
    freq = freq_ref[pl.ds(first, count), :]
    row = lax.broadcasted_iota(jnp.int32, (count, 1), 0) + first
    phase = ((row // width) % 2).astype(jnp.float32) * (lon_count // 4)
    longitude = lax.broadcasted_iota(jnp.int32, (count, lon_count), 1).astype(jnp.float32)
    turns = freq * longitude + phase
    whole = jnp.floor(turns * (1.0 / lon_count) + 0.5)
    rest = jnp.abs(turns - whole * lon_count) * (1.0 / lon_count)
    angle = (0.25 - rest) * (2.0 * math.pi)
    square = angle * angle
    value = jnp.full_like(square, -1.0 / 39916800.0)
    for term in (1.0 / 362880.0, -1.0 / 5040.0, 1.0 / 120.0, -1.0 / 6.0, 1.0):
        value = value * square + term
    return (value * angle * (1.0 / math.sqrt(lon_count))).astype(jnp.bfloat16)


def dft_kernel(lats_ref, grid_ref, *refs, widths, low, pairs):
    count = len(widths)
    freqs, outs, tables = refs[:count], refs[count : 2 * count], refs[2 * count :]
    lon_count = grid_ref.shape[3]

    @pl.when(pl.program_id(0) == 0)
    def _():
        for freq, table, width in zip(freqs, tables, widths):
            step = 2 * width

            @pl.loop(0, table.shape[0] // step)
            def _(i):
                first = pl.multiple_of(i * step, step)
                table[pl.ds(first, step), :] = cosine_rows(freq, first, step, width, lon_count)

    fields = grid_ref.shape[0]
    rows = []
    for slot in range(pairs * low):
        rows.append(grid_ref[:, slot].reshape(2 * fields, lon_count))
    values = jnp.concatenate(rows, 0)
    for out, table, width in zip(outs, tables, widths):
        spectra = dot(table[...], values, NT)
        for pair in range(pairs):
            part = spectra[:, pair * LANES : (pair + 1) * LANES]
            out[:, :, pair] = part.reshape(-1, 2, width, LANES).astype(jnp.bfloat16)


def dft(grid, freqs, widths, owners, low):
    fields, lats, _, lon_count = grid.shape
    count = lats // low
    pairs = 2 if count % 2 == 0 else 1
    lats_order = jnp.arange(lats, dtype=jnp.int32)
    specs = [pl.BlockSpec((fields, pairs * low, 2, lon_count), lambda i, _: (0, i, 0, 0))]
    specs += [pl.BlockSpec(f.shape, lambda i, _: (0, 0)) for f in freqs]
    return pl.pallas_call(
        functools.partial(dft_kernel, widths=widths, low=low, pairs=pairs),
        grid_spec=pltpu.PrefetchScalarGridSpec(
            num_scalar_prefetch=1,
            grid=(count // pairs,),
            in_specs=specs,
            out_specs=[
                pl.BlockSpec((owners, 2, pairs, w, LANES), lambda i, _: (0, 0, i, 0, 0))
                for w in widths
            ],
            scratch_shapes=[pltpu.VMEM((f.shape[0], lon_count), jnp.bfloat16) for f in freqs],
        ),
        out_shape=[
            jax.ShapeDtypeStruct((owners, 2, count, w, LANES), jnp.bfloat16) for w in widths
        ],
        name="dft",
    )(lats_order, grid, *freqs)


def middle_kernel(meta, data, legendre, select, into, back, implicit, out, held, made, *, levels):
    step = pl.program_id(0)
    owners, _, count, width, _ = data.shape
    groups = owners // levels
    half = LANES // 2
    lat_count, row_count = legendre.shape[1], legendre.shape[2]

    @pl.when(step == 0)
    def _():
        for owner in range(owners):
            group, level = owner // levels, owner % levels
            for part in range(2):
                first = ((level * 2 + part) * groups + group) * count
                block = data[owner, part].astype(jnp.float32)
                held[pl.ds(first * width, count * width), :] = block.reshape(-1, LANES)

    wavenum, trim = meta[0, step], meta[1, step]
    slots = groups * count
    north, south = [], []
    for combo in range(2 * levels):
        block = held[pl.ds(combo * slots * width + step, slots, stride=width), :]
        turned = block.T
        north.append(turned[:half])
        south.append(turned[half:])
    first = jnp.concatenate(north, 0).astype(jnp.bfloat16)
    second = jnp.concatenate(south, 0).astype(jnp.bfloat16)
    basis = legendre[0]
    ordered = dot(first, select[0]) + dot(second, select[1])
    latitude = lax.broadcasted_iota(jnp.int32, (1, lat_count), 1)
    keep = latitude >= LBLK * trim
    ordered = jnp.where(keep, ordered, 0.0).astype(jnp.bfloat16)
    coeffs = dot(ordered, basis)
    row = lax.broadcasted_iota(jnp.int32, (1, row_count), 1)
    degree = (row + wavenum).astype(jnp.float32)
    factor = degree * (degree + 1.0) * (1.0 / float(row_count * (row_count - 1)))
    south_side = lax.broadcasted_iota(jnp.int32, (coeffs.shape[0], 1), 0) % 2
    flip = (south_side * (row % 2)) == 1
    coeffs = jnp.where(flip, -coeffs, coeffs).astype(jnp.bfloat16)
    modal = dot(into[...], coeffs)
    scaled = (modal / (1.0 + factor * implicit[...])).astype(jnp.bfloat16)
    solved = dot(back[...], scaled)
    solved = jnp.where(row + wavenum < row_count, solved, 0.0)
    solved = jnp.where(flip, -solved, solved).astype(jnp.bfloat16)
    sides = dot(solved, basis, NT)
    sides = jnp.where(keep, sides, 0.0).astype(jnp.bfloat16)
    first = dot(sides, select[0], NT)
    second = dot(sides, select[1], NT)
    for combo in range(2 * levels):
        span = slice(combo * half, (combo + 1) * half)
        block = jnp.concatenate([first[span], second[span]], 0).T
        made[pl.ds(combo * slots * width + step, slots, stride=width), :] = block

    @pl.when(step == pl.num_programs(0) - 1)
    def _():
        for owner in range(owners):
            group, level = owner // levels, owner % levels
            for part in range(2):
                first = ((level * 2 + part) * groups + group) * count
                block = made[pl.ds(first * width, count * width), :]
                out[owner, part] = block.reshape(count, width, LANES).astype(jnp.bfloat16)


def middle(data, meta, legendre, select, into, back, implicit, levels):
    owners, _, count, width, _ = data.shape
    whole = lambda a: pl.BlockSpec(a.shape, lambda i, _: (0,) * a.ndim)
    rows = owners * 2 * count * width
    return pl.pallas_call(
        functools.partial(middle_kernel, levels=levels),
        grid_spec=pltpu.PrefetchScalarGridSpec(
            num_scalar_prefetch=1,
            grid=(width,),
            in_specs=[
                whole(data),
                pl.BlockSpec((1,) + legendre.shape[1:], lambda i, meta: (meta[2, i], 0, 0)),
                whole(select),
                whole(into),
                whole(back),
                whole(implicit),
            ],
            out_specs=whole(data),
            scratch_shapes=[pltpu.VMEM((rows, LANES), jnp.float32)] * 2,
        ),
        out_shape=jax.ShapeDtypeStruct(data.shape, jnp.bfloat16),
        name="middle",
    )(meta, data, legendre, select, into, back, implicit)


def place_kernel(*refs, count, final, with_start, split):
    blocks, targets = refs[:count], refs[count : 2 * count]
    refs = refs[2 * count :]
    start = refs[0] if with_start else None
    out = refs[1] if with_start else refs[0]
    tables = refs[-count:]

    @pl.when(pl.program_id(0) == 0)
    def _():
        for target, table in zip(targets, tables):
            column = lax.broadcasted_iota(jnp.int32, table.shape, 1)
            per = table.shape[0] // split
            goal = target[...]
            for piece in range(split):
                span = slice(piece * per, (piece + 1) * per)
                wanted = goal[span] - piece * table.shape[1]
                table[span, :] = jnp.where(column[span] == wanted, 1.0, 0.0).astype(jnp.bfloat16)

    turned = []
    for block in blocks:
        rows = block[:, :, 0].astype(jnp.float32).reshape(-1, LANES)
        turned.append(rows.T.astype(jnp.bfloat16))
    pieces = []
    for piece in range(split):
        total = None
        for rows, table in zip(turned, tables):
            per = table.shape[0] // split
            span = slice(piece * per, (piece + 1) * per)
            part = dot(rows[:, span], table[span, :])
            total = part if total is None else total + part
        pieces.append(total)
    placed = jnp.concatenate(pieces, 1) if split > 1 else pieces[0]
    if with_start:
        placed = placed + start[...].astype(jnp.float32)
    placed = placed.astype(jnp.bfloat16)
    if not final:
        out[...] = placed
        return
    low, fields = out.shape[1], out.shape[0]
    per = 2 * fields
    for slot in range(low):
        block = placed[slot * per : (slot + 1) * per]
        out[:, slot] = block.reshape(fields, 2, block.shape[1])


def place(blocks, targets, start, columns, fields, low, final):
    owners, _, count, _, _ = blocks[0].shape
    split = 2 if owners % 2 == 0 and (columns // 2) % LANES == 0 else 1
    specs = [
        pl.BlockSpec((owners, 2, 1) + b.shape[3:], lambda i: (0, 0, i, 0, 0)) for b in blocks
    ]
    specs += [pl.BlockSpec(t.shape, lambda i: (0, 0)) for t in targets]
    args = list(blocks) + list(targets)
    if start is not None:
        specs.append(pl.BlockSpec((LANES, columns), lambda i: (i, 0)))
        args.append(start)
    if final:
        out_spec = pl.BlockSpec((fields, low, 2, columns), lambda i: (0, i, 0, 0))
        out_shape = jax.ShapeDtypeStruct((fields, low * count, 2, columns), jnp.bfloat16)
    else:
        out_spec = pl.BlockSpec((LANES, columns), lambda i: (i, 0))
        out_shape = jax.ShapeDtypeStruct((LANES * count, columns), jnp.bfloat16)
    return pl.pallas_call(
        functools.partial(
            place_kernel, count=len(blocks), final=final, with_start=start is not None, split=split
        ),
        grid=(count,),
        in_specs=specs,
        out_specs=out_spec,
        out_shape=out_shape,
        scratch_shapes=[
            pltpu.VMEM((t.shape[0], columns // split), jnp.bfloat16) for t in targets
        ],
        name="place",
    )(*args)


def chunk_widths(tiles):
    if tiles < 3:
        return [TILE] * tiles
    return [TILE, (tiles - 2) * TILE, TILE]


def local(grid, lat_order, wave_order, trim, legendre, modes_in, modes_out, implicit):
    fields, lats, _, lon_count = grid.shape
    per_device, row_count, lat_count = legendre.shape
    levels = lax.axis_size("lev")
    groups = lax.axis_size("wave")
    owners = groups * levels
    low = LANES // (2 * fields)
    count = lats // low
    share = per_device // levels
    tiles = -(-share // TILE)
    widths = chunk_widths(tiles)

    me = lax.axis_index("wave") * levels + lax.axis_index("lev")
    slot = jnp.arange(tiles * TILE, dtype=jnp.int32)
    inside = jnp.minimum(slot, share - 1)
    owner_waves = wave_order.reshape(owners, share)[:, inside]
    my_waves = lax.dynamic_slice_in_dim(owner_waves, me, 1)[0]
    my_index = lax.axis_index("lev") * share + inside
    meta = jnp.stack([my_waves, trim[my_waves], my_index])
    first_column = jnp.arange(owners, dtype=jnp.int32)[:, None] * (2 * share)
    columns = jnp.where(slot < share, first_column + 2 * slot, -4 * per_device * owners)

    freqs, metas, targets, first = [], [], [], 0
    for width in widths:
        span = slice(first, first + width)
        waves = jnp.broadcast_to(owner_waves[:, None, span], (owners, 2, width))
        freqs.append(waves.reshape(-1, 1).astype(jnp.float32))
        goal = columns[:, None, span] + jnp.arange(2, dtype=jnp.int32)[None, :, None]
        targets.append(goal.reshape(-1, 1))
        metas.append(meta[:, span])
        first += width

    sent = dft(grid, freqs[:1], widths[:1], owners, low)
    if len(widths) > 1:
        sent += dft(grid, freqs[1:], widths[1:], owners, low)

    slots = lat_order.reshape(groups * count, low).T
    select = (slots[:, :, None] == jnp.arange(lat_count, dtype=jnp.int32)).astype(jnp.bfloat16)
    same = jnp.eye(2, dtype=jnp.bfloat16)
    split_in = modes_in.reshape(-1, levels, fields)
    into = jnp.einsum("klf,cd->ckldf", split_in, same)
    into = jnp.repeat(into.reshape(2 * levels * fields, 2 * levels * fields), 2, axis=1)
    split_out = modes_out.reshape(levels, fields, -1)
    back = jnp.einsum("lfk,cd->lcfdk", split_out, same)
    back = jnp.repeat(back.reshape(2 * levels * fields, 2 * levels * fields), 2, axis=0)
    tall = jnp.concatenate([implicit, implicit])[:, None]
    turned = jnp.swapaxes(legendre, 1, 2)

    exchange = functools.partial(
        lax.all_to_all, axis_name=AXES, split_axis=0, concat_axis=0, tiled=True
    )
    returned = []
    received = [exchange(block) for block in sent]
    for block, chunk in zip(received, metas):
        made = middle(block, chunk, turned, select, into, back, tall, levels)
        returned.append(exchange(made))
    start = None
    if len(widths) > 1:
        start = place(returned[:-1], targets[:-1], None, lon_count, fields, low, False)
    return place(returned[-1:], targets[-1:], start, lon_count, fields, low, True)


def solution(mesh):
    in_specs = (
        P(("member", "lev"), "wave", None, None),
        P(),
        P(),
        P(),
        P("wave", None, None),
        P(),
        P(),
        P(),
    )
    out_specs = P(("member", "lev"), "wave", None, None)
    return jax.shard_map(local, mesh=mesh, in_specs=in_specs, out_specs=out_specs, check_vma=False)
```

time: 928 us -> 379 us (0.41); the launches traced: 914 us -> 375 us
  local copies, waits for them, and re-layouts: 386 us -> 14.8 us
  blocking collectives: 255 us -> 39.5 us
  Pallas kernels: 0 us -> 146 us
  matrix products: 97.8 us -> 0 us
  other arithmetic: 82.7 us -> 1.63 us
  starting transfers between devices: 7.31 us -> 55.3 us
  waiting for transfers between devices: 85.1 us -> 117 us
    all_to_all x3 -> x1, blocking collectives: 255 us -> 39.5 us  [local(): received = [exchange(block) for block in sent]]
    pallas_call x0 -> x7, Pallas kernels: none -> 146 us  [the longest x3 78.8 us: middle(): pl.pallas_call(functools.partial(middle_kernel, levels=levels), grid_spec...]
    unnamed x17 -> x19, local copies, waits for them, and re-layouts: 119 us -> 2.33 us
    dot_general x5 -> x0, matrix products: 97.8 us -> none  [the longest x1 29.8 us: inverse(): jnp.einsum('wael,waex->welx', paired, flattened, preferred_element_type=j...]
    all_to_all x5 -> x0, local copies, waits for them, and re-layouts: 77.5 us -> none  [the longest x2 35.2 us: local(): lax.all_to_all(result, 'wave', split_axis=1, concat_axis=3, tiled=True)]
    reshape x4 -> x6, local copies, waits for them, and re-layouts: 57.7 us -> 1.91 us  [the longest x2 0.84 us: local(): owner_waves = wave_order.reshape(owners, share)[:, inside]]
    all_to_all x1 -> x5, starting transfers between devices: 7.31 us -> 55.3 us  [the longest x3 43.2 us: local(): returned.append(exchange(made))]
    convert_element_type x5 -> x3, local copies, waits for them, and re-layouts: 47.2 us -> 2.46 us  [local(): freqs.append(waves.reshape(-1, 1).astype(jnp.float32))]
  transfers between devices with their start and end apart: 1 -> 5, of which waited for: 1 -> 4; matrix products, arithmetic and copies ran while one was open for 6% -> 3% of each run, Pallas kernels for 0% -> 32%
where the time goes in v1:
time: 379 us; the launch traced here: 375 us
  Pallas kernels  146 us (39%)
  waiting for transfers between devices  117 us (31%)
  starting transfers between devices  55.3 us (15%)
  blocking collectives  39.5 us (10%)
  local copies, waits for them, and re-layouts  14.8 us (4%)
    pallas_call x3, Pallas kernels, middle(): pl.pallas_call(functools.partial(middle_kernel, levels=levels), grid_spec...  78.8 us
    all_to_all x3, waiting for transfers between devices, local(): returned.append(exchange(made))  62.8 us
    all_to_all x2, waiting for transfers between devices, local(): received = [exchange(block) for block in sent]  54.1 us
    all_to_all x3, starting transfers between devices, local(): returned.append(exchange(made))  43.2 us
    all_to_all x1, blocking collectives, local(): received = [exchange(block) for block in sent]  39.5 us
    pallas_call x2, Pallas kernels, place(): pl.pallas_call(functools.partial(place_kernel, count=len(blocks), final=f...  34.2 us
    pallas_call x2, Pallas kernels, dft(): pl.pallas_call(functools.partial(dft_kernel, widths=widths, low=low, pair...  33.4 us
    all_to_all x2, starting transfers between devices, local(): received = [exchange(block) for block in sent]  12.1 us
  transfers between devices with their start and end apart: 5, of which 4 were waited for; matrix products, arithmetic and copies ran while one was open for 3% of the time, Pallas kernels for 32%

profile of v1, /device:TPU:0, one launch (start us, length us, event | category | flops | bytes accessed | tf_op | source)
XLA Modules:
  0.0 374.8 jit_solution(8192044321360653847)
XLA Ops:
  1.6 0.8 convert_element_type.28.refs_0_
  2.9 12.1 %dft.3 = bf16[16,2,20,8,128]{4,3,2,1,0:T(8,128)(2,1)} custom-call(s32[40]{0:T(128)} %iota.70.lats_ref, bf16[32,40,2,1280]{3,2,1,0:T(2,128)(2,1)} %grid_ref.3, f32[256,1]{1,0:T(8,128)} %convert_element_type.28.refs_0_), custom_call_target="tpu_custom_call" | custom-call | tf_op jit(solution)/shard_map/dft/pallas_call | solution.py:73
  15.1 7.4 %all-to-all-start.2 = ((bf16[16,2,20,8,128]{4,3,2,1,0:T(8,128)(2,1)}), bf16[16,2,20,8,128]{4,3,2,1,0:T(8,128)(2,1)S(1)}, u32[]{:S(2)}, u32[]{:S(2)}) async-start(bf16[16,2,20,8,128]{4,3,2,1,0:T(8,128)(2,1)} %dft.3), calls=%async_computation.2 | async-start | bytes 2621440 | tf_op jit(solution)/shard_map/all_to_all | solution.py:314
  23.4 0.9 convert_element_type.26.refs_0_
  24.9 21.3 %dft.2 = (bf16[16,2,20,24,128]{4,3,2,1,0:T(8,128)(2,1)}, bf16[16,2,20,8,128]{4,3,2,1,0:T(8,128)(2,1)}) custom-call(s32[40]{0:T(128)} %iota.64.lats_ref, bf16[32,40,2,1280]{3,2,1,0:T(2,128)(2,1)} %grid_ref.3, f32[768,1]{1,0:T(8,128)} %convert_element_type.26.refs_0_, f32[256,1]{1,0:T(8,128)} %convert_element_type.27.refs_1_), custom_call_target="tpu_custom_call" | custom-call | tf_op jit(solution)/shard_map/dft/pallas_call | solution.py:73
  46.2 3.6 all-to-all-done.2.data
  49.8 39.5 %all_to_all.30.data = bf16[16,2,20,8,128]{4,3,2,1,0:T(8,128)(2,1)} all-to-all(bf16[16,2,20,8,128]{4,3,2,1,0:T(8,128)(2,1)} %get-tuple-element.7), channel_id=1, replica_groups=mesh['member'=2,'wave'=8,'lev'=2] {'wave','lev'}, dimensions={0} | all-to-all | bytes 2621440 | tf_op jit(solution)/shard_map/all_to_all | solution.py:314
  89.3 4.7 %all-to-all-start.4 = ((bf16[16,2,20,24,128]{4,3,2,1,0:T(8,128)(2,1)}), bf16[16,2,20,24,128]{4,3,2,1,0:T(8,128)(2,1)}, u32[]{:S(2)}, u32[]{:S(2)}) async-start(bf16[16,2,20,24,128]{4,3,2,1,0:T(8,128)(2,1)} %get-tuple-element.8), calls=%async_computation.4 | async-start | bytes 7864320 | tf_op jit(solution)/shard_map/all_to_all | solution.py:314
  98.1 0.8 fusion.select
  99.5 16.8 %middle.4 = bf16[16,2,20,8,128]{4,3,2,1,0:T(8,128)(2,1)} custom-call(s32[3,8]{1,0:T(4,128)} %get-tuple-element.15.meta, bf16[16,2,20,8,128]{4,3,2,1,0:T(8,128)(2,1)} %copy-done.2, bf16[80,320,640]{2,1,0:T(8,128)(2,1)} %bitcast.19, bf16[2,160,320]{2,1,0:T(8,128)(2,1)} %fusion.select, bf16[128,256]{1,0:T(8,128)(2,1)} %copy.41.into, bf16[256,128]{1,0:T(8,128)(2,1)} %bitcast.22, ...), custom_call_target="tpu_custom_call" | custom-call | tf_op jit(solution)/shard_map/middle/pallas_call | solution.py:158
  116.3 50.5 %all-to-all-done.4.data = bf16[16,2,20,24,128]{4,3,2,1,0:T(8,128)(2,1)} async-done(((bf16[16,2,20,24,128]{4,3,2,1,0:T(8,128)(2,1)}), bf16[16,2,20,24,128]{4,3,2,1,0:T(8,128)(2,1)}, u32[]{:S(2)}, u32[]{:S(2)}) %all-to-all-start.4) | async-done | bytes 3932192 | tf_op jit(solution)/shard_map/all_to_all | solution.py:314
  166.9 18.6 %all-to-all-start.3 = ((bf16[16,2,20,8,128]{4,3,2,1,0:T(8,128)(2,1)}), bf16[16,2,20,8,128]{4,3,2,1,0:T(8,128)(2,1)S(1)}, u32[]{:S(2)}, u32[]{:S(2)}) async-start(bf16[16,2,20,8,128]{4,3,2,1,0:T(8,128)(2,1)} %middle.4), calls=%async_computation.3 | async-start | bytes 2621440 | tf_op jit(solution)/shard_map/all_to_all | solution.py:317
  186.1 45.3 %middle.5 = bf16[16,2,20,24,128]{4,3,2,1,0:T(8,128)(2,1)} custom-call(s32[3,24]{1,0:T(4,128)} %slice.33.meta, bf16[16,2,20,24,128]{4,3,2,1,0:T(8,128)(2,1)} %all-to-all-done.4.data, bf16[80,320,640]{2,1,0:T(8,128)(2,1)} %bitcast.20, bf16[2,160,320]{2,1,0:T(8,128)(2,1)} %fusion.select, bf16[128,256]{1,0:T(8,128)(2,1)} %copy.41.into, ...), custom_call_target="tpu_custom_call" | custom-call | tf_op jit(solution)/shard_map/middle/pallas_call | solution.py:158
  231.4 1.1 copy-done.3
  232.5 6.1 %all-to-all-start.5 = ((bf16[16,2,20,24,128]{4,3,2,1,0:T(8,128)(2,1)}), bf16[16,2,20,24,128]{4,3,2,1,0:T(8,128)(2,1)}, u32[]{:S(2)}, u32[]{:S(2)}) async-start(bf16[16,2,20,24,128]{4,3,2,1,0:T(8,128)(2,1)} %middle.5), calls=%async_computation.5 | async-start | bytes 7864320 | tf_op jit(solution)/shard_map/all_to_all | solution.py:317
  238.6 16.8 %middle.3 = bf16[16,2,20,8,128]{4,3,2,1,0:T(8,128)(2,1)} custom-call(s32[3,8]{1,0:T(4,128)} %get-tuple-element.16.meta, bf16[16,2,20,8,128]{4,3,2,1,0:T(8,128)(2,1)} %all_to_all.30.data, bf16[80,320,640]{2,1,0:T(8,128)(2,1)} %bitcast.21, bf16[2,160,320]{2,1,0:T(8,128)(2,1)} %fusion.select, bf16[128,256]{1,0:T(8,128)(2,1)} %copy.41.into, ...), custom_call_target="tpu_custom_call" | custom-call | tf_op jit(solution)/shard_map/middle/pallas_call | solution.py:158
  255.3 56.2 %all-to-all-done.5.refs_1_ = bf16[16,2,20,24,128]{4,3,2,1,0:T(8,128)(2,1)} async-done(((bf16[16,2,20,24,128]{4,3,2,1,0:T(8,128)(2,1)}), bf16[16,2,20,24,128]{4,3,2,1,0:T(8,128)(2,1)}, u32[]{:S(2)}, u32[]{:S(2)}) %all-to-all-start.5) | async-done | bytes 3932192 | tf_op jit(solution)/shard_map/all_to_all | solution.py:317
  311.6 18.6 %all-to-all-start.1 = ((bf16[16,2,20,8,128]{4,3,2,1,0:T(8,128)(2,1)}), bf16[16,2,20,8,128]{4,3,2,1,0:T(8,128)(2,1)S(1)}, u32[]{:S(2)}, u32[]{:S(2)}) async-start(bf16[16,2,20,8,128]{4,3,2,1,0:T(8,128)(2,1)} %middle.3), calls=%async_computation.1 | async-start | bytes 2621440 | tf_op jit(solution)/shard_map/all_to_all | solution.py:317
  330.4 0.8 add.148.refs_1_
  332.0 0.9 add.150.refs_3_
  332.9 17.9 %place.2.refs_2_ = bf16[2560,1280]{1,0:T(8,128)(2,1)} custom-call(bf16[16,2,20,8,128]{4,3,2,1,0:T(8,128)(2,1)} %copy-done.3, bf16[16,2,20,24,128]{4,3,2,1,0:T(8,128)(2,1)} %all-to-all-done.5.refs_1_, s32[256,1]{1,0:T(8,128)} %add.149.refs_2_, s32[768,1]{1,0:T(8,128)} %add.150.refs_3_), custom_call_target="tpu_custom_call" | custom-call | tf_op jit(solution)/shard_map/place/pallas_call | solution.py:241
  350.8 6.6 %all-to-all-done.1.refs_0_ = bf16[16,2,20,8,128]{4,3,2,1,0:T(8,128)(2,1)S(1)} async-done(((bf16[16,2,20,8,128]{4,3,2,1,0:T(8,128)(2,1)}), bf16[16,2,20,8,128]{4,3,2,1,0:T(8,128)(2,1)S(1)}, u32[]{:S(2)}, u32[]{:S(2)}) %all-to-all-start.1) | async-done | bytes 1310752 | tf_op jit(solution)/shard_map/all_to_all | solution.py:317
  357.4 1.1 copy-done.4
  358.5 16.3 %place.3 = bf16[32,40,2,1280]{3,2,1,0:T(2,128)(2,1)} custom-call(bf16[16,2,20,8,128]{4,3,2,1,0:T(8,128)(2,1)} %copy-done.4, s32[256,1]{1,0:T(8,128)} %add.148.refs_1_, bf16[2560,1280]{1,0:T(8,128)(2,1)} %place.2.refs_2_), custom_call_target="tpu_custom_call" | custom-call | tf_op jit(solution)/shard_map/place/pallas_call | solution.py:241
  (62 shorter events, 10.0 us)
Async XLA Ops:
  0.0 96.7 %copy-start = (s32[640]{0:T(1024)S(1)}, s32[640]{0:T(1024)}, u32[]{:S(2)}) copy-start(s32[640]{0:T(1024)} %param.11) | copy-start | bytes 7684
  15.1 34.7 %all-to-all-start.2 = ((bf16[16,2,20,8,128]{4,3,2,1,0:T(8,128)(2,1)}), bf16[16,2,20,8,128]{4,3,2,1,0:T(8,128)(2,1)S(1)}, u32[]{:S(2)}, u32[]{:S(2)}) async-start(bf16[16,2,20,8,128]{4,3,2,1,0:T(8,128)(2,1)} %dft.3), calls=%async_computation.2 | async-start | bytes 2621440 | tf_op jit(solution)/shard_map/all_to_all | solution.py:314
  49.8 39.5 %copy-start.2 = (bf16[16,2,20,8,128]{4,3,2,1,0:T(8,128)(2,1)}, bf16[16,2,20,8,128]{4,3,2,1,0:T(8,128)(2,1)S(1)}, u32[]{:S(2)}) copy-start(bf16[16,2,20,8,128]{4,3,2,1,0:T(8,128)(2,1)S(1)} %all-to-all-done.2.data) | copy-start | bytes 3932164
  89.3 4.8 %copy-start.6 = (bf16[64,64]{1,0:T(8,128)(2,1)S(1)}, bf16[64,64]{1,0:T(8,128)(2,1)}, u32[]{:S(2)}) copy-start(bf16[64,64]{1,0:T(8,128)(2,1)} %param.13) | copy-start | bytes 24580
  89.3 5.9 %copy-start.8 = (f32[64]{0:T(128)S(1)}, f32[64]{0:T(128)}, u32[]{:S(2)}) copy-start(f32[64]{0:T(128)} %param.15) | copy-start | bytes 772
  89.3 6.7 %copy-start.5 = (bf16[64,64]{1,0:T(8,128)(2,1)S(1)}, bf16[64,64]{1,0:T(8,128)(2,1)}, u32[]{:S(2)}) copy-start(bf16[64,64]{1,0:T(8,128)(2,1)} %param.14) | copy-start | bytes 24580
  89.3 7.0 %copy-start.7 = (s32[320]{0:T(512)S(1)}, s32[320]{0:T(512)}, u32[]{:S(2)}) copy-start(s32[320]{0:T(512)} %param.9) | copy-start | bytes 3844
  89.3 77.6 %all-to-all-start.4 = ((bf16[16,2,20,24,128]{4,3,2,1,0:T(8,128)(2,1)}), bf16[16,2,20,24,128]{4,3,2,1,0:T(8,128)(2,1)}, u32[]{:S(2)}, u32[]{:S(2)}) async-start(bf16[16,2,20,24,128]{4,3,2,1,0:T(8,128)(2,1)} %get-tuple-element.8), calls=%async_computation.4 | async-start | bytes 7864320 | tf_op jit(solution)/shard_map/all_to_all | solution.py:314
  166.9 64.5 %all-to-all-start.3 = ((bf16[16,2,20,8,128]{4,3,2,1,0:T(8,128)(2,1)}), bf16[16,2,20,8,128]{4,3,2,1,0:T(8,128)(2,1)S(1)}, u32[]{:S(2)}, u32[]{:S(2)}) async-start(bf16[16,2,20,8,128]{4,3,2,1,0:T(8,128)(2,1)} %middle.4), calls=%async_computation.3 | async-start | bytes 2621440 | tf_op jit(solution)/shard_map/all_to_all | solution.py:317
  231.4 1.1 copy-start.3
  232.5 79.1 %all-to-all-start.5 = ((bf16[16,2,20,24,128]{4,3,2,1,0:T(8,128)(2,1)}), bf16[16,2,20,24,128]{4,3,2,1,0:T(8,128)(2,1)}, u32[]{:S(2)}, u32[]{:S(2)}) async-start(bf16[16,2,20,24,128]{4,3,2,1,0:T(8,128)(2,1)} %middle.5), calls=%async_computation.5 | async-start | bytes 7864320 | tf_op jit(solution)/shard_map/all_to_all | solution.py:317
  311.6 45.9 %all-to-all-start.1 = ((bf16[16,2,20,8,128]{4,3,2,1,0:T(8,128)(2,1)}), bf16[16,2,20,8,128]{4,3,2,1,0:T(8,128)(2,1)S(1)}, u32[]{:S(2)}, u32[]{:S(2)}) async-start(bf16[16,2,20,8,128]{4,3,2,1,0:T(8,128)(2,1)} %middle.3), calls=%async_computation.1 | async-start | bytes 2621440 | tf_op jit(solution)/shard_map/all_to_all | solution.py:317
  332.9 41.9 %copy-start.1 = (s32[640]{0:T(1024)S(1)}, s32[640]{0:T(1024)}, u32[]{:S(2)}) copy-start(s32[640]{0:T(1024)} %param.11) | copy-start | bytes 7684
  357.4 1.1 copy-start.4

commit v2 on v1

v2 whole, which is shorter than its diff:
```python
import functools
import math

import jax
import jax.numpy as jnp
from jax import lax
from jax.experimental import pallas as pl
from jax.experimental.pallas import tpu as pltpu
from jax.sharding import PartitionSpec as P


LBLK = 64
LANES = 128
TILE = 8
AXES = ("wave", "lev")
NT = (((1,), (1,)), ((), ()))
NN = (((1,), (0,)), ((), ()))


def dot(a, b, dims=NN):
    return lax.dot_general(a, b, dims, preferred_element_type=jnp.float32)


def cosine_rows(freq_ref, first, count, width, lon_count):
    freq = freq_ref[pl.ds(first, count), :]
    row = lax.broadcasted_iota(jnp.int32, (count, 1), 0) + first
    phase = ((row // width) % 2).astype(jnp.float32) * (lon_count // 4)
    longitude = lax.broadcasted_iota(jnp.int32, (count, lon_count), 1).astype(jnp.float32)
    turns = freq * longitude + phase
    whole = jnp.floor(turns * (1.0 / lon_count) + 0.5)
    rest = jnp.abs(turns - whole * lon_count) * (1.0 / lon_count)
    angle = (0.25 - rest) * (2.0 * math.pi)
    square = angle * angle
    value = jnp.full_like(square, -1.0 / 39916800.0)
    for term in (1.0 / 362880.0, -1.0 / 5040.0, 1.0 / 120.0, -1.0 / 6.0, 1.0):
        value = value * square + term
    return (value * angle * (1.0 / math.sqrt(lon_count))).astype(jnp.bfloat16)


def dft_kernel(grid_ref, freq, *refs, width, low, pairs):
    outs, table = refs[:-1], refs[-1]
    fields, lon_count = grid_ref.shape[0], grid_ref.shape[3]

    @pl.when(pl.program_id(0) == 0)
    def _():
        step = 2 * width

        @pl.loop(0, table.shape[0] // step)
        def _(i):
            first = pl.multiple_of(i * step, step)
            table[pl.ds(first, step), :] = cosine_rows(freq, first, step, width, lon_count)

    rows = [grid_ref[:, slot].reshape(2 * fields, lon_count) for slot in range(pairs * low)]
    spectra = dot(table[...], jnp.concatenate(rows, 0), NT)
    for pair in range(pairs):
        part = spectra[:, pair * LANES : (pair + 1) * LANES]
        part = part.reshape(-1, 2, width, LANES).astype(jnp.bfloat16)
        if len(outs) == 1:
            outs[0][:, :, pair] = part
        else:
            for piece, out in enumerate(outs):
                out[0, :, pair] = part[piece]


def dft(grid, freq, width, owners, low, separate):
    fields, lats, _, lon_count = grid.shape
    count = lats // low
    pairs = 2 if count % 2 == 0 else 1
    pieces, each = (owners, 1) if separate else (1, owners)
    return pl.pallas_call(
        functools.partial(dft_kernel, width=width, low=low, pairs=pairs),
        grid=(count // pairs,),
        in_specs=[
            pl.BlockSpec((fields, pairs * low, 2, lon_count), lambda i: (0, i, 0, 0)),
            pl.BlockSpec(freq.shape, lambda i: (0, 0)),
        ],
        out_specs=[pl.BlockSpec((each, 2, pairs, width, LANES), lambda i: (0, 0, i, 0, 0))]
        * pieces,
        out_shape=[jax.ShapeDtypeStruct((each, 2, count, width, LANES), jnp.bfloat16)] * pieces,
        scratch_shapes=[pltpu.VMEM((freq.shape[0], lon_count), jnp.bfloat16)],
        name="dft",
    )(grid, freq)


def middle_kernel(meta, peers, *refs, levels, pieces):
    data, refs = refs[:pieces], refs[pieces:]
    legendre, select, into, back, implicit = refs[:5]
    out, (held, made) = refs[5 : 5 + pieces], refs[5 + pieces :]
    step = pl.program_id(0)
    each, _, count, width, _ = data[0].shape
    owners = each * pieces
    groups = owners // levels
    half = LANES // 2
    lat_count, row_count = legendre.shape[1], legendre.shape[2]

    def place_of(owner, part):
        first = ((owner % levels) * 2 + part) * groups + owner // levels
        return pl.ds(pl.multiple_of(first * (count * width), TILE), count * width)

    @pl.when(step == 0)
    def _():
        for piece in range(owners):
            for part in range(2):
                block = data[piece // each][piece % each, part].astype(jnp.float32)
                held[place_of(peers[0, piece], part), :] = block.reshape(-1, LANES)

    wavenum, trim = meta[0, step], meta[1, step]
    slots = groups * count
    north, south = [], []
    for combo in range(2 * levels):
        block = held[pl.ds(combo * slots * width + step, slots, stride=width), :]
        turned = block.T
        north.append(turned[:half])
        south.append(turned[half:])
    first = jnp.concatenate(north, 0).astype(jnp.bfloat16)
    second = jnp.concatenate(south, 0).astype(jnp.bfloat16)
    basis = legendre[0]
    ordered = dot(first, select[0]) + dot(second, select[1])
    latitude = lax.broadcasted_iota(jnp.int32, (1, lat_count), 1)
    keep = latitude >= LBLK * trim
    ordered = jnp.where(keep, ordered, 0.0).astype(jnp.bfloat16)
    coeffs = dot(ordered, basis)
    row = lax.broadcasted_iota(jnp.int32, (1, row_count), 1)
    degree = (row + wavenum).astype(jnp.float32)
    factor = degree * (degree + 1.0) * (1.0 / float(row_count * (row_count - 1)))
    south_side = lax.broadcasted_iota(jnp.int32, (coeffs.shape[0], 1), 0) % 2
    flip = (south_side * (row % 2)) == 1
    coeffs = jnp.where(flip, -coeffs, coeffs).astype(jnp.bfloat16)
    modal = dot(into[...], coeffs)
    scaled = (modal / (1.0 + factor * implicit[...])).astype(jnp.bfloat16)
    solved = dot(back[...], scaled)
    solved = jnp.where(row + wavenum < row_count, solved, 0.0)
    solved = jnp.where(flip, -solved, solved).astype(jnp.bfloat16)
    sides = dot(solved, basis, NT)
    sides = jnp.where(keep, sides, 0.0).astype(jnp.bfloat16)
    first = dot(sides, select[0], NT)
    second = dot(sides, select[1], NT)
    for combo in range(2 * levels):
        span = slice(combo * half, (combo + 1) * half)
        block = jnp.concatenate([first[span], second[span]], 0).T
        made[pl.ds(combo * slots * width + step, slots, stride=width), :] = block

    @pl.when(step == pl.num_programs(0) - 1)
    def _():
        for piece in range(owners):
            for part in range(2):
                block = made[place_of(peers[1, piece], part), :].reshape(count, width, LANES)
                out[piece // each][piece % each, part] = block.astype(jnp.bfloat16)


def middle(data, meta, peers, legendre, select, into, back, implicit, levels):
    each, _, count, width, _ = data[0].shape
    whole = lambda a: pl.BlockSpec(a.shape, lambda i, *_: (0,) * a.ndim)
    rows = each * len(data) * 2 * count * width
    return pl.pallas_call(
        functools.partial(middle_kernel, levels=levels, pieces=len(data)),
        grid_spec=pltpu.PrefetchScalarGridSpec(
            num_scalar_prefetch=2,
            grid=(width,),
            in_specs=[whole(a) for a in data]
            + [pl.BlockSpec((1,) + legendre.shape[1:], lambda i, meta, _: (meta[2, i], 0, 0))]
            + [whole(a) for a in (select, into, back, implicit)],
            out_specs=[whole(a) for a in data],
            scratch_shapes=[pltpu.VMEM((rows, LANES), jnp.float32)] * 2,
        ),
        out_shape=[jax.ShapeDtypeStruct(a.shape, jnp.bfloat16) for a in data],
        name="middle",
    )(meta, peers, *data, legendre, select, into, back, implicit)


def place_kernel(peers, *refs, pieces, final, with_start, split):
    blocks, refs = refs[:pieces], refs[pieces:]
    target, refs = refs[0], refs[1:]
    start = refs[0] if with_start else None
    out, table, gathered = refs[-3:]
    per = table.shape[0] // split

    @pl.when(pl.program_id(0) == 0)
    def _():
        column = lax.broadcasted_iota(jnp.int32, table.shape, 1)
        goal = target[...]
        for piece in range(split):
            span = slice(piece * per, (piece + 1) * per)
            wanted = goal[span] - piece * table.shape[1]
            table[span, :] = jnp.where(column[span] == wanted, 1.0, 0.0).astype(jnp.bfloat16)

    each, _, _, width, _ = blocks[0].shape
    for piece in range(each * pieces):
        first = pl.multiple_of(peers[0, piece] * (2 * width), TILE)
        block = blocks[piece // each][piece % each, :, 0].astype(jnp.float32)
        gathered[pl.ds(first, 2 * width), :] = block.reshape(2 * width, LANES)
    rows = gathered[...].T.astype(jnp.bfloat16)
    placed = []
    for piece in range(split):
        span = slice(piece * per, (piece + 1) * per)
        placed.append(dot(rows[:, span], table[span, :]))
    placed = jnp.concatenate(placed, 1) if split > 1 else placed[0]
    placed = placed.astype(jnp.bfloat16)
    if with_start:
        placed = placed + start[...]
    if not final:
        out[...] = placed
        return
    low, fields = out.shape[1], out.shape[0]
    for slot in range(low):
        block = placed[slot * 2 * fields : (slot + 1) * 2 * fields]
        out[:, slot] = block.reshape(fields, 2, block.shape[1])


def place(blocks, peers, target, start, columns, fields, low, final):
    each, _, count, width, _ = blocks[0].shape
    owners = each * len(blocks)
    split = 2 if owners % 2 == 0 and (columns // 2) % LANES == 0 else 1
    specs = [pl.BlockSpec((each, 2, 1, width, LANES), lambda i, _: (0, 0, i, 0, 0))] * len(blocks)
    specs.append(pl.BlockSpec(target.shape, lambda i, _: (0, 0)))
    args = list(blocks) + [target]
    if start is not None:
        specs.append(pl.BlockSpec((LANES, columns), lambda i, _: (i, 0)))
        args.append(start)
    if final:
        out_spec = pl.BlockSpec((fields, low, 2, columns), lambda i, _: (0, i, 0, 0))
        out_shape = jax.ShapeDtypeStruct((fields, low * count, 2, columns), jnp.bfloat16)
    else:
        out_spec = pl.BlockSpec((LANES, columns), lambda i, _: (i, 0))
        out_shape = jax.ShapeDtypeStruct((LANES * count, columns), jnp.bfloat16)
    return pl.pallas_call(
        functools.partial(
            place_kernel, pieces=len(blocks), final=final, with_start=start is not None, split=split
        ),
        grid_spec=pltpu.PrefetchScalarGridSpec(
            num_scalar_prefetch=1,
            grid=(count,),
            in_specs=specs,
            out_specs=out_spec,
            scratch_shapes=[
                pltpu.VMEM((target.shape[0], columns // split), jnp.bfloat16),
                pltpu.VMEM((owners * 2 * width, LANES), jnp.float32),
            ],
        ),
        out_shape=out_shape,
        name="place",
    )(peers, *args)


def chunk_widths(tiles):
    if tiles == 1:
        return [TILE]
    first = max(1, tiles * 2 // 5)
    return [first * TILE, (tiles - first) * TILE]


def partner(me, piece, groups, levels, back):
    fast = 2 * levels if groups % 2 == 0 else levels
    slow = groups * levels // fast
    far = piece // fast
    high = (me // fast + (slow - far if back else far)) % slow
    near = me % fast
    if fast & (fast - 1) == 0:
        low = near ^ (piece % fast)
    else:
        low = (near + (fast - piece % fast if back else piece % fast)) % fast
    return high * fast + low


def shift(pieces, groups, levels):
    owners = groups * levels
    moved = [pieces[0]]
    for piece in range(1, owners):
        pairs = [(i, partner(i, piece, groups, levels, False)) for i in range(owners)]
        moved.append(lax.ppermute(pieces[piece], AXES, pairs))
    return moved


def local(grid, lat_order, wave_order, trim, legendre, modes_in, modes_out, implicit):
    fields, lats, _, lon_count = grid.shape
    per_device, _, lat_count = legendre.shape
    levels = lax.axis_size("lev")
    groups = lax.axis_size("wave")
    owners = groups * levels
    low = LANES // (2 * fields)
    count = lats // low
    share = per_device // levels
    tiles = -(-share // TILE)
    widths = chunk_widths(tiles)

    me = lax.axis_index("wave") * levels + lax.axis_index("lev")
    slot = jnp.arange(tiles * TILE, dtype=jnp.int32)
    inside = jnp.minimum(slot, share - 1)
    owner_waves = wave_order.reshape(owners, share)[:, inside]
    my_waves = lax.dynamic_slice_in_dim(owner_waves, me, 1)[0]
    my_index = lax.axis_index("lev") * share + inside
    meta = jnp.stack([my_waves, trim[my_waves], my_index])
    first_column = jnp.arange(owners, dtype=jnp.int32)[:, None] * (2 * share)
    columns = jnp.where(slot < share, first_column + 2 * slot, -4 * per_device * owners)

    piece = jnp.arange(owners, dtype=jnp.int32)
    natural = jnp.stack([piece, piece])
    paired = jnp.stack(
        [partner(me, piece, groups, levels, back) for back in (True, False)]
    )
    peers = [natural, paired]

    freqs, metas, targets, first = [], [], [], 0
    for which, width in enumerate(widths):
        span = slice(first, first + width)
        waves = owner_waves[:, span] if which == 0 else owner_waves[paired[1]][:, span]
        waves = jnp.broadcast_to(waves[:, None], (owners, 2, width))
        freqs.append(waves.reshape(-1, 1).astype(jnp.float32))
        goal = columns[:, None, span] + jnp.arange(2, dtype=jnp.int32)[None, :, None]
        targets.append(goal.reshape(-1, 1))
        metas.append(meta[:, span])
        first += width

    sent = []
    for which, (freq, width) in enumerate(zip(freqs, widths)):
        sent.append(dft(grid, freq, width, owners, low, which > 0))

    slots = lat_order.reshape(groups * count, low).T
    select = (slots[:, :, None] == jnp.arange(lat_count, dtype=jnp.int32)).astype(jnp.bfloat16)
    same = jnp.eye(2, dtype=jnp.bfloat16)
    split_in = modes_in.reshape(-1, levels, fields)
    into = jnp.einsum("klf,cd->ckldf", split_in, same)
    into = jnp.repeat(into.reshape(2 * levels * fields, 2 * levels * fields), 2, axis=1)
    split_out = modes_out.reshape(levels, fields, -1)
    back = jnp.einsum("lfk,cd->lcfdk", split_out, same)
    back = jnp.repeat(back.reshape(2 * levels * fields, 2 * levels * fields), 2, axis=0)
    tall = jnp.concatenate([implicit, implicit])[:, None]
    turned = jnp.swapaxes(legendre, 1, 2)

    def exchange(blocks):
        if len(blocks) == 1:
            return [lax.all_to_all(blocks[0], AXES, split_axis=0, concat_axis=0, tiled=True)]
        return shift(blocks, groups, levels)

    received = []
    for blocks in sent:
        received.append(exchange(blocks))
    returned = []
    for blocks, chunk, who in zip(received, metas, peers):
        made = middle(blocks, chunk, who, turned, select, into, back, tall, levels)
        returned.append(exchange(made))
    result = None
    for which, blocks in enumerate(returned):
        final = which == len(returned) - 1
        result = place(
            blocks, peers[which], targets[which], result, lon_count, fields, low, final
        )
    return result


def solution(mesh):
    in_specs = (
        P(("member", "lev"), "wave", None, None),
        P(),
        P(),
        P(),
        P("wave", None, None),
        P(),
        P(),
        P(),
    )
    out_specs = P(("member", "lev"), "wave", None, None)
    return jax.shard_map(local, mesh=mesh, in_specs=in_specs, out_specs=out_specs, check_vma=False)
```

time: 379 us -> 437 us (1.15)
  starting transfers between devices: 55.3 us -> 129 us
  blocking collectives: 39.5 us -> 0 us
  waiting for transfers between devices: 117 us -> 142 us
    ppermute x0 -> x30, starting transfers between devices: none -> 108 us  [shift(): moved.append(lax.ppermute(pieces[piece], AXES, pairs))]
    ppermute x0 -> x30, waiting for transfers between devices: none -> 97.7 us  [shift(): moved.append(lax.ppermute(pieces[piece], AXES, pairs))]
    all_to_all x5 -> x2, waiting for transfers between devices: 117 us -> 44.7 us  [exchange(): lax.all_to_all(blocks[0], AXES, split_axis=0, concat_axis=0, tiled=True)]
    all_to_all x1 -> x0, blocking collectives: 39.5 us -> none  [local(): received = [exchange(block) for block in sent]]
    all_to_all x5 -> x2, starting transfers between devices: 55.3 us -> 20.9 us  [exchange(): lax.all_to_all(blocks[0], AXES, split_axis=0, concat_axis=0, tiled=True)]
    pallas_call x7 -> x6, Pallas kernels: 146 us -> 148 us  [the longest x2 80.2 us: middle(): pl.pallas_call(functools.partial(middle_kernel, levels=levels, pieces=len...]
  transfers between devices with their start and end apart: 5 -> 32, of which waited for: 4 -> 14; matrix products, arithmetic and copies ran while one was open for 3% -> 2% of each run, Pallas kernels for 32% -> 18%
where the time goes in v2:
time: 437 us; the launch traced here: 435 us
  Pallas kernels  148 us (34%)
  waiting for transfers between devices  142 us (32%)
  starting transfers between devices  129 us (30%)
  local copies, waits for them, and re-layouts  12.3 us (3%)
    ppermute x30, starting transfers between devices, shift(): moved.append(lax.ppermute(pieces[piece], AXES, pairs))  108 us
    ppermute x30, waiting for transfers between devices, shift(): moved.append(lax.ppermute(pieces[piece], AXES, pairs))  97.7 us
    pallas_call x2, Pallas kernels, middle(): pl.pallas_call(functools.partial(middle_kernel, levels=levels, pieces=len...  80.2 us
    all_to_all x2, waiting for transfers between devices, exchange(): lax.all_to_all(blocks[0], AXES, split_axis=0, concat_axis=0, tiled=True)  44.7 us
    pallas_call x2, Pallas kernels, place(): pl.pallas_call(functools.partial(place_kernel, pieces=len(blocks), final=...  36.4 us
    pallas_call x2, Pallas kernels, dft(): pl.pallas_call(functools.partial(dft_kernel, width=width, low=low, pairs=...  31.1 us
    all_to_all x2, starting transfers between devices, exchange(): lax.all_to_all(blocks[0], AXES, split_axis=0, concat_axis=0, tiled=True)  20.9 us
  transfers between devices with their start and end apart: 32, of which 14 were waited for; matrix products, arithmetic and copies ran while one was open for 2% of the time, Pallas kernels for 18%

profile of v2, /device:TPU:0, one launch (start us, length us, event | category | flops | bytes accessed | tf_op | source)
XLA Modules:
  0.0 435.0 jit_solution(10988078068051173471)
XLA Ops:
  2.4 13.8 %dft.3 = bf16[16,2,20,16,128]{4,3,2,1,0:T(8,128)(2,1)} custom-call(bf16[32,40,2,1280]{3,2,1,0:T(2,128)(2,1)} %grid_ref.3, f32[512,1]{1,0:T(8,128)} %convert_element_type.20.freq), custom_call_target="tpu_custom_call" | custom-call | tf_op jit(solution)/shard_map/dft/pallas_call | solution.py:70
  16.3 7.4 %all-to-all-start = ((bf16[16,2,20,16,128]{4,3,2,1,0:T(8,128)(2,1)}), bf16[16,2,20,16,128]{4,3,2,1,0:T(8,128)(2,1)S(1)}, u32[]{:S(2)}, u32[]{:S(2)}) async-start(bf16[16,2,20,16,128]{4,3,2,1,0:T(8,128)(2,1)} %dft.3), calls=%async_computation | async-start | bytes 5242880 | tf_op jit(solution)/shard_map/all_to_all | solution.py:332
  29.1 44.7 %all-to-all-done.refs_0_ = bf16[16,2,20,16,128]{4,3,2,1,0:T(8,128)(2,1)S(1)} async-done(((bf16[16,2,20,16,128]{4,3,2,1,0:T(8,128)(2,1)}), bf16[16,2,20,16,128]{4,3,2,1,0:T(8,128)(2,1)S(1)}, u32[]{:S(2)}, u32[]{:S(2)}) %all-to-all-start) | async-done | bytes 2621472 | tf_op jit(solution)/shard_map/all_to_all | solution.py:332
  75.3 33.1 %middle.3 = bf16[16,2,20,16,128]{4,3,2,1,0:T(8,128)(2,1)} custom-call(s32[3,16]{1,0:T(4,128)} %bitcast.33, s32[2,16]{1,0:T(2,128)} %pad_add_fusion.2.peers, bf16[16,2,20,16,128]{4,3,2,1,0:T(8,128)(2,1)} %copy-done.2, bf16[80,320,640]{2,1,0:T(8,128)(2,1)} %bitcast.23, bf16[2,160,320]{2,1,0:T(8,128)(2,1)} %fusion.refs_17_.refs_2_, ...), custom_call_target="tpu_custom_call" | custom-call | tf_op jit(solution)/shard_map/middle/pallas_call | solution.py:155
  108.4 13.5 %all-to-all-start.1 = ((bf16[16,2,20,16,128]{4,3,2,1,0:T(8,128)(2,1)}), bf16[16,2,20,16,128]{4,3,2,1,0:T(8,128)(2,1)S(1)}, u32[]{:S(2)}, u32[]{:S(2)}) async-start(bf16[16,2,20,16,128]{4,3,2,1,0:T(8,128)(2,1)} %middle.3), calls=%async_computation.1 | async-start | bytes 5242880 | tf_op jit(solution)/shard_map/all_to_all | solution.py:332
  123.6 17.3 %dft.2 = (bf16[1,2,20,24,128]{4,3,2,1,0:T(8,128)(2,1)}, bf16[1,2,20,24,128]{4,3,2,1,0:T(8,128)(2,1)}, bf16[1,2,20,24,128]{4,3,2,1,0:T(8,128)(2,1)}, bf16[1,2,20,...) custom-call(bf16[32,40,2,1280]{3,2,1,0:T(2,128)(2,1)} %grid_ref.3, ...), custom_call_target="tpu_custom_call" | custom-call | tf_op jit(solution)/shard_map/dft/pallas_call | solution.py:70
  148.3 7.6 %collective-permute-done.1.refs_2_ = bf16[1,2,20,24,128]{4,3,2,1,0:T(8,128)(2,1)S(1)} collective-permute-done((bf16[1,2,20,24,128]{4,3,2,1,0:T(8,128)(2,1)}, bf16[1,2,20,24,128]{4,3,2,1,0:T(8,128)(2,1)S(1)}, u32[]{:S(2)}, u32[]{:S(2)}) %collective-permute-start.1) | collective-permute-done | bytes 245792 | tf_op jit(solution)/shard_map/ppermute | solution.py:270
  155.9 8.0 %collective-permute-done.2.refs_3_ = bf16[1,2,20,24,128]{4,3,2,1,0:T(8,128)(2,1)S(1)} collective-permute-done((bf16[1,2,20,24,128]{4,3,2,1,0:T(8,128)(2,1)}, bf16[1,2,20,24,128]{4,3,2,1,0:T(8,128)(2,1)S(1)}, u32[]{:S(2)}, u32[]{:S(2)}) %collective-permute-start.2) | collective-permute-done | bytes 245792 | tf_op jit(solution)/shard_map/ppermute | solution.py:270
  164.9 10.3 %collective-permute-done.3.refs_4_ = bf16[1,2,20,24,128]{4,3,2,1,0:T(8,128)(2,1)} collective-permute-done((bf16[1,2,20,24,128]{4,3,2,1,0:T(8,128)(2,1)}, bf16[1,2,20,24,128]{4,3,2,1,0:T(8,128)(2,1)}, u32[]{:S(2)}, u32[]{:S(2)}) %collective-permute-start.3) | collective-permute-done | bytes 245792 | tf_op jit(solution)/shard_map/ppermute | solution.py:270
  175.2 12.1 %collective-permute-start.8 = (bf16[1,2,20,24,128]{4,3,2,1,0:T(8,128)(2,1)}, bf16[1,2,20,24,128]{4,3,2,1,0:T(8,128)(2,1)}, u32[]{:S(2)}, u32[]{:S(2)}) collective-permute-start(bf16[1,2,20,24,128]{4,3,2,1,0:T(8,128)(2,1)} %get-tuple-element.46), channel_id=1, source_target_pairs={{0,9},{1,8},{2,11},{3,10},{4,13},{5,12},{6,15},{7,14},{8,1},{9,0},... | collective-permute-start | bytes 737288 | tf_op jit(solution)/shard_map/ppermute | solution.py:270
  187.3 16.9 %collective-permute-start.9 = (bf16[1,2,20,24,128]{4,3,2,1,0:T(8,128)(2,1)}, bf16[1,2,20,24,128]{4,3,2,1,0:T(8,128)(2,1)}, u32[]{:S(2)}, u32[]{:S(2)}) collective-permute-start(bf16[1,2,20,24,128]{4,3,2,1,0:T(8,128)(2,1)} %get-tuple-element.47), channel_id=1, source_target_pairs={{0,10},{1,11},{2,8},{3,9},{4,14},{5,15},{6,12},{7,13},{8,2},{9,3},... | collective-permute-start | bytes 737288 | tf_op jit(solution)/shard_map/ppermute | solution.py:270
  209.5 20.9 %collective-permute-done.7.refs_8_ = bf16[1,2,20,24,128]{4,3,2,1,0:T(8,128)(2,1)} collective-permute-done((bf16[1,2,20,24,128]{4,3,2,1,0:T(8,128)(2,1)}, bf16[1,2,20,24,128]{4,3,2,1,0:T(8,128)(2,1)}, u32[]{:S(2)}, u32[]{:S(2)}) %collective-permute-start.7) | collective-permute-done | bytes 245792 | tf_op jit(solution)/shard_map/ppermute | solution.py:270
  230.4 5.2 %collective-permute-start.12 = (bf16[1,2,20,24,128]{4,3,2,1,0:T(8,128)(2,1)}, bf16[1,2,20,24,128]{4,3,2,1,0:T(8,128)(2,1)}, u32[]{:S(2)}, u32[]{:S(2)}) collective-permute-start(bf16[1,2,20,24,128]{4,3,2,1,0:T(8,128)(2,1)} %get-tuple-element.50), channel_id=1, source_target_pairs={{0,13},{1,12},{2,15},{3,14},{4,1},{5,0},{6,3},{7,2},{8,5},{9,4},{1... | collective-permute-start | bytes 737288 | tf_op jit(solution)/shard_map/ppermute | solution.py:270
  235.6 6.4 %collective-permute-start.13 = (bf16[1,2,20,24,128]{4,3,2,1,0:T(8,128)(2,1)}, bf16[1,2,20,24,128]{4,3,2,1,0:T(8,128)(2,1)}, u32[]{:S(2)}, u32[]{:S(2)}) collective-permute-start(bf16[1,2,20,24,128]{4,3,2,1,0:T(8,128)(2,1)} %get-tuple-element.51), channel_id=1, source_target_pairs={{0,14},{1,15},{2,12},{3,13},{4,2},{5,3},{6,0},{7,1},{8,6},{9,7},{1... | collective-permute-start | bytes 737288 | tf_op jit(solution)/shard_map/ppermute | solution.py:270
  242.0 13.0 %collective-permute-start.14 = (bf16[1,2,20,24,128]{4,3,2,1,0:T(8,128)(2,1)}, bf16[1,2,20,24,128]{4,3,2,1,0:T(8,128)(2,1)}, u32[]{:S(2)}, u32[]{:S(2)}) collective-permute-start(bf16[1,2,20,24,128]{4,3,2,1,0:T(8,128)(2,1)} %get-tuple-element.52), channel_id=1, source_target_pairs={{0,15},{1,14},{2,13},{3,12},{4,3},{5,2},{6,1},{7,0},{8,7},{9,6},{1... | collective-permute-start | bytes 737288 | tf_op jit(solution)/shard_map/ppermute | solution.py:270
  256.2 6.0 %collective-permute-done.13.refs_14_ = bf16[1,2,20,24,128]{4,3,2,1,0:T(8,128)(2,1)} collective-permute-done((bf16[1,2,20,24,128]{4,3,2,1,0:T(8,128)(2,1)}, bf16[1,2,20,24,128]{4,3,2,1,0:T(8,128)(2,1)}, u32[]{:S(2)}, u32[]{:S(2)}) %collective-permute-start.13) | collective-permute-done | bytes 245792 | tf_op jit(solution)/shard_map/ppermute | solution.py:270
  262.4 47.1 %middle.2 = (bf16[1,2,20,24,128]{4,3,2,1,0:T(8,128)(2,1)}, bf16[1,2,20,24,128]{4,3,2,1,0:T(8,128)(2,1)}, bf16[1,2,20,24,128]{4,3,2,1,0:T(8,128)(2,1)}, bf16[1,2,...) custom-call(s32[3,24]{1,0:T(4,128)} %slice.18.meta, ...), custom_call_target="tpu_custom_call" | custom-call | tf_op jit(solution)/shard_map/middle/pallas_call | solution.py:155
  330.7 6.6 %collective-permute-done.20.refs_6_ = bf16[1,2,20,24,128]{4,3,2,1,0:T(8,128)(2,1)} collective-permute-done((bf16[1,2,20,24,128]{4,3,2,1,0:T(8,128)(2,1)}, bf16[1,2,20,24,128]{4,3,2,1,0:T(8,128)(2,1)}, u32[]{:S(2)}, u32[]{:S(2)}) %collective-permute-start.20) | collective-permute-done | bytes 245792 | tf_op jit(solution)/shard_map/ppermute | solution.py:270
  341.8 25.5 %collective-permute-done.22.refs_8_ = bf16[1,2,20,24,128]{4,3,2,1,0:T(8,128)(2,1)} collective-permute-done((bf16[1,2,20,24,128]{4,3,2,1,0:T(8,128)(2,1)}, bf16[1,2,20,24,128]{4,3,2,1,0:T(8,128)(2,1)}, u32[]{:S(2)}, u32[]{:S(2)}) %collective-permute-start.22) | collective-permute-done | bytes 245792 | tf_op jit(solution)/shard_map/ppermute | solution.py:270
  367.3 5.9 %collective-permute-start.27 = (bf16[1,2,20,24,128]{4,3,2,1,0:T(8,128)(2,1)}, bf16[1,2,20,24,128]{4,3,2,1,0:T(8,128)(2,1)}, u32[]{:S(2)}, u32[]{:S(2)}) collective-permute-start(bf16[1,2,20,24,128]{4,3,2,1,0:T(8,128)(2,1)} %get-tuple-element.66), channel_id=1, source_target_pairs={{0,13},{1,12},{2,15},{3,14},{4,1},{5,0},{6,3},{7,2},{8,5},{9,4},{1... | collective-permute-start | bytes 737288 | tf_op jit(solution)/shard_map/ppermute | solution.py:270
  373.2 5.4 %collective-permute-start.28 = (bf16[1,2,20,24,128]{4,3,2,1,0:T(8,128)(2,1)}, bf16[1,2,20,24,128]{4,3,2,1,0:T(8,128)(2,1)}, u32[]{:S(2)}, u32[]{:S(2)}) collective-permute-start(bf16[1,2,20,24,128]{4,3,2,1,0:T(8,128)(2,1)} %get-tuple-element.67), channel_id=1, source_target_pairs={{0,14},{1,15},{2,12},{3,13},{4,2},{5,3},{6,0},{7,1},{8,6},{9,7},{1... | collective-permute-start | bytes 737288 | tf_op jit(solution)/shard_map/ppermute | solution.py:270
  379.0 16.2 %collective-permute-start.29 = (bf16[1,2,20,24,128]{4,3,2,1,0:T(8,128)(2,1)}, bf16[1,2,20,24,128]{4,3,2,1,0:T(8,128)(2,1)}, u32[]{:S(2)}, u32[]{:S(2)}) collective-permute-start(bf16[1,2,20,24,128]{4,3,2,1,0:T(8,128)(2,1)} %get-tuple-element.68), channel_id=1, source_target_pairs={{0,15},{1,14},{2,13},{3,12},{4,3},{5,2},{6,1},{7,0},{8,7},{9,6},{1... | collective-permute-start | bytes 737288 | tf_op jit(solution)/shard_map/ppermute | solution.py:270
  398.5 16.2 %place.2.refs_17_ = bf16[2560,1280]{1,0:T(8,128)(2,1)} custom-call(s32[2,16]{1,0:T(2,128)} %pad_add_fusion.2.peers, bf16[16,2,20,16,128]{4,3,2,1,0:T(8,128)(2,1)} %copy-done.3, s32[512,1]{1,0:T(8,128)} %add.289.refs_1_), custom_call_target="tpu_custom_call" | custom-call | tf_op jit(solution)/shard_map/place/pallas_call | solution.py:226
  414.8 20.2 %place.3 = bf16[32,40,2,1280]{3,2,1,0:T(2,128)(2,1)} custom-call(s32[2,16]{1,0:T(2,128)} %pad_add_fusion.1.peers, bf16[1,2,20,24,128]{4,3,2,1,0:T(8,128)(2,1)} %get-tuple-element.53.refs_0_, bf16[1,2,20,24,128]{4,3,2,1,0:T(8,128)(2,1)} %copy-done.7, bf16[1,2,20,24,128]{4,3,2,1,0:T(8,128)(2,1)} %copy-done.8, bf16[1,2,20,24,128]{4,3,2,1,0:T(8,128)(2,1)} %copy-done.9, ...), custom_call_target="tpu_custom_call" | custom-call | tf_op jit(solution)/shard_map/place/pallas_call | solution.py:226
  (126 shorter events, 55.7 us)
Async XLA Ops:
  16.3 57.5 %all-to-all-start = ((bf16[16,2,20,16,128]{4,3,2,1,0:T(8,128)(2,1)}), bf16[16,2,20,16,128]{4,3,2,1,0:T(8,128)(2,1)S(1)}, u32[]{:S(2)}, u32[]{:S(2)}) async-start(bf16[16,2,20,16,128]{4,3,2,1,0:T(8,128)(2,1)} %dft.3), calls=%async_computation | async-start | bytes 5242880 | tf_op jit(solution)/shard_map/all_to_all | solution.py:332
  108.4 288.6 %all-to-all-start.1 = ((bf16[16,2,20,16,128]{4,3,2,1,0:T(8,128)(2,1)}), bf16[16,2,20,16,128]{4,3,2,1,0:T(8,128)(2,1)S(1)}, u32[]{:S(2)}, u32[]{:S(2)}) async-start(bf16[16,2,20,16,128]{4,3,2,1,0:T(8,128)(2,1)} %middle.3), calls=%async_computation.1 | async-start | bytes 5242880 | tf_op jit(solution)/shard_map/all_to_all | solution.py:332
  143.0 20.9 %collective-permute-start.2 = (bf16[1,2,20,24,128]{4,3,2,1,0:T(8,128)(2,1)}, bf16[1,2,20,24,128]{4,3,2,1,0:T(8,128)(2,1)S(1)}, u32[]{:S(2)}, u32[]{:S(2)}) collective-permute-start(bf16[1,2,20,24,128]{4,3,2,1,0:T(8,128)(2,1)} %get-tuple-element.40), channel_id=1, source_target_pairs={{0,3},{1,2},{2,1},{3,0},{4,7},{5,6},{6,5},{7,4},{8,11},{9,10},{10,... | collective-permute-start | bytes 737288 | tf_op jit(solution)/shard_map/ppermute | solution.py:270
  143.0 32.3 %collective-permute-start.3 = (bf16[1,2,20,24,128]{4,3,2,1,0:T(8,128)(2,1)}, bf16[1,2,20,24,128]{4,3,2,1,0:T(8,128)(2,1)}, u32[]{:S(2)}, u32[]{:S(2)}) collective-permute-start(bf16[1,2,20,24,128]{4,3,2,1,0:T(8,128)(2,1)} %get-tuple-element.41), channel_id=1, source_target_pairs={{0,4},{1,5},{2,6},{3,7},{4,8},{5,9},{6,10},{7,11},{8,12},{9,13},{1... | collective-permute-start | bytes 737288 | tf_op jit(solution)/shard_map/ppermute | solution.py:270
  144.7 42.6 %collective-permute-start.4 = (bf16[1,2,20,24,128]{4,3,2,1,0:T(8,128)(2,1)}, bf16[1,2,20,24,128]{4,3,2,1,0:T(8,128)(2,1)}, u32[]{:S(2)}, u32[]{:S(2)}) collective-permute-start(bf16[1,2,20,24,128]{4,3,2,1,0:T(8,128)(2,1)} %get-tuple-element.42), channel_id=1, source_target_pairs={{0,5},{1,4},{2,7},{3,6},{4,9},{5,8},{6,11},{7,10},{8,13},{9,12},{1... | collective-permute-start | bytes 737288 | tf_op jit(solution)/shard_map/ppermute | solution.py:270
  145.9 58.3 %collective-permute-start.5 = (bf16[1,2,20,24,128]{4,3,2,1,0:T(8,128)(2,1)}, bf16[1,2,20,24,128]{4,3,2,1,0:T(8,128)(2,1)}, u32[]{:S(2)}, u32[]{:S(2)}) collective-permute-start(bf16[1,2,20,24,128]{4,3,2,1,0:T(8,128)(2,1)} %get-tuple-element.43), channel_id=1, source_target_pairs={{0,6},{1,7},{2,4},{3,5},{4,10},{5,11},{6,8},{7,9},{8,14},{9,15},{1... | collective-permute-start | bytes 737288 | tf_op jit(solution)/shard_map/ppermute | solution.py:270
  155.9 53.5 %collective-permute-start.6 = (bf16[1,2,20,24,128]{4,3,2,1,0:T(8,128)(2,1)}, bf16[1,2,20,24,128]{4,3,2,1,0:T(8,128)(2,1)}, u32[]{:S(2)}, u32[]{:S(2)}) collective-permute-start(bf16[1,2,20,24,128]{4,3,2,1,0:T(8,128)(2,1)} %get-tuple-element.44), channel_id=1, source_target_pairs={{0,7},{1,6},{2,5},{3,4},{4,11},{5,10},{6,9},{7,8},{8,15},{9,14},{1... | collective-permute-start | bytes 737288 | tf_op jit(solution)/shard_map/ppermute | solution.py:270
  163.8 66.6 %collective-permute-start.7 = (bf16[1,2,20,24,128]{4,3,2,1,0:T(8,128)(2,1)}, bf16[1,2,20,24,128]{4,3,2,1,0:T(8,128)(2,1)}, u32[]{:S(2)}, u32[]{:S(2)}) collective-permute-start(bf16[1,2,20,24,128]{4,3,2,1,0:T(8,128)(2,1)} %get-tuple-element.45), channel_id=1, source_target_pairs={{0,8},{1,9},{2,10},{3,11},{4,12},{5,13},{6,14},{7,15},{8,0},{9,1},... | collective-permute-start | bytes 737288 | tf_op jit(solution)/shard_map/ppermute | solution.py:270
  175.2 60.4 %collective-permute-start.8 = (bf16[1,2,20,24,128]{4,3,2,1,0:T(8,128)(2,1)}, bf16[1,2,20,24,128]{4,3,2,1,0:T(8,128)(2,1)}, u32[]{:S(2)}, u32[]{:S(2)}) collective-permute-start(bf16[1,2,20,24,128]{4,3,2,1,0:T(8,128)(2,1)} %get-tuple-element.46), channel_id=1, source_target_pairs={{0,9},{1,8},{2,11},{3,10},{4,13},{5,12},{6,15},{7,14},{8,1},{9,0},... | collective-permute-start | bytes 737288 | tf_op jit(solution)/shard_map/ppermute | solution.py:270
  187.3 54.7 %collective-permute-start.9 = (bf16[1,2,20,24,128]{4,3,2,1,0:T(8,128)(2,1)}, bf16[1,2,20,24,128]{4,3,2,1,0:T(8,128)(2,1)}, u32[]{:S(2)}, u32[]{:S(2)}) collective-permute-start(bf16[1,2,20,24,128]{4,3,2,1,0:T(8,128)(2,1)} %get-tuple-element.47), channel_id=1, source_target_pairs={{0,10},{1,11},{2,8},{3,9},{4,14},{5,15},{6,12},{7,13},{8,2},{9,3},... | collective-permute-start | bytes 737288 | tf_op jit(solution)/shard_map/ppermute | solution.py:270
  204.2 52.0 %collective-permute-start.10 = (bf16[1,2,20,24,128]{4,3,2,1,0:T(8,128)(2,1)}, bf16[1,2,20,24,128]{4,3,2,1,0:T(8,128)(2,1)}, u32[]{:S(2)}, u32[]{:S(2)}) collective-permute-start(bf16[1,2,20,24,128]{4,3,2,1,0:T(8,128)(2,1)} %get-tuple-element.48), channel_id=1, source_target_pairs={{0,11},{1,10},{2,9},{3,8},{4,15},{5,14},{6,13},{7,12},{8,3},{9,2},... | collective-permute-start | bytes 737288 | tf_op jit(solution)/shard_map/ppermute | solution.py:270
  209.3 46.9 %collective-permute-start.11 = (bf16[1,2,20,24,128]{4,3,2,1,0:T(8,128)(2,1)}, bf16[1,2,20,24,128]{4,3,2,1,0:T(8,128)(2,1)}, u32[]{:S(2)}, u32[]{:S(2)}) collective-permute-start(bf16[1,2,20,24,128]{4,3,2,1,0:T(8,128)(2,1)} %get-tuple-element.49), channel_id=1, source_target_pairs={{0,12},{1,13},{2,14},{3,15},{4,0},{5,1},{6,2},{7,3},{8,4},{9,5},{1... | collective-permute-start | bytes 737288 | tf_op jit(solution)/shard_map/ppermute | solution.py:270
  230.4 25.8 %collective-permute-start.12 = (bf16[1,2,20,24,128]{4,3,2,1,0:T(8,128)(2,1)}, bf16[1,2,20,24,128]{4,3,2,1,0:T(8,128)(2,1)}, u32[]{:S(2)}, u32[]{:S(2)}) collective-permute-start(bf16[1,2,20,24,128]{4,3,2,1,0:T(8,128)(2,1)} %get-tuple-element.50), channel_id=1, source_target_pairs={{0,13},{1,12},{2,15},{3,14},{4,1},{5,0},{6,3},{7,2},{8,5},{9,4},{1... | collective-permute-start | bytes 737288 | tf_op jit(solution)/shard_map/ppermute | solution.py:270
  235.6 26.6 %collective-permute-start.13 = (bf16[1,2,20,24,128]{4,3,2,1,0:T(8,128)(2,1)}, bf16[1,2,20,24,128]{4,3,2,1,0:T(8,128)(2,1)}, u32[]{:S(2)}, u32[]{:S(2)}) collective-permute-start(bf16[1,2,20,24,128]{4,3,2,1,0:T(8,128)(2,1)} %get-tuple-element.51), channel_id=1, source_target_pairs={{0,14},{1,15},{2,12},{3,13},{4,2},{5,3},{6,0},{7,1},{8,6},{9,7},{1... | collective-permute-start | bytes 737288 | tf_op jit(solution)/shard_map/ppermute | solution.py:270
  242.0 20.4 %collective-permute-start.14 = (bf16[1,2,20,24,128]{4,3,2,1,0:T(8,128)(2,1)}, bf16[1,2,20,24,128]{4,3,2,1,0:T(8,128)(2,1)}, u32[]{:S(2)}, u32[]{:S(2)}) collective-permute-start(bf16[1,2,20,24,128]{4,3,2,1,0:T(8,128)(2,1)} %get-tuple-element.52), channel_id=1, source_target_pairs={{0,15},{1,14},{2,13},{3,12},{4,3},{5,2},{6,1},{7,0},{8,7},{9,6},{1... | collective-permute-start | bytes 737288 | tf_op jit(solution)/shard_map/ppermute | solution.py:270
  317.0 20.2 %collective-permute-start.20 = (bf16[1,2,20,24,128]{4,3,2,1,0:T(8,128)(2,1)}, bf16[1,2,20,24,128]{4,3,2,1,0:T(8,128)(2,1)}, u32[]{:S(2)}, u32[]{:S(2)}) collective-permute-start(bf16[1,2,20,24,128]{4,3,2,1,0:T(8,128)(2,1)} %get-tuple-element.59), channel_id=1, source_target_pairs={{0,6},{1,7},{2,4},{3,5},{4,10},{5,11},{6,8},{7,9},{8,14},{9,15},{1... | collective-permute-start | bytes 737288 | tf_op jit(solution)/shard_map/ppermute | solution.py:270
  325.9 41.4 %collective-permute-start.22 = (bf16[1,2,20,24,128]{4,3,2,1,0:T(8,128)(2,1)}, bf16[1,2,20,24,128]{4,3,2,1,0:T(8,128)(2,1)}, u32[]{:S(2)}, u32[]{:S(2)}) collective-permute-start(bf16[1,2,20,24,128]{4,3,2,1,0:T(8,128)(2,1)} %get-tuple-element.61), channel_id=1, source_target_pairs={{0,8},{1,9},{2,10},{3,11},{4,12},{5,13},{6,14},{7,15},{8,0},{9,1},... | collective-permute-start | bytes 737288 | tf_op jit(solution)/shard_map/ppermute | solution.py:270
  326.6 46.6 %collective-permute-start.23 = (bf16[1,2,20,24,128]{4,3,2,1,0:T(8,128)(2,1)}, bf16[1,2,20,24,128]{4,3,2,1,0:T(8,128)(2,1)}, u32[]{:S(2)}, u32[]{:S(2)}) collective-permute-start(bf16[1,2,20,24,128]{4,3,2,1,0:T(8,128)(2,1)} %get-tuple-element.62), channel_id=1, source_target_pairs={{0,9},{1,8},{2,11},{3,10},{4,13},{5,12},{6,15},{7,14},{8,1},{9,0},... | collective-permute-start | bytes 737288 | tf_op jit(solution)/shard_map/ppermute | solution.py:270
  329.9 49.0 %collective-permute-start.24 = (bf16[1,2,20,24,128]{4,3,2,1,0:T(8,128)(2,1)}, bf16[1,2,20,24,128]{4,3,2,1,0:T(8,128)(2,1)}, u32[]{:S(2)}, u32[]{:S(2)}) collective-permute-start(bf16[1,2,20,24,128]{4,3,2,1,0:T(8,128)(2,1)} %get-tuple-element.63), channel_id=1, source_target_pairs={{0,10},{1,11},{2,8},{3,9},{4,14},{5,15},{6,12},{7,13},{8,2},{9,3},... | collective-permute-start | bytes 737288 | tf_op jit(solution)/shard_map/ppermute | solution.py:270
  337.2 77.5 %collective-permute-start.25 = (bf16[1,2,20,24,128]{4,3,2,1,0:T(8,128)(2,1)}, bf16[1,2,20,24,128]{4,3,2,1,0:T(8,128)(2,1)}, u32[]{:S(2)}, u32[]{:S(2)}) collective-permute-start(bf16[1,2,20,24,128]{4,3,2,1,0:T(8,128)(2,1)} %get-tuple-element.64), channel_id=1, source_target_pairs={{0,11},{1,10},{2,9},{3,8},{4,15},{5,14},{6,13},{7,12},{8,3},{9,2},... | collective-permute-start | bytes 737288 | tf_op jit(solution)/shard_map/ppermute | solution.py:270
  341.8 72.9 %collective-permute-start.26 = (bf16[1,2,20,24,128]{4,3,2,1,0:T(8,128)(2,1)}, bf16[1,2,20,24,128]{4,3,2,1,0:T(8,128)(2,1)}, u32[]{:S(2)}, u32[]{:S(2)}) collective-permute-start(bf16[1,2,20,24,128]{4,3,2,1,0:T(8,128)(2,1)} %get-tuple-element.65), channel_id=1, source_target_pairs={{0,12},{1,13},{2,14},{3,15},{4,0},{5,1},{6,2},{7,3},{8,4},{9,5},{1... | collective-permute-start | bytes 737288 | tf_op jit(solution)/shard_map/ppermute | solution.py:270
  367.3 47.4 %collective-permute-start.27 = (bf16[1,2,20,24,128]{4,3,2,1,0:T(8,128)(2,1)}, bf16[1,2,20,24,128]{4,3,2,1,0:T(8,128)(2,1)}, u32[]{:S(2)}, u32[]{:S(2)}) collective-permute-start(bf16[1,2,20,24,128]{4,3,2,1,0:T(8,128)(2,1)} %get-tuple-element.66), channel_id=1, source_target_pairs={{0,13},{1,12},{2,15},{3,14},{4,1},{5,0},{6,3},{7,2},{8,5},{9,4},{1... | collective-permute-start | bytes 737288 | tf_op jit(solution)/shard_map/ppermute | solution.py:270
  373.2 41.5 %collective-permute-start.28 = (bf16[1,2,20,24,128]{4,3,2,1,0:T(8,128)(2,1)}, bf16[1,2,20,24,128]{4,3,2,1,0:T(8,128)(2,1)}, u32[]{:S(2)}, u32[]{:S(2)}) collective-permute-start(bf16[1,2,20,24,128]{4,3,2,1,0:T(8,128)(2,1)} %get-tuple-element.67), channel_id=1, source_target_pairs={{0,14},{1,15},{2,12},{3,13},{4,2},{5,3},{6,0},{7,1},{8,6},{9,7},{1... | collective-permute-start | bytes 737288 | tf_op jit(solution)/shard_map/ppermute | solution.py:270
  379.0 35.7 %collective-permute-start.29 = (bf16[1,2,20,24,128]{4,3,2,1,0:T(8,128)(2,1)}, bf16[1,2,20,24,128]{4,3,2,1,0:T(8,128)(2,1)}, u32[]{:S(2)}, u32[]{:S(2)}) collective-permute-start(bf16[1,2,20,24,128]{4,3,2,1,0:T(8,128)(2,1)} %get-tuple-element.68), channel_id=1, source_target_pairs={{0,15},{1,14},{2,13},{3,12},{4,3},{5,2},{6,1},{7,0},{8,7},{9,6},{1... | collective-permute-start | bytes 737288 | tf_op jit(solution)/shard_map/ppermute | solution.py:270
  (23 other events, 981.6 us)

commit v3 on v2

v3 whole, which is shorter than its diff:
```python
import functools
import math

import jax
import jax.numpy as jnp
from jax import lax
from jax.experimental import pallas as pl
from jax.experimental.pallas import tpu as pltpu
from jax.sharding import PartitionSpec as P


LBLK = 64
LANES = 128
TILE = 8
AXES = ("wave", "lev")
NT = (((1,), (1,)), ((), ()))
NN = (((1,), (0,)), ((), ()))


def dot(a, b, dims=NN):
    return lax.dot_general(a, b, dims, preferred_element_type=jnp.float32)


def cosine_rows(freq_ref, first, count, lon_count):
    freq = freq_ref[pl.ds(first, count), :]
    row = lax.broadcasted_iota(jnp.int32, (count, 1), 0) + first
    phase = ((row // TILE) % 2).astype(jnp.float32) * (lon_count // 4)
    longitude = lax.broadcasted_iota(jnp.int32, (count, lon_count), 1).astype(jnp.float32)
    turns = freq * longitude + phase
    whole = jnp.floor(turns * (1.0 / lon_count) + 0.5)
    rest = jnp.abs(turns - whole * lon_count) * (1.0 / lon_count)
    angle = (0.25 - rest) * (2.0 * math.pi)
    square = angle * angle
    value = jnp.full_like(square, -1.0 / 39916800.0)
    for term in (1.0 / 362880.0, -1.0 / 5040.0, 1.0 / 120.0, -1.0 / 6.0, 1.0):
        value = value * square + term
    return (value * angle * (1.0 / math.sqrt(lon_count))).astype(jnp.bfloat16)


def units(depths):
    starts, first = [], 0
    for depth in depths:
        starts.append((first, first + depth))
        first += 2 * depth
    return starts, first


def dft_kernel(lats_ref, *refs, depths, pairs, slots):
    views, freq, outs, table = refs[:slots], refs[slots], refs[slots + 1 : -1], refs[-1]
    fields, lon_count = views[0].shape[0], views[0].shape[3]
    step = pl.program_id(0)

    @pl.when(step == 0)
    def _():
        rows = 4 * TILE if table.shape[0] % (4 * TILE) == 0 else 2 * TILE

        @pl.loop(0, table.shape[0] // rows)
        def _(i):
            first = pl.multiple_of(i * rows, rows)
            table[pl.ds(first, rows), :] = cosine_rows(freq, first, rows, lon_count)

    values = [view[:, 0].reshape(2 * fields, lon_count) for view in views]
    spectra = dot(table[...], jnp.concatenate(values, 0), NT)
    spectra = spectra.reshape(-1, len(depths), 2, TILE, pairs * LANES)
    starts, _ = units(depths)
    each = outs[0].shape[0]

    def store(tile, pair, where):
        for part in range(2):
            block = spectra[:, tile, part, :, pair * LANES : (pair + 1) * LANES]
            block = block.astype(jnp.bfloat16)
            for piece, out in enumerate(outs):
                out[:, starts[tile][part] + where] = block[piece * each : (piece + 1) * each]

    for pair in range(pairs):
        where = step * pairs + pair
        for tile, depth in enumerate(depths):
            pl.when(where < depth)(functools.partial(store, tile, pair, where))


def dft(grid, order, freq, depths, owners, low, separate):
    fields, lats, _, lon_count = grid.shape
    count = lats // low
    pairs = 2 if count % 2 == 0 else 1
    slots = pairs * low
    pieces, each = (owners, 1) if separate else (1, owners)
    shape = (each, units(depths)[1], TILE, LANES)

    def view(slot):
        return pl.BlockSpec(
            (fields, 1, 2, lon_count), lambda i, order: (0, order[i * slots + slot], 0, 0)
        )

    return pl.pallas_call(
        functools.partial(dft_kernel, depths=depths, pairs=pairs, slots=slots),
        grid_spec=pltpu.PrefetchScalarGridSpec(
            num_scalar_prefetch=1,
            grid=(count // pairs,),
            in_specs=[view(slot) for slot in range(slots)]
            + [pl.BlockSpec(freq.shape, lambda i, _: (0, 0))],
            out_specs=[pl.BlockSpec(shape, lambda i, _: (0, 0, 0, 0))] * pieces,
            scratch_shapes=[pltpu.VMEM((freq.shape[0], lon_count), jnp.bfloat16)],
        ),
        out_shape=[jax.ShapeDtypeStruct(shape, jnp.bfloat16)] * pieces,
        name="dft",
    )(order, *([grid] * slots), freq)


def middle_kernel(meta, peers, *refs, levels, pieces, depths, count):
    data, refs = refs[:pieces], refs[pieces:]
    legendre, select, into, back, implicit = refs[:5]
    out, (held, made) = refs[5 : 5 + pieces], refs[5 + pieces :]
    step = pl.program_id(0)
    each = data[0].shape[0]
    owners = each * pieces
    starts, _ = units(depths)
    groups = owners // levels
    half = LANES // 2
    lat_count, row_count = legendre.shape[1], legendre.shape[2]

    slots = groups * count
    tile_rows = 2 * levels * slots * TILE

    def place_of(owner, tile, part, first, rows):
        near = ((owner % levels) * 2 + part) * groups + owner // levels
        start = near * (count * TILE) + (tile * tile_rows + first * TILE)
        return pl.ds(pl.multiple_of(start, TILE), rows * TILE)

    @pl.when(step == 0)
    def _():
        for piece in range(owners):
            owner = peers[0, piece]
            for tile, depth in enumerate(depths):
                for part in range(2):
                    first = starts[tile][part]
                    block = data[piece // each][piece % each, first : first + depth]
                    block = block.astype(jnp.float32).reshape(-1, LANES)
                    held[place_of(owner, tile, part, 0, depth), :] = block
                    if depth < count:
                        rest = count - depth
                        empty = jnp.zeros((rest * TILE, LANES), jnp.float32)
                        held[place_of(owner, tile, part, depth, rest), :] = empty

    origin = (step // TILE) * tile_rows + step % TILE

    def column(combo):
        return pl.ds(origin + combo * slots * TILE, slots, stride=TILE)

    wavenum, trim = meta[0, step], meta[1, step]
    north, south = [], []
    for combo in range(2 * levels):
        block = held[column(combo), :]
        turned = block.T
        north.append(turned[:half])
        south.append(turned[half:])
    first = jnp.concatenate(north, 0).astype(jnp.bfloat16)
    second = jnp.concatenate(south, 0).astype(jnp.bfloat16)
    basis = legendre[0]
    ordered = dot(first, select[0]) + dot(second, select[1])
    latitude = lax.broadcasted_iota(jnp.int32, (1, lat_count), 1)
    keep = latitude >= LBLK * trim
    ordered = jnp.where(keep, ordered, 0.0).astype(jnp.bfloat16)
    coeffs = dot(ordered, basis)
    row = lax.broadcasted_iota(jnp.int32, (1, row_count), 1)
    degree = (row + wavenum).astype(jnp.float32)
    factor = degree * (degree + 1.0) * (1.0 / float(row_count * (row_count - 1)))
    south_side = lax.broadcasted_iota(jnp.int32, (coeffs.shape[0], 1), 0) % 2
    flip = (south_side * (row % 2)) == 1
    coeffs = jnp.where(flip, -coeffs, coeffs).astype(jnp.bfloat16)
    modal = dot(into[...], coeffs)
    scaled = (modal / (1.0 + factor * implicit[...])).astype(jnp.bfloat16)
    solved = dot(back[...], scaled)
    solved = jnp.where(row + wavenum < row_count, solved, 0.0)
    solved = jnp.where(flip, -solved, solved).astype(jnp.bfloat16)
    sides = dot(solved, basis, NT)
    sides = jnp.where(keep, sides, 0.0).astype(jnp.bfloat16)
    first = dot(sides, select[0], NT)
    second = dot(sides, select[1], NT)
    for combo in range(2 * levels):
        span = slice(combo * half, (combo + 1) * half)
        block = jnp.concatenate([first[span], second[span]], 0).T
        made[column(combo), :] = block

    @pl.when(step == pl.num_programs(0) - 1)
    def _():
        for piece in range(owners):
            owner = peers[1, piece]
            for tile, depth in enumerate(depths):
                for part in range(2):
                    first = starts[tile][part]
                    block = made[place_of(owner, tile, part, 0, depth), :]
                    block = block.reshape(depth, TILE, LANES).astype(jnp.bfloat16)
                    out[piece // each][piece % each, first : first + depth] = block


def middle(data, meta, peers, legendre, select, into, back, implicit, levels, depths, count):
    each = data[0].shape[0]
    whole = lambda a: pl.BlockSpec(a.shape, lambda i, *_: (0,) * a.ndim)
    rows = each * len(data) * 2 * count * TILE * len(depths)
    return pl.pallas_call(
        functools.partial(
            middle_kernel, levels=levels, pieces=len(data), depths=depths, count=count
        ),
        grid_spec=pltpu.PrefetchScalarGridSpec(
            num_scalar_prefetch=2,
            grid=(len(depths) * TILE,),
            in_specs=[whole(a) for a in data]
            + [pl.BlockSpec((1,) + legendre.shape[1:], lambda i, meta, _: (meta[2, i], 0, 0))]
            + [whole(a) for a in (select, into, back, implicit)],
            out_specs=[whole(a) for a in data],
            scratch_shapes=[pltpu.VMEM((rows, LANES), jnp.float32)] * 2,
        ),
        out_shape=[jax.ShapeDtypeStruct(a.shape, jnp.bfloat16) for a in data],
        name="middle",
    )(meta, peers, *data, legendre, select, into, back, implicit)


def place_kernel(peers, rank, *refs, pieces, final, with_start, split, depths, low, batch):
    blocks, refs = refs[:pieces], refs[pieces:]
    target, refs = refs[0], refs[1:]
    start = refs[0] if with_start else None
    out, table, gathered = refs[-3:]
    per = table.shape[0] // split
    each = blocks[0].shape[0]
    span_rows = 2 * TILE * len(depths)
    span = LANES // low
    starts, _ = units(depths)
    step = pl.program_id(0)

    @pl.when(step == 0)
    def _():
        column = lax.broadcasted_iota(jnp.int32, table.shape, 1)
        goal = target[...]
        for piece in range(split):
            rows = slice(piece * per, (piece + 1) * per)
            wanted = goal[rows] - piece * table.shape[1]
            table[rows, :] = jnp.where(column[rows] == wanted, 1.0, 0.0).astype(jnp.bfloat16)

    lane = lax.broadcasted_iota(jnp.int32, (1, LANES), 1) // span
    turned = []
    for item in range(batch):
        merged = None
        for slot in range(low):
            index = rank[(step * batch + item) * low + slot]
            where, side = index // low, index % low
            for piece in range(each * pieces):
                base = peers[0, piece] * span_rows
                for tile, depth in enumerate(depths):
                    near = jnp.minimum(where, depth - 1)
                    for part in range(2):
                        unit = starts[tile][part] + near
                        block = blocks[piece // each][piece % each, unit].astype(jnp.float32)
                        if depth < max_depth(rank, low):
                            block = jnp.where(where < depth, block, 0.0)
                        first = base + (2 * tile + part) * TILE
                        gathered[slot, pl.ds(pl.multiple_of(first, TILE), TILE), :] = block
            values = pltpu.roll(gathered[slot], ((slot - side) % low) * span, 1)
            merged = values if merged is None else jnp.where(lane == slot, values, merged)
        turned.append(merged.T.astype(jnp.bfloat16))
    rows = jnp.concatenate(turned, 0)
    placed = []
    for piece in range(split):
        part = slice(piece * per, (piece + 1) * per)
        placed.append(dot(rows[:, part], table[part, :]))
    placed = jnp.concatenate(placed, 1) if split > 1 else placed[0]
    placed = placed.astype(jnp.bfloat16)
    if with_start:
        placed = placed + start[...]
    if not final:
        out[...] = placed
        return
    fields = out.shape[0]
    for slot in range(batch * low):
        block = placed[slot * 2 * fields : (slot + 1) * 2 * fields]
        out[:, slot] = block.reshape(fields, 2, block.shape[1])


def max_depth(rank, low):
    return rank.shape[0] // low


def place(blocks, peers, rank, target, start, columns, fields, low, final, depths):
    each = blocks[0].shape[0]
    owners = each * len(blocks)
    count = rank.shape[0] // low
    batch = max(b for b in (1, 2, 4) if count % b == 0)
    split = 2 if owners % 2 == 0 and (columns // 2) % LANES == 0 else 1
    specs = [pl.BlockSpec(b.shape, lambda i, *_: (0, 0, 0, 0)) for b in blocks]
    specs.append(pl.BlockSpec(target.shape, lambda i, *_: (0, 0)))
    args = list(blocks) + [target]
    if start is not None:
        specs.append(pl.BlockSpec((batch * LANES, columns), lambda i, *_: (i, 0)))
        args.append(start)
    if final:
        out_spec = pl.BlockSpec((fields, low * batch, 2, columns), lambda i, *_: (0, i, 0, 0))
        out_shape = jax.ShapeDtypeStruct((fields, low * count, 2, columns), jnp.bfloat16)
    else:
        out_spec = pl.BlockSpec((batch * LANES, columns), lambda i, *_: (i, 0))
        out_shape = jax.ShapeDtypeStruct((LANES * count, columns), jnp.bfloat16)
    rows = target.shape[0]
    return pl.pallas_call(
        functools.partial(
            place_kernel,
            pieces=len(blocks),
            final=final,
            with_start=start is not None,
            split=split,
            depths=depths,
            low=low,
            batch=batch,
        ),
        grid_spec=pltpu.PrefetchScalarGridSpec(
            num_scalar_prefetch=2,
            grid=(count // batch,),
            in_specs=specs,
            out_specs=out_spec,
            scratch_shapes=[
                pltpu.VMEM((rows, columns // split), jnp.bfloat16),
                pltpu.VMEM((low, rows, LANES), jnp.float32),
            ],
        ),
        out_shape=out_shape,
        name="place",
    )(peers, rank, *args)


def chunk_tiles(tiles):
    first = max(1, tiles * 2 // 5)
    return [first, tiles - first] if tiles > first else [first]


def partner(me, piece, groups, levels, back):
    fast = 2 * levels if groups % 2 == 0 else levels
    slow = groups * levels // fast
    far = piece // fast
    high = (me // fast + (slow - far if back else far)) % slow
    near = me % fast
    if fast & (fast - 1) == 0:
        low = near ^ (piece % fast)
    else:
        low = (near + (fast - piece % fast if back else piece % fast)) % fast
    return high * fast + low


def shift(pieces, groups, levels):
    owners = groups * levels
    moved = [pieces[0]]
    for piece in range(1, owners):
        pairs = [(i, partner(i, piece, groups, levels, False)) for i in range(owners)]
        moved.append(lax.ppermute(pieces[piece], AXES, pairs))
    return moved


def ordered(keys):
    rank = jnp.sum((keys[:, None, :] < keys[:, :, None]).astype(jnp.int32), 2)
    spot = jnp.arange(keys.shape[1], dtype=jnp.int32)
    chosen = jnp.where(rank[:, :, None] == spot, keys[:, :, None], 0)
    return jnp.sum(chosen, 1), rank


def profiles(tiles, count):
    shares = [(0.4, 1.0), (0.6, 0.95), (0.8, 0.8), (1.0, 0.6)]
    small = []
    for tile in range(tiles):
        share = next(share for bound, share in shares if tile + 0.5 < bound * tiles)
        small.append(min(count, math.ceil(share * count - 1e-6)))
    return [small, [count] * tiles]


def local(grid, lat_order, wave_order, trim, legendre, modes_in, modes_out, implicit):
    fields, lats, _, lon_count = grid.shape
    per_device, row_count, lat_count = legendre.shape
    levels = lax.axis_size("lev")
    groups = lax.axis_size("wave")
    owners = groups * levels
    low = LANES // (2 * fields)
    count = lats // low
    share = per_device // levels
    tiles = -(-share // TILE)
    group = lax.axis_index("wave")
    me = group * levels + lax.axis_index("lev")

    trims = trim[wave_order].reshape(groups, per_device)
    near = jnp.arange(per_device, dtype=jnp.int32)
    keys = (trims * per_device + near) * row_count + wave_order.reshape(groups, per_device)
    keys, _ = ordered(keys)
    keys = keys.reshape(groups, share, levels).transpose(0, 2, 1).reshape(owners, share)
    slot = jnp.arange(tiles * TILE, dtype=jnp.int32)
    keys = keys[:, jnp.minimum(slot, share - 1)]
    owner_waves, owner_near = keys % row_count, keys // row_count % per_device
    owner_trims = keys // (row_count * per_device)
    table = (lat_count - 1 - lat_order).reshape(groups, lats)
    table, rank = ordered(table * lats + jnp.arange(lats, dtype=jnp.int32))
    slot_lats, slot_order = lat_count - 1 - table // lats, table % lats
    order = lax.dynamic_slice_in_dim(slot_order, group, 1)[0]
    rank = lax.dynamic_slice_in_dim(rank, group, 1)[0]

    mine = lax.dynamic_slice_in_dim(keys, me, 1)[0]
    meta = jnp.stack(
        [mine % row_count, mine // (row_count * per_device), mine // row_count % per_device]
    )
    first_column = (jnp.arange(owners, dtype=jnp.int32) // levels * (2 * per_device))[:, None]
    columns = jnp.where(slot < share, first_column + 2 * owner_near, -4 * per_device * owners)

    piece = jnp.arange(owners, dtype=jnp.int32)
    natural = jnp.stack([piece, piece])
    paired = jnp.stack(
        [partner(me, piece, groups, levels, back) for back in (True, False)]
    )
    peers = [natural, paired]

    freqs, metas, targets, spans, first = [], [], [], [], 0
    for which, size in enumerate(chunk_tiles(tiles)):
        spans.append(slice(first, first + size))
        span = slice(first * TILE, (first + size) * TILE)
        shape = (owners, size, 2, TILE)
        waves = owner_waves if which == 0 else owner_waves[paired[1]]
        waves = jnp.broadcast_to(waves[:, span].reshape(owners, size, 1, TILE), shape)
        freqs.append(waves.reshape(-1, 1).astype(jnp.float32))
        goal = columns[:, span].reshape(owners, size, 1, TILE)
        goal = goal + jnp.arange(2, dtype=jnp.int32)[:, None]
        targets.append(jnp.broadcast_to(goal, shape).reshape(-1, 1))
        metas.append(meta[:, span])
        first += size

    slots = slot_lats.reshape(groups * count, low).T
    select = (slots[:, :, None] == jnp.arange(lat_count, dtype=jnp.int32)).astype(jnp.bfloat16)
    same = jnp.eye(2, dtype=jnp.bfloat16)
    split_in = modes_in.reshape(-1, levels, fields)
    into = jnp.einsum("klf,cd->ckldf", split_in, same)
    into = jnp.repeat(into.reshape(2 * levels * fields, 2 * levels * fields), 2, axis=1)
    split_out = modes_out.reshape(levels, fields, -1)
    back = jnp.einsum("lfk,cd->lcfdk", split_out, same)
    back = jnp.repeat(back.reshape(2 * levels * fields, 2 * levels * fields), 2, axis=0)
    tall = jnp.concatenate([implicit, implicit])[:, None]
    turned = jnp.swapaxes(legendre, 1, 2)

    def exchange(blocks):
        if len(blocks) == 1:
            return [lax.all_to_all(blocks[0], AXES, split_axis=0, concat_axis=0, tiled=True)]
        return shift(blocks, groups, levels)

    def run(depths):
        depths = [tuple(depths[span]) for span in spans]
        sent = []
        for which, freq in enumerate(freqs):
            sent.append(dft(grid, order, freq, depths[which], owners, low, which > 0))
        received = []
        for blocks in sent:
            received.append(exchange(blocks))
        returned = []
        for which, blocks in enumerate(received):
            made = middle(
                blocks, metas[which], peers[which], turned, select, into, back, tall,
                levels, depths[which], count,
            )
            returned.append(exchange(made))
        result = None
        for which, blocks in enumerate(returned):
            final = which == len(returned) - 1
            result = place(
                blocks, peers[which], rank, targets[which], result, lon_count, fields, low,
                final, depths[which],
            )
        return result

    least = jnp.min(owner_trims[:, ::TILE], 0)
    needed = jnp.sum((slot_lats[:, None, :] >= LBLK * least[:, None]).astype(jnp.int32), 2)
    needed = jnp.max(needed, 0)
    choices = profiles(tiles, count)
    if PROFILE is not None:
        return run(choices[PROFILE])
    fits = jnp.all(needed <= low * jnp.array(choices[0], jnp.int32))
    return lax.cond(fits, lambda: run(choices[0]), lambda: run(choices[1]))


PROFILE = None


def solution(mesh):
    in_specs = (
        P(("member", "lev"), "wave", None, None),
        P(),
        P(),
        P(),
        P("wave", None, None),
        P(),
        P(),
        P(),
    )
    out_specs = P(("member", "lev"), "wave", None, None)
    return jax.shard_map(local, mesh=mesh, in_specs=in_specs, out_specs=out_specs, check_vma=False)
```

time: 437 us -> 399 us (0.913)
  waiting for transfers between devices: 142 us -> 123 us
  Pallas kernels: 148 us -> 134 us
  starting transfers between devices: 129 us -> 117 us
  local copies, waits for them, and re-layouts: 12.3 us -> 16.9 us
    ppermute x30, waiting for transfers between devices: 97.7 us -> 75.1 us  [shift(): moved.append(lax.ppermute(pieces[piece], AXES, pairs))]
    pallas_call x2, Pallas kernels: 36.4 us -> 22.9 us  [place(): pl.pallas_call(functools.partial(place_kernel, pieces=len(blocks), final=...]
    ppermute x30, starting transfers between devices: 108 us -> 96.1 us  [shift(): moved.append(lax.ppermute(pieces[piece], AXES, pairs))]
  transfers between devices with their start and end apart: 32 -> 32, of which waited for: 14 -> 16; matrix products, arithmetic and copies ran while one was open for 2% -> 2% of each run, Pallas kernels for 18% -> 19%
where the time goes in v3:
time: 399 us; the launch traced here: 398 us
  Pallas kernels  134 us (34%)
  waiting for transfers between devices  123 us (31%)
  starting transfers between devices  117 us (29%)
  local copies, waits for them, and re-layouts  16.9 us (4%)
  other arithmetic  5.56 us (1%)
    ppermute x30, starting transfers between devices, shift(): moved.append(lax.ppermute(pieces[piece], AXES, pairs))  96.1 us
    pallas_call x2, Pallas kernels, middle(): pl.pallas_call(functools.partial(middle_kernel, levels=levels, pieces=len...  77.2 us
    ppermute x30, waiting for transfers between devices, shift(): moved.append(lax.ppermute(pieces[piece], AXES, pairs))  75.1 us
    all_to_all x2, waiting for transfers between devices, exchange(): lax.all_to_all(blocks[0], AXES, split_axis=0, concat_axis=0, tiled=True)  48.4 us
    pallas_call x2, Pallas kernels, dft(): pl.pallas_call(functools.partial(dft_kernel, depths=depths, pairs=pairs,...  34.1 us
    pallas_call x2, Pallas kernels, place(): pl.pallas_call(functools.partial(place_kernel, pieces=len(blocks), final=...  22.9 us
    all_to_all x2, starting transfers between devices, exchange(): lax.all_to_all(blocks[0], AXES, split_axis=0, concat_axis=0, tiled=True)  20.7 us
  transfers between devices with their start and end apart: 32, of which 16 were waited for; matrix products, arithmetic and copies ran while one was open for 2% of the time, Pallas kernels for 19%

profile of v3, /device:TPU:0, one launch (start us, length us, event | category | flops | bytes accessed | tf_op | source)
XLA Modules:
  0.0 398.3 jit_solution(12680199385302842550)
XLA Ops:
  12.1 385.5 %conditional.1 = (bf16[32,40,2,1280]{3,2,1,0:T(2,128)(2,1)}) conditional(s32[]{:T(128)} %convert_element_type.55, (s32[8,40]{1,0:T(8,128)S(1)}, bf16[32,40,2,1280]{3,2,1,0:T(2,128)(2,1)}, f32[16,24]{1,0:T(8,128)S(1)}, s32[3,40]{1,0:T(4,128)S(1)}, s32[2,16]{1,0:T(2,128)S(1)}, /*index=5*/bf16[80,320,640]{2,1,0:T(8,128)(2,1)}, ...), branch_computations={%region_8.9_spmd, %region_9.10_spmd} | conditional | flops 2560 | bytes 69670280 | solution.py:474
  13.9 15.4 %dft.7 = bf16[16,80,8,128]{3,2,1,0:T(8,128)(2,1)} custom-call(s32[40]{0:T(128)} %fusion.3.lats_ref, bf16[32,40,2,1280]{3,2,1,0:T(2,128)(2,1)} %get-tuple-element.200.refs_0_.refs_1_.refs_2_.refs_3_, bf16[32,40,2,1280]{3,2,1,0:T(2,128)(2,1)} %get-tuple-element.200.refs_0_.refs_1_.refs_2_.refs_3_, ...), custom_call_target="tpu_custom_call" | custom-call | tf_op jit(solution)/shard_map/cond/branch_1_fun/dft/pallas_call | solution.py:94
  29.3 7.4 %all-to-all-start.2 = ((bf16[16,80,8,128]{3,2,1,0:T(8,128)(2,1)}), bf16[16,80,8,128]{3,2,1,0:T(8,128)(2,1)S(1)}, u32[]{:S(2)}, u32[]{:S(2)}) async-start(bf16[16,80,8,128]{3,2,1,0:T(8,128)(2,1)} %dft.7), calls=%async_computation.2 | async-start | bytes 5242880 | tf_op jit(solution)/shard_map/cond/branch_1_fun/all_to_all | solution.py:440
  38.4 48.4 %all-to-all-done.2.refs_0_ = bf16[16,80,8,128]{3,2,1,0:T(8,128)(2,1)S(1)} async-done(((bf16[16,80,8,128]{3,2,1,0:T(8,128)(2,1)}), bf16[16,80,8,128]{3,2,1,0:T(8,128)(2,1)S(1)}, u32[]{:S(2)}, u32[]{:S(2)}) %all-to-all-start.2) | async-done | bytes 2621472 | tf_op jit(solution)/shard_map/cond/branch_1_fun/all_to_all | solution.py:440
  88.4 30.8 %middle.7 = bf16[16,80,8,128]{3,2,1,0:T(8,128)(2,1)} custom-call(s32[3,16]{1,0:T(4,128)S(1)} %bitcast.114, s32[2,16]{1,0:T(2,128)S(1)} %get-tuple-element.164.peers, bf16[16,80,8,128]{3,2,1,0:T(8,128)(2,1)} %copy-done.3, bf16[80,320,640]{2,1,0:T(8,128)(2,1)} %get-tuple-element.142.refs_16_.refs_1_, ...), custom_call_target="tpu_custom_call" | custom-call | tf_op jit(solution)/shard_map/cond/branch_1_fun/middle/pallas_call | solution.py:200
  119.2 13.3 %all-to-all-start.3 = ((bf16[16,80,8,128]{3,2,1,0:T(8,128)(2,1)}), bf16[16,80,8,128]{3,2,1,0:T(8,128)(2,1)S(1)}, u32[]{:S(2)}, u32[]{:S(2)}) async-start(bf16[16,80,8,128]{3,2,1,0:T(8,128)(2,1)} %middle.7), calls=%async_computation.3 | async-start | bytes 5242880 | tf_op jit(solution)/shard_map/cond/branch_1_fun/all_to_all | solution.py:440
  133.6 18.7 %dft.6 = (bf16[1,94,8,128]{3,2,1,0:T(8,128)(2,1)}, bf16[1,94,8,128]{3,2,1,0:T(8,128)(2,1)}, bf16[1,94,8,128]{3,2,1,0:T(8,128)(2,1)}, bf16[1,94,8,128]{3,2,1,0:T(...) custom-call(s32[40]{0:T(128)} %fusion.3.lats_ref, ...), custom_call_target="tpu_custom_call" | custom-call | tf_op jit(solution)/shard_map/cond/branch_1_fun/dft/pallas_call | solution.py:94
  159.7 5.6 %collective-permute-done.31.refs_2_ = bf16[1,94,8,128]{3,2,1,0:T(8,128)(2,1)S(1)} collective-permute-done((bf16[1,94,8,128]{3,2,1,0:T(8,128)(2,1)}, bf16[1,94,8,128]{3,2,1,0:T(8,128)(2,1)S(1)}, u32[]{:S(2)}, u32[]{:S(2)}) %collective-permute-start.31) | collective-permute-done | bytes 192544 | tf_op jit(solution)/shard_map/cond/branch_1_fun/ppermute | solution.py:350
  165.4 6.8 %collective-permute-done.32.refs_3_ = bf16[1,94,8,128]{3,2,1,0:T(8,128)(2,1)} collective-permute-done((bf16[1,94,8,128]{3,2,1,0:T(8,128)(2,1)}, bf16[1,94,8,128]{3,2,1,0:T(8,128)(2,1)}, u32[]{:S(2)}, u32[]{:S(2)}) %collective-permute-start.32) | collective-permute-done | bytes 192544 | tf_op jit(solution)/shard_map/cond/branch_1_fun/ppermute | solution.py:350
  172.2 12.5 %collective-permute-done.33.refs_4_ = bf16[1,94,8,128]{3,2,1,0:T(8,128)(2,1)} collective-permute-done((bf16[1,94,8,128]{3,2,1,0:T(8,128)(2,1)}, bf16[1,94,8,128]{3,2,1,0:T(8,128)(2,1)}, u32[]{:S(2)}, u32[]{:S(2)}) %collective-permute-start.33) | collective-permute-done | bytes 192544 | tf_op jit(solution)/shard_map/cond/branch_1_fun/ppermute | solution.py:350
  184.6 16.3 %collective-permute-start.38 = (bf16[1,94,8,128]{3,2,1,0:T(8,128)(2,1)}, bf16[1,94,8,128]{3,2,1,0:T(8,128)(2,1)}, u32[]{:S(2)}, u32[]{:S(2)}) collective-permute-start(bf16[1,94,8,128]{3,2,1,0:T(8,128)(2,1)} %get-tuple-element.135), channel_id=1, source_target_pairs={{0,9},{1,8},{2,11},{3,10},{4,13},{5,12},{6,15},{7,14},{8,1},{9,0},... | collective-permute-start | bytes 577544 | tf_op jit(solution)/shard_map/cond/branch_1_fun/ppermute | solution.py:350
  200.9 5.2 %collective-permute-start.39 = (bf16[1,94,8,128]{3,2,1,0:T(8,128)(2,1)}, bf16[1,94,8,128]{3,2,1,0:T(8,128)(2,1)}, u32[]{:S(2)}, u32[]{:S(2)}) collective-permute-start(bf16[1,94,8,128]{3,2,1,0:T(8,128)(2,1)} %get-tuple-element.136), channel_id=1, source_target_pairs={{0,10},{1,11},{2,8},{3,9},{4,14},{5,15},{6,12},{7,13},{8,2},{9,3},... | collective-permute-start | bytes 577544 | tf_op jit(solution)/shard_map/cond/branch_1_fun/ppermute | solution.py:350
  206.8 9.5 %collective-permute-start.40 = (bf16[1,94,8,128]{3,2,1,0:T(8,128)(2,1)}, bf16[1,94,8,128]{3,2,1,0:T(8,128)(2,1)}, u32[]{:S(2)}, u32[]{:S(2)}) collective-permute-start(bf16[1,94,8,128]{3,2,1,0:T(8,128)(2,1)} %get-tuple-element.137), channel_id=1, source_target_pairs={{0,11},{1,10},{2,9},{3,8},{4,15},{5,14},{6,13},{7,12},{8,3},{9,2},... | collective-permute-start | bytes 577544 | tf_op jit(solution)/shard_map/cond/branch_1_fun/ppermute | solution.py:350
  218.7 12.0 %collective-permute-done.37.refs_8_ = bf16[1,94,8,128]{3,2,1,0:T(8,128)(2,1)} collective-permute-done((bf16[1,94,8,128]{3,2,1,0:T(8,128)(2,1)}, bf16[1,94,8,128]{3,2,1,0:T(8,128)(2,1)}, u32[]{:S(2)}, u32[]{:S(2)}) %collective-permute-start.37) | collective-permute-done | bytes 192544 | tf_op jit(solution)/shard_map/cond/branch_1_fun/ppermute | solution.py:350
  230.7 4.1 %collective-permute-start.42 = (bf16[1,94,8,128]{3,2,1,0:T(8,128)(2,1)}, bf16[1,94,8,128]{3,2,1,0:T(8,128)(2,1)}, u32[]{:S(2)}, u32[]{:S(2)}) collective-permute-start(bf16[1,94,8,128]{3,2,1,0:T(8,128)(2,1)} %get-tuple-element.139), channel_id=1, source_target_pairs={{0,13},{1,12},{2,15},{3,14},{4,1},{5,0},{6,3},{7,2},{8,5},{9,4},{1... | collective-permute-start | bytes 577544 | tf_op jit(solution)/shard_map/cond/branch_1_fun/ppermute | solution.py:350
  234.8 5.2 %collective-permute-start.43 = (bf16[1,94,8,128]{3,2,1,0:T(8,128)(2,1)}, bf16[1,94,8,128]{3,2,1,0:T(8,128)(2,1)}, u32[]{:S(2)}, u32[]{:S(2)}) collective-permute-start(bf16[1,94,8,128]{3,2,1,0:T(8,128)(2,1)} %get-tuple-element.140), channel_id=1, source_target_pairs={{0,14},{1,15},{2,12},{3,13},{4,2},{5,3},{6,0},{7,1},{8,6},{9,7},{1... | collective-permute-start | bytes 577544 | tf_op jit(solution)/shard_map/cond/branch_1_fun/ppermute | solution.py:350
  240.1 12.2 %collective-permute-start.44 = (bf16[1,94,8,128]{3,2,1,0:T(8,128)(2,1)}, bf16[1,94,8,128]{3,2,1,0:T(8,128)(2,1)}, u32[]{:S(2)}, u32[]{:S(2)}) collective-permute-start(bf16[1,94,8,128]{3,2,1,0:T(8,128)(2,1)} %get-tuple-element.141), channel_id=1, source_target_pairs={{0,15},{1,14},{2,13},{3,12},{4,3},{5,2},{6,1},{7,0},{8,7},{9,6},{1... | collective-permute-start | bytes 577544 | tf_op jit(solution)/shard_map/cond/branch_1_fun/ppermute | solution.py:350
  252.6 4.3 %collective-permute-done.44.refs_15_ = bf16[1,94,8,128]{3,2,1,0:T(8,128)(2,1)} collective-permute-done((bf16[1,94,8,128]{3,2,1,0:T(8,128)(2,1)}, bf16[1,94,8,128]{3,2,1,0:T(8,128)(2,1)}, u32[]{:S(2)}, u32[]{:S(2)}) %collective-permute-start.44) | collective-permute-done | bytes 192544 | tf_op jit(solution)/shard_map/cond/branch_1_fun/ppermute | solution.py:350
  256.9 46.3 %middle.6 = (bf16[1,94,8,128]{3,2,1,0:T(8,128)(2,1)}, bf16[1,94,8,128]{3,2,1,0:T(8,128)(2,1)}, bf16[1,94,8,128]{3,2,1,0:T(8,128)(2,1)}, bf16[1,94,8,128]{3,2,1,0...) custom-call(s32[3,24]{1,0:T(4,128)} %slice.29.meta, ...), custom_call_target="tpu_custom_call" | custom-call | tf_op jit(solution)/shard_map/cond/branch_1_fun/middle/pallas_call | solution.py:200
  321.5 4.7 %collective-permute-done.50.refs_6_ = bf16[1,94,8,128]{3,2,1,0:T(8,128)(2,1)} collective-permute-done((bf16[1,94,8,128]{3,2,1,0:T(8,128)(2,1)}, bf16[1,94,8,128]{3,2,1,0:T(8,128)(2,1)}, u32[]{:S(2)}, u32[]{:S(2)}) %collective-permute-start.50) | collective-permute-done | bytes 192544 | tf_op jit(solution)/shard_map/cond/branch_1_fun/ppermute | solution.py:350
  331.7 18.2 %collective-permute-done.52.refs_8_ = bf16[1,94,8,128]{3,2,1,0:T(8,128)(2,1)} collective-permute-done((bf16[1,94,8,128]{3,2,1,0:T(8,128)(2,1)}, bf16[1,94,8,128]{3,2,1,0:T(8,128)(2,1)}, u32[]{:S(2)}, u32[]{:S(2)}) %collective-permute-start.52) | collective-permute-done | bytes 192544 | tf_op jit(solution)/shard_map/cond/branch_1_fun/ppermute | solution.py:350
  358.6 12.2 %collective-permute-start.59 = (bf16[1,94,8,128]{3,2,1,0:T(8,128)(2,1)}, bf16[1,94,8,128]{3,2,1,0:T(8,128)(2,1)}, u32[]{:S(2)}, u32[]{:S(2)}) collective-permute-start(bf16[1,94,8,128]{3,2,1,0:T(8,128)(2,1)} %get-tuple-element.162), channel_id=1, source_target_pairs={{0,15},{1,14},{2,13},{3,12},{4,3},{5,2},{6,1},{7,0},{8,7},{9,6},{1... | collective-permute-start | bytes 577544 | tf_op jit(solution)/shard_map/cond/branch_1_fun/ppermute | solution.py:350
  374.7 9.5 %place.6.refs_17_ = bf16[2560,1280]{1,0:T(8,128)(2,1)} custom-call(s32[2,16]{1,0:T(2,128)S(1)} %get-tuple-element.164.peers, s32[40]{0:T(128)} %fusion.2.rank, bf16[16,80,8,128]{3,2,1,0:T(8,128)(2,1)} %copy-done.5, s32[512,1]{1,0:T(8,128)} %add.384.refs_1_), custom_call_target="tpu_custom_call" | custom-call | tf_op jit(solution)/shard_map/cond/branch_1_fun/place/pallas_call | solution.py:301
  384.2 13.4 %place.7 = bf16[32,40,2,1280]{3,2,1,0:T(2,128)(2,1)} custom-call(s32[2,16]{1,0:T(2,128)S(1)} %get-tuple-element.120.peers, s32[40]{0:T(128)} %fusion.2.rank, bf16[1,94,8,128]{3,2,1,0:T(8,128)(2,1)} %get-tuple-element.147.refs_0_, bf16[1,94,8,128]{3,2,1,0:T(8,128)(2,1)} %copy-done.11, bf16[1,94,8,128]{3,2,1,0:T(8,128)(2,1)} %copy-done.12, ...), custom_call_target="tpu_custom_call" | custom-call | tf_op jit(solution)/shard_map/cond/branch_1_fun/place/pallas_call | solution.py:301
  (156 shorter events, 64.9 us)
Async XLA Ops:
  29.3 57.5 %all-to-all-start.2 = ((bf16[16,80,8,128]{3,2,1,0:T(8,128)(2,1)}), bf16[16,80,8,128]{3,2,1,0:T(8,128)(2,1)S(1)}, u32[]{:S(2)}, u32[]{:S(2)}) async-start(bf16[16,80,8,128]{3,2,1,0:T(8,128)(2,1)} %dft.7), calls=%async_computation.2 | async-start | bytes 5242880 | tf_op jit(solution)/shard_map/cond/branch_1_fun/all_to_all | solution.py:440
  119.2 254.0 %all-to-all-start.3 = ((bf16[16,80,8,128]{3,2,1,0:T(8,128)(2,1)}), bf16[16,80,8,128]{3,2,1,0:T(8,128)(2,1)S(1)}, u32[]{:S(2)}, u32[]{:S(2)}) async-start(bf16[16,80,8,128]{3,2,1,0:T(8,128)(2,1)} %middle.7), calls=%async_computation.3 | async-start | bytes 5242880 | tf_op jit(solution)/shard_map/cond/branch_1_fun/all_to_all | solution.py:440
  154.5 17.7 %collective-permute-start.32 = (bf16[1,94,8,128]{3,2,1,0:T(8,128)(2,1)}, bf16[1,94,8,128]{3,2,1,0:T(8,128)(2,1)}, u32[]{:S(2)}, u32[]{:S(2)}) collective-permute-start(bf16[1,94,8,128]{3,2,1,0:T(8,128)(2,1)} %get-tuple-element.129), channel_id=1, source_target_pairs={{0,3},{1,2},{2,1},{3,0},{4,7},{5,6},{6,5},{7,4},{8,11},{9,10},{10,... | collective-permute-start | bytes 577544 | tf_op jit(solution)/shard_map/cond/branch_1_fun/ppermute | solution.py:350
  154.5 30.2 %collective-permute-start.33 = (bf16[1,94,8,128]{3,2,1,0:T(8,128)(2,1)}, bf16[1,94,8,128]{3,2,1,0:T(8,128)(2,1)}, u32[]{:S(2)}, u32[]{:S(2)}) collective-permute-start(bf16[1,94,8,128]{3,2,1,0:T(8,128)(2,1)} %get-tuple-element.130), channel_id=1, source_target_pairs={{0,4},{1,5},{2,6},{3,7},{4,8},{5,9},{6,10},{7,11},{8,12},{9,13},{1... | collective-permute-start | bytes 577544 | tf_op jit(solution)/shard_map/cond/branch_1_fun/ppermute | solution.py:350
  156.2 44.7 %collective-permute-start.34 = (bf16[1,94,8,128]{3,2,1,0:T(8,128)(2,1)}, bf16[1,94,8,128]{3,2,1,0:T(8,128)(2,1)}, u32[]{:S(2)}, u32[]{:S(2)}) collective-permute-start(bf16[1,94,8,128]{3,2,1,0:T(8,128)(2,1)} %get-tuple-element.131), channel_id=1, source_target_pairs={{0,5},{1,4},{2,7},{3,6},{4,9},{5,8},{6,11},{7,10},{8,13},{9,12},{1... | collective-permute-start | bytes 577544 | tf_op jit(solution)/shard_map/cond/branch_1_fun/ppermute | solution.py:350
  157.4 49.4 %collective-permute-start.35 = (bf16[1,94,8,128]{3,2,1,0:T(8,128)(2,1)}, bf16[1,94,8,128]{3,2,1,0:T(8,128)(2,1)}, u32[]{:S(2)}, u32[]{:S(2)}) collective-permute-start(bf16[1,94,8,128]{3,2,1,0:T(8,128)(2,1)} %get-tuple-element.132), channel_id=1, source_target_pairs={{0,6},{1,7},{2,4},{3,5},{4,10},{5,11},{6,8},{7,9},{8,14},{9,15},{1... | collective-permute-start | bytes 577544 | tf_op jit(solution)/shard_map/cond/branch_1_fun/ppermute | solution.py:350
  165.4 50.9 %collective-permute-start.36 = (bf16[1,94,8,128]{3,2,1,0:T(8,128)(2,1)}, bf16[1,94,8,128]{3,2,1,0:T(8,128)(2,1)}, u32[]{:S(2)}, u32[]{:S(2)}) collective-permute-start(bf16[1,94,8,128]{3,2,1,0:T(8,128)(2,1)} %get-tuple-element.133), channel_id=1, source_target_pairs={{0,7},{1,6},{2,5},{3,4},{4,11},{5,10},{6,9},{7,8},{8,15},{9,14},{1... | collective-permute-start | bytes 577544 | tf_op jit(solution)/shard_map/cond/branch_1_fun/ppermute | solution.py:350
  172.1 58.6 %collective-permute-start.37 = (bf16[1,94,8,128]{3,2,1,0:T(8,128)(2,1)}, bf16[1,94,8,128]{3,2,1,0:T(8,128)(2,1)}, u32[]{:S(2)}, u32[]{:S(2)}) collective-permute-start(bf16[1,94,8,128]{3,2,1,0:T(8,128)(2,1)} %get-tuple-element.134), channel_id=1, source_target_pairs={{0,8},{1,9},{2,10},{3,11},{4,12},{5,13},{6,14},{7,15},{8,0},{9,1},... | collective-permute-start | bytes 577544 | tf_op jit(solution)/shard_map/cond/branch_1_fun/ppermute | solution.py:350
  184.6 50.2 %collective-permute-start.38 = (bf16[1,94,8,128]{3,2,1,0:T(8,128)(2,1)}, bf16[1,94,8,128]{3,2,1,0:T(8,128)(2,1)}, u32[]{:S(2)}, u32[]{:S(2)}) collective-permute-start(bf16[1,94,8,128]{3,2,1,0:T(8,128)(2,1)} %get-tuple-element.135), channel_id=1, source_target_pairs={{0,9},{1,8},{2,11},{3,10},{4,13},{5,12},{6,15},{7,14},{8,1},{9,0},... | collective-permute-start | bytes 577544 | tf_op jit(solution)/shard_map/cond/branch_1_fun/ppermute | solution.py:350
  200.9 39.1 %collective-permute-start.39 = (bf16[1,94,8,128]{3,2,1,0:T(8,128)(2,1)}, bf16[1,94,8,128]{3,2,1,0:T(8,128)(2,1)}, u32[]{:S(2)}, u32[]{:S(2)}) collective-permute-start(bf16[1,94,8,128]{3,2,1,0:T(8,128)(2,1)} %get-tuple-element.136), channel_id=1, source_target_pairs={{0,10},{1,11},{2,8},{3,9},{4,14},{5,15},{6,12},{7,13},{8,2},{9,3},... | collective-permute-start | bytes 577544 | tf_op jit(solution)/shard_map/cond/branch_1_fun/ppermute | solution.py:350
  206.8 45.5 %collective-permute-start.40 = (bf16[1,94,8,128]{3,2,1,0:T(8,128)(2,1)}, bf16[1,94,8,128]{3,2,1,0:T(8,128)(2,1)}, u32[]{:S(2)}, u32[]{:S(2)}) collective-permute-start(bf16[1,94,8,128]{3,2,1,0:T(8,128)(2,1)} %get-tuple-element.137), channel_id=1, source_target_pairs={{0,11},{1,10},{2,9},{3,8},{4,15},{5,14},{6,13},{7,12},{8,3},{9,2},... | collective-permute-start | bytes 577544 | tf_op jit(solution)/shard_map/cond/branch_1_fun/ppermute | solution.py:350
  216.3 36.1 %collective-permute-start.41 = (bf16[1,94,8,128]{3,2,1,0:T(8,128)(2,1)}, bf16[1,94,8,128]{3,2,1,0:T(8,128)(2,1)}, u32[]{:S(2)}, u32[]{:S(2)}) collective-permute-start(bf16[1,94,8,128]{3,2,1,0:T(8,128)(2,1)} %get-tuple-element.138), channel_id=1, source_target_pairs={{0,12},{1,13},{2,14},{3,15},{4,0},{5,1},{6,2},{7,3},{8,4},{9,5},{1... | collective-permute-start | bytes 577544 | tf_op jit(solution)/shard_map/cond/branch_1_fun/ppermute | solution.py:350
  230.7 21.6 %collective-permute-start.42 = (bf16[1,94,8,128]{3,2,1,0:T(8,128)(2,1)}, bf16[1,94,8,128]{3,2,1,0:T(8,128)(2,1)}, u32[]{:S(2)}, u32[]{:S(2)}) collective-permute-start(bf16[1,94,8,128]{3,2,1,0:T(8,128)(2,1)} %get-tuple-element.139), channel_id=1, source_target_pairs={{0,13},{1,12},{2,15},{3,14},{4,1},{5,0},{6,3},{7,2},{8,5},{9,4},{1... | collective-permute-start | bytes 577544 | tf_op jit(solution)/shard_map/cond/branch_1_fun/ppermute | solution.py:350
  234.8 17.8 %collective-permute-start.43 = (bf16[1,94,8,128]{3,2,1,0:T(8,128)(2,1)}, bf16[1,94,8,128]{3,2,1,0:T(8,128)(2,1)}, u32[]{:S(2)}, u32[]{:S(2)}) collective-permute-start(bf16[1,94,8,128]{3,2,1,0:T(8,128)(2,1)} %get-tuple-element.140), channel_id=1, source_target_pairs={{0,14},{1,15},{2,12},{3,13},{4,2},{5,3},{6,0},{7,1},{8,6},{9,7},{1... | collective-permute-start | bytes 577544 | tf_op jit(solution)/shard_map/cond/branch_1_fun/ppermute | solution.py:350
  240.1 16.8 %collective-permute-start.44 = (bf16[1,94,8,128]{3,2,1,0:T(8,128)(2,1)}, bf16[1,94,8,128]{3,2,1,0:T(8,128)(2,1)}, u32[]{:S(2)}, u32[]{:S(2)}) collective-permute-start(bf16[1,94,8,128]{3,2,1,0:T(8,128)(2,1)} %get-tuple-element.141), channel_id=1, source_target_pairs={{0,15},{1,14},{2,13},{3,12},{4,3},{5,2},{6,1},{7,0},{8,7},{9,6},{1... | collective-permute-start | bytes 577544 | tf_op jit(solution)/shard_map/cond/branch_1_fun/ppermute | solution.py:350
  308.6 17.6 %collective-permute-start.50 = (bf16[1,94,8,128]{3,2,1,0:T(8,128)(2,1)}, bf16[1,94,8,128]{3,2,1,0:T(8,128)(2,1)}, u32[]{:S(2)}, u32[]{:S(2)}) collective-permute-start(bf16[1,94,8,128]{3,2,1,0:T(8,128)(2,1)} %get-tuple-element.153), channel_id=1, source_target_pairs={{0,6},{1,7},{2,4},{3,5},{4,10},{5,11},{6,8},{7,9},{8,14},{9,15},{1... | collective-permute-start | bytes 577544 | tf_op jit(solution)/shard_map/cond/branch_1_fun/ppermute | solution.py:350
  316.3 33.6 %collective-permute-start.52 = (bf16[1,94,8,128]{3,2,1,0:T(8,128)(2,1)}, bf16[1,94,8,128]{3,2,1,0:T(8,128)(2,1)}, u32[]{:S(2)}, u32[]{:S(2)}) collective-permute-start(bf16[1,94,8,128]{3,2,1,0:T(8,128)(2,1)} %get-tuple-element.155), channel_id=1, source_target_pairs={{0,8},{1,9},{2,10},{3,11},{4,12},{5,13},{6,14},{7,15},{8,0},{9,1},... | collective-permute-start | bytes 577544 | tf_op jit(solution)/shard_map/cond/branch_1_fun/ppermute | solution.py:350
  317.1 36.8 %collective-permute-start.53 = (bf16[1,94,8,128]{3,2,1,0:T(8,128)(2,1)}, bf16[1,94,8,128]{3,2,1,0:T(8,128)(2,1)}, u32[]{:S(2)}, u32[]{:S(2)}) collective-permute-start(bf16[1,94,8,128]{3,2,1,0:T(8,128)(2,1)} %get-tuple-element.156), channel_id=1, source_target_pairs={{0,9},{1,8},{2,11},{3,10},{4,13},{5,12},{6,15},{7,14},{8,1},{9,0},... | collective-permute-start | bytes 577544 | tf_op jit(solution)/shard_map/cond/branch_1_fun/ppermute | solution.py:350
  320.6 38.0 %collective-permute-start.54 = (bf16[1,94,8,128]{3,2,1,0:T(8,128)(2,1)}, bf16[1,94,8,128]{3,2,1,0:T(8,128)(2,1)}, u32[]{:S(2)}, u32[]{:S(2)}) collective-permute-start(bf16[1,94,8,128]{3,2,1,0:T(8,128)(2,1)} %get-tuple-element.157), channel_id=1, source_target_pairs={{0,10},{1,11},{2,8},{3,9},{4,14},{5,15},{6,12},{7,13},{8,2},{9,3},... | collective-permute-start | bytes 577544 | tf_op jit(solution)/shard_map/cond/branch_1_fun/ppermute | solution.py:350
  326.2 58.0 %collective-permute-start.55 = (bf16[1,94,8,128]{3,2,1,0:T(8,128)(2,1)}, bf16[1,94,8,128]{3,2,1,0:T(8,128)(2,1)}, u32[]{:S(2)}, u32[]{:S(2)}) collective-permute-start(bf16[1,94,8,128]{3,2,1,0:T(8,128)(2,1)} %get-tuple-element.158), channel_id=1, source_target_pairs={{0,11},{1,10},{2,9},{3,8},{4,15},{5,14},{6,13},{7,12},{8,3},{9,2},... | collective-permute-start | bytes 577544 | tf_op jit(solution)/shard_map/cond/branch_1_fun/ppermute | solution.py:350
  329.2 55.0 %collective-permute-start.56 = (bf16[1,94,8,128]{3,2,1,0:T(8,128)(2,1)}, bf16[1,94,8,128]{3,2,1,0:T(8,128)(2,1)}, u32[]{:S(2)}, u32[]{:S(2)}) collective-permute-start(bf16[1,94,8,128]{3,2,1,0:T(8,128)(2,1)} %get-tuple-element.159), channel_id=1, source_target_pairs={{0,12},{1,13},{2,14},{3,15},{4,0},{5,1},{6,2},{7,3},{8,4},{9,5},{1... | collective-permute-start | bytes 577544 | tf_op jit(solution)/shard_map/cond/branch_1_fun/ppermute | solution.py:350
  349.8 34.4 %collective-permute-start.57 = (bf16[1,94,8,128]{3,2,1,0:T(8,128)(2,1)}, bf16[1,94,8,128]{3,2,1,0:T(8,128)(2,1)}, u32[]{:S(2)}, u32[]{:S(2)}) collective-permute-start(bf16[1,94,8,128]{3,2,1,0:T(8,128)(2,1)} %get-tuple-element.160), channel_id=1, source_target_pairs={{0,13},{1,12},{2,15},{3,14},{4,1},{5,0},{6,3},{7,2},{8,5},{9,4},{1... | collective-permute-start | bytes 577544 | tf_op jit(solution)/shard_map/cond/branch_1_fun/ppermute | solution.py:350
  354.0 30.3 %collective-permute-start.58 = (bf16[1,94,8,128]{3,2,1,0:T(8,128)(2,1)}, bf16[1,94,8,128]{3,2,1,0:T(8,128)(2,1)}, u32[]{:S(2)}, u32[]{:S(2)}) collective-permute-start(bf16[1,94,8,128]{3,2,1,0:T(8,128)(2,1)} %get-tuple-element.161), channel_id=1, source_target_pairs={{0,14},{1,15},{2,12},{3,13},{4,2},{5,3},{6,0},{7,1},{8,6},{9,7},{1... | collective-permute-start | bytes 577544 | tf_op jit(solution)/shard_map/cond/branch_1_fun/ppermute | solution.py:350
  358.6 25.6 %collective-permute-start.59 = (bf16[1,94,8,128]{3,2,1,0:T(8,128)(2,1)}, bf16[1,94,8,128]{3,2,1,0:T(8,128)(2,1)}, u32[]{:S(2)}, u32[]{:S(2)}) collective-permute-start(bf16[1,94,8,128]{3,2,1,0:T(8,128)(2,1)} %get-tuple-element.162), channel_id=1, source_target_pairs={{0,15},{1,14},{2,13},{3,12},{4,3},{5,2},{6,1},{7,0},{8,7},{9,6},{1... | collective-permute-start | bytes 577544 | tf_op jit(solution)/shard_map/cond/branch_1_fun/ppermute | solution.py:350
  (20 other events, 521.8 us)

commit v4 on v3

--- a/solution.py
+++ b/solution.py
@@ -78,8 +78,8 @@
             pl.when(where < depth)(functools.partial(store, tile, pair, where))
 
 
-def dft(grid, order, freq, depths, owners, low, separate):
-    fields, lats, _, lon_count = grid.shape
+def dft(grid, order, freq, depths, owners, lats, low, separate):
+    fields, _, _, lon_count = grid.shape
     count = lats // low
     pairs = 2 if count % 2 == 0 else 1
     slots = pairs * low
@@ -88,7 +88,7 @@
 
     def view(slot):
         return pl.BlockSpec(
-            (fields, 1, 2, lon_count), lambda i, order: (0, order[i * slots + slot], 0, 0)
+            (fields, 1, 2, lon_count), lambda i, order: (0, order[0, i * slots + slot], 0, 0)
         )
 
     return pl.pallas_call(
@@ -104,6 +104,80 @@
         out_shape=[jax.ShapeDtypeStruct(shape, jnp.bfloat16)] * pieces,
         name="dft",
     )(order, *([grid] * slots), freq)
+
+
+def as_column(row):
+    return jnp.broadcast_to(row, (LANES, row.shape[1])).T[:, :1]
+
+
+def plan_kernel(
+    waves_ref, trim_ref, lats_ref, *outs, groups, levels, share, low, small, sizes, axes
+):
+    freqs, notes = outs[:-1], outs[-1]
+    total = waves_ref.shape[1]
+    near_count = total // groups
+    waves = waves_ref[...].astype(jnp.float32)
+    lane = lax.broadcasted_iota(jnp.int32, (1, total), 1).astype(jnp.float32)
+    number = lax.broadcasted_iota(jnp.int32, (total, 1), 0).astype(jnp.float32)
+    trim_column = as_column(trim_ref[...].astype(jnp.float32))
+    trims = jnp.sum(jnp.where(number == waves, trim_column, 0.0), 0, keepdims=True)
+    base = jnp.floor((lane + 0.5) * (1.0 / near_count)) * near_count
+    keys = (base * 8.0 + trims * near_count) + (lane - base)
+    rank = jnp.sum(jnp.where(as_column(keys) < keys, 1.0, 0.0), 0, keepdims=True)
+
+    group = lax.axis_index(axes[0])
+    me = group * levels + lax.axis_index(axes[1])
+    first = 0
+    for which, (freq, size) in enumerate(zip(freqs, sizes)):
+        rows = size * 2 * TILE
+        row = lax.broadcasted_iota(jnp.int32, (rows, 1), 0)
+        tile, wave = row // (2 * TILE), row % TILE
+        slot = jnp.minimum((first + tile) * TILE + wave, share - 1) * levels
+        slot = slot.astype(jnp.float32)
+        for piece in range(groups * levels):
+            owner = jnp.int32(piece)
+            if which > 0:
+                owner = partner(me, jnp.int32(piece), groups, levels, False)
+            start = ((owner // levels) * near_count + owner % levels).astype(jnp.float32)
+            chosen = jnp.where(rank == slot + start, waves, 0.0)
+            freq[piece * rows : (piece + 1) * rows, :] = jnp.sum(chosen, 1, keepdims=True)
+        first += size
+
+    lats = lats_ref[...]
+    fits = jnp.full((1, 1), 1, jnp.int32)
+    for tile, depth in enumerate(small):
+        spot = (rank - base) == float(min(tile * TILE, share - 1) * levels)
+        least = jnp.min(jnp.where(spot, trims, 8.0), 1, keepdims=True).astype(jnp.int32)
+        needed = jnp.where(lats >= LBLK * least, 1.0, 0.0)
+        needed = jnp.max(jnp.sum(needed, 1, keepdims=True), 0, keepdims=True)
+        fits = fits * jnp.where(needed <= float(low * depth), 1, 0)
+
+    count = lats.shape[1]
+    mine = lats_ref[pl.ds(group, 1), :].astype(jnp.float32)
+    mine = jnp.concatenate([mine, jnp.full((1, LANES - count), -1.0, jnp.float32)], 1)
+    spot = lax.broadcasted_iota(jnp.int32, (1, LANES), 1).astype(jnp.float32)
+    mine = mine * LANES - spot
+    place_of = jnp.sum(jnp.where(as_column(mine) > mine, 1.0, 0.0), 0, keepdims=True)
+    index = lax.broadcasted_iota(jnp.int32, (LANES, 1), 0).astype(jnp.float32)
+    order = jnp.sum(jnp.where(as_column(place_of) == spot, index, 0.0), 0, keepdims=True)
+    notes[0:1, :] = order.astype(jnp.int32)
+    notes[1:2, :] = jnp.broadcast_to(fits, (1, LANES))
+
+
+def plan(wave_order, trim, lat_order, groups, levels, share, low, small, sizes):
+    total = wave_order.shape[0]
+    owners = groups * levels
+    return pl.pallas_call(
+        functools.partial(
+            plan_kernel, groups=groups, levels=levels, share=share, low=low, small=small,
+            sizes=sizes, axes=AXES,
+        ),
+        out_shape=[
+            jax.ShapeDtypeStruct((owners * size * 2 * TILE, 1), jnp.float32) for size in sizes
+        ]
+        + [jax.ShapeDtypeStruct((TILE, LANES), jnp.int32)],
+        name="plan",
+    )(wave_order.reshape(1, total), trim.reshape(1, total), lat_order.reshape(groups, -1))
 
 
 def middle_kernel(meta, peers, *refs, levels, pieces, depths, count):
@@ -215,7 +289,7 @@
     )(meta, peers, *data, legendre, select, into, back, implicit)
 
 
-def place_kernel(peers, rank, *refs, pieces, final, with_start, split, depths, low, batch):
+def place_kernel(rank, *refs, pieces, final, with_start, split, depths, low, batch):
     blocks, refs = refs[:pieces], refs[pieces:]
     target, refs = refs[0], refs[1:]
     start = refs[0] if with_start else None
@@ -244,16 +318,15 @@
             index = rank[(step * batch + item) * low + slot]
             where, side = index // low, index % low
             for piece in range(each * pieces):
-                base = peers[0, piece] * span_rows
                 for tile, depth in enumerate(depths):
                     near = jnp.minimum(where, depth - 1)
                     for part in range(2):
                         unit = starts[tile][part] + near
                         block = blocks[piece // each][piece % each, unit].astype(jnp.float32)
-                        if depth < max_depth(rank, low):
+                        if depth < rank.shape[0] // low:
                             block = jnp.where(where < depth, block, 0.0)
-                        first = base + (2 * tile + part) * TILE
-                        gathered[slot, pl.ds(pl.multiple_of(first, TILE), TILE), :] = block
+                        first = piece * span_rows + (2 * tile + part) * TILE
+                        gathered[slot, first : first + TILE, :] = block
             values = pltpu.roll(gathered[slot], ((slot - side) % low) * span, 1)
             merged = values if merged is None else jnp.where(lane == slot, values, merged)
         turned.append(merged.T.astype(jnp.bfloat16))
@@ -275,16 +348,12 @@
         out[:, slot] = block.reshape(fields, 2, block.shape[1])
 
 
-def max_depth(rank, low):
-    return rank.shape[0] // low
-
-
-def place(blocks, peers, rank, target, start, columns, fields, low, final, depths):
+def place(blocks, rank, target, start, columns, fields, low, final, depths):
     each = blocks[0].shape[0]
     owners = each * len(blocks)
     count = rank.shape[0] // low
     batch = max(b for b in (1, 2, 4) if count % b == 0)
-    split = 2 if owners % 2 == 0 and (columns // 2) % LANES == 0 else 1
+    split = 2 if len(blocks) == 1 and owners % 2 == 0 and (columns // 2) % LANES == 0 else 1
     specs = [pl.BlockSpec(b.shape, lambda i, *_: (0, 0, 0, 0)) for b in blocks]
     specs.append(pl.BlockSpec(target.shape, lambda i, *_: (0, 0)))
     args = list(blocks) + [target]
@@ -310,7 +379,7 @@
             batch=batch,
         ),
         grid_spec=pltpu.PrefetchScalarGridSpec(
-            num_scalar_prefetch=2,
+            num_scalar_prefetch=1,
             grid=(count // batch,),
             in_specs=specs,
             out_specs=out_spec,
@@ -321,7 +390,7 @@
         ),
         out_shape=out_shape,
         name="place",
-    )(peers, rank, *args)
+    )(rank, *args)
 
 
 def chunk_tiles(tiles):
@@ -380,60 +449,57 @@
     group = lax.axis_index("wave")
     me = group * levels + lax.axis_index("lev")
 
-    trims = trim[wave_order].reshape(groups, per_device)
-    near = jnp.arange(per_device, dtype=jnp.int32)
-    keys = (trims * per_device + near) * row_count + wave_order.reshape(groups, per_device)
-    keys, _ = ordered(keys)
-    keys = keys.reshape(groups, share, levels).transpose(0, 2, 1).reshape(owners, share)
-    slot = jnp.arange(tiles * TILE, dtype=jnp.int32)
-    keys = keys[:, jnp.minimum(slot, share - 1)]
-    owner_waves, owner_near = keys % row_count, keys // row_count % per_device
-    owner_trims = keys // (row_count * per_device)
-    table = (lat_count - 1 - lat_order).reshape(groups, lats)
-    table, rank = ordered(table * lats + jnp.arange(lats, dtype=jnp.int32))
-    slot_lats, slot_order = lat_count - 1 - table // lats, table % lats
-    order = lax.dynamic_slice_in_dim(slot_order, group, 1)[0]
-    rank = lax.dynamic_slice_in_dim(rank, group, 1)[0]
-
-    mine = lax.dynamic_slice_in_dim(keys, me, 1)[0]
-    meta = jnp.stack(
-        [mine % row_count, mine // (row_count * per_device), mine // row_count % per_device]
-    )
-    first_column = (jnp.arange(owners, dtype=jnp.int32) // levels * (2 * per_device))[:, None]
-    columns = jnp.where(slot < share, first_column + 2 * owner_near, -4 * per_device * owners)
-
-    piece = jnp.arange(owners, dtype=jnp.int32)
-    natural = jnp.stack([piece, piece])
-    paired = jnp.stack(
-        [partner(me, piece, groups, levels, back) for back in (True, False)]
-    )
-    peers = [natural, paired]
-
-    freqs, metas, targets, spans, first = [], [], [], [], 0
-    for which, size in enumerate(chunk_tiles(tiles)):
-        spans.append(slice(first, first + size))
-        span = slice(first * TILE, (first + size) * TILE)
-        shape = (owners, size, 2, TILE)
-        waves = owner_waves if which == 0 else owner_waves[paired[1]]
-        waves = jnp.broadcast_to(waves[:, span].reshape(owners, size, 1, TILE), shape)
-        freqs.append(waves.reshape(-1, 1).astype(jnp.float32))
-        goal = columns[:, span].reshape(owners, size, 1, TILE)
-        goal = goal + jnp.arange(2, dtype=jnp.int32)[:, None]
-        targets.append(jnp.broadcast_to(goal, shape).reshape(-1, 1))
-        metas.append(meta[:, span])
-        first += size
-
-    slots = slot_lats.reshape(groups * count, low).T
-    select = (slots[:, :, None] == jnp.arange(lat_count, dtype=jnp.int32)).astype(jnp.bfloat16)
-    same = jnp.eye(2, dtype=jnp.bfloat16)
-    split_in = modes_in.reshape(-1, levels, fields)
-    into = jnp.einsum("klf,cd->ckldf", split_in, same)
-    into = jnp.repeat(into.reshape(2 * levels * fields, 2 * levels * fields), 2, axis=1)
-    split_out = modes_out.reshape(levels, fields, -1)
-    back = jnp.einsum("lfk,cd->lcfdk", split_out, same)
-    back = jnp.repeat(back.reshape(2 * levels * fields, 2 * levels * fields), 2, axis=0)
-    tall = jnp.concatenate([implicit, implicit])[:, None]
-    turned = jnp.swapaxes(legendre, 1, 2)
+    def tables():
+        trims = trim[wave_order].reshape(groups, per_device)
+        near = jnp.arange(per_device, dtype=jnp.int32)
+        keys = (trims * per_device + near) * row_count + wave_order.reshape(groups, per_device)
+        keys, _ = ordered(keys)
+        keys = keys.reshape(groups, share, levels).transpose(0, 2, 1).reshape(owners, share)
+        slot = jnp.arange(tiles * TILE, dtype=jnp.int32)
+        keys = keys[:, jnp.minimum(slot, share - 1)]
+        owner_near = keys // row_count % per_device
+        table = (lat_count - 1 - lat_order).reshape(groups, lats)
+        table, rank = ordered(table * lats + jnp.arange(lats, dtype=jnp.int32))
+        slot_lats = lat_count - 1 - table // lats
+        rank = lax.dynamic_slice_in_dim(rank, group, 1)[0]
+
+        mine = lax.dynamic_slice_in_dim(keys, me, 1)[0]
+        meta = jnp.stack(
+            [mine % row_count, mine // (row_count * per_device), mine // row_count % per_device]
+        )
+        first_column = (jnp.arange(owners, dtype=jnp.int32) // levels * (2 * per_device))[:, None]
+        columns = jnp.where(slot < share, first_column + 2 * owner_near, -4 * per_device * owners)
+
+        piece = jnp.arange(owners, dtype=jnp.int32)
+        natural = jnp.stack([piece, piece])
+        paired = jnp.stack(
+            [partner(me, piece, groups, levels, back) for back in (True, False)]
+        )
+        peers = [natural, paired]
+
+        metas, targets, first = [], [], 0
+        for which, size in enumerate(sizes):
+            span = slice(first * TILE, (first + size) * TILE)
+            shape = (owners, size, 2, TILE)
+            goal = columns if which == 0 else columns[paired[0]]
+            goal = goal[:, span].reshape(owners, size, 1, TILE)
+            goal = goal + jnp.arange(2, dtype=jnp.int32)[:, None]
+            targets.append(jnp.broadcast_to(goal, shape).reshape(-1, 1))
+            metas.append(meta[:, span])
+            first += size
+
+        slots = slot_lats.reshape(groups * count, low).T
+        select = (slots[:, :, None] == jnp.arange(lat_count, dtype=jnp.int32)).astype(jnp.bfloat16)
+        same = jnp.eye(2, dtype=jnp.bfloat16)
+        split_in = modes_in.reshape(-1, levels, fields)
+        into = jnp.einsum("klf,cd->ckldf", split_in, same)
+        into = jnp.repeat(into.reshape(2 * levels * fields, 2 * levels * fields), 2, axis=1)
+        split_out = modes_out.reshape(levels, fields, -1)
+        back = jnp.einsum("lfk,cd->lcfdk", split_out, same)
+        back = jnp.repeat(back.reshape(2 * levels * fields, 2 * levels * fields), 2, axis=0)
+        tall = jnp.concatenate([implicit, implicit])[:, None]
+        turned = jnp.swapaxes(legendre, 1, 2)
+        return metas, peers, rank, targets, (turned, select, into, back, tall)
 
     def exchange(blocks):
         if len(blocks) == 1:
@@ -444,34 +510,42 @@
         depths = [tuple(depths[span]) for span in spans]
         sent = []
         for which, freq in enumerate(freqs):
-            sent.append(dft(grid, order, freq, depths[which], owners, low, which > 0))
+            sent.append(dft(grid, notes, freq, depths[which], owners, lats, low, which > 0))
+        metas, peers, rank, targets, weights = tables()
         received = []
         for blocks in sent:
             received.append(exchange(blocks))
         returned = []
         for which, blocks in enumerate(received):
             made = middle(
-                blocks, metas[which], peers[which], turned, select, into, back, tall,
-                levels, depths[which], count,
+                blocks, metas[which], peers[which], *weights, levels, depths[which], count
             )
             returned.append(exchange(made))
         result = None
         for which, blocks in enumerate(returned):
-            final = which == len(returned) - 1
-            result = place(
-                blocks, peers[which], rank, targets[which], result, lon_count, fields, low,
-                final, depths[which],
-            )
+            last = which == len(returned) - 1
+            kept = len(blocks) * 3 // 4
+            parts = [slice(0, kept), slice(kept, None)] if kept else [slice(0, None)]
+            for part in parts:
+                target = targets[which].reshape(len(blocks), -1)[part].reshape(-1, 1)
+                result = place(
+                    blocks[part], rank, target, result, lon_count, fields, low,
+                    last and part is parts[-1], depths[which],
+                )
         return result
 
-    least = jnp.min(owner_trims[:, ::TILE], 0)
-    needed = jnp.sum((slot_lats[:, None, :] >= LBLK * least[:, None]).astype(jnp.int32), 2)
-    needed = jnp.max(needed, 0)
-    choices = profiles(tiles, count)
+    sizes = chunk_tiles(tiles)
+    spans, first = [], 0
+    for size in sizes:
+        spans.append(slice(first, first + size))
+        first += size
+    small, full = profiles(tiles, count)
+    *freqs, notes = plan(
+        wave_order, trim, lat_order, groups, levels, share, low, small, sizes
+    )
     if PROFILE is not None:
-        return run(choices[PROFILE])
-    fits = jnp.all(needed <= low * jnp.array(choices[0], jnp.int32))
-    return lax.cond(fits, lambda: run(choices[0]), lambda: run(choices[1]))
+        return run((small, full)[PROFILE])
+    return lax.cond(notes[1, 0] > 0, lambda: run(small), lambda: run(full))
 
 
 PROFILE = None

time: 399 us -> 403 us (1.010)
  Pallas kernels: 134 us -> 145 us
  waiting for transfers between devices: 123 us -> 114 us
    all_to_all x2, waiting for transfers between devices: 48.4 us -> 40 us  [exchange(): lax.all_to_all(blocks[0], AXES, split_axis=0, concat_axis=0, tiled=True)]
    pallas_call x2 -> x3, Pallas kernels: 22.9 us -> 31.1 us  [place(): pl.pallas_call(functools.partial(place_kernel, pieces=len(blocks), final=...]
    reshape x5 -> x10, local copies, waits for them, and re-layouts: 1.78 us -> 6.56 us  [the longest x2 1.6 us: run(): target = targets[which].reshape(len(blocks), -1)[part].reshape(-1, 1)]
  transfers between devices with their start and end apart: 32 -> 32, of which waited for: 16 -> 14; matrix products, arithmetic and copies ran while one was open for 2% -> 4% of each run, Pallas kernels for 19% -> 22%
where the time goes in v4:
time: 403 us; the launch traced here: 402 us
  Pallas kernels  145 us (36%)
  starting transfers between devices  118 us (29%)
  waiting for transfers between devices  114 us (28%)
  local copies, waits for them, and re-layouts  19.7 us (5%)
  other arithmetic  4.65 us (1%)
    ppermute x30, starting transfers between devices, shift(): moved.append(lax.ppermute(pieces[piece], AXES, pairs))  97.2 us
    pallas_call x2, Pallas kernels, middle(): pl.pallas_call(functools.partial(middle_kernel, levels=levels, pieces=len...  77.7 us
    ppermute x30, waiting for transfers between devices, shift(): moved.append(lax.ppermute(pieces[piece], AXES, pairs))  73.6 us
    all_to_all x2, waiting for transfers between devices, exchange(): lax.all_to_all(blocks[0], AXES, split_axis=0, concat_axis=0, tiled=True)  40 us
    pallas_call x2, Pallas kernels, dft(): pl.pallas_call(functools.partial(dft_kernel, depths=depths, pairs=pairs,...  33.7 us
    pallas_call x3, Pallas kernels, place(): pl.pallas_call(functools.partial(place_kernel, pieces=len(blocks), final=...  31.1 us
    all_to_all x2, starting transfers between devices, exchange(): lax.all_to_all(blocks[0], AXES, split_axis=0, concat_axis=0, tiled=True)  20.9 us
  transfers between devices with their start and end apart: 32, of which 14 were waited for; matrix products, arithmetic and copies ran while one was open for 4% of the time, Pallas kernels for 22%

profile of v4, /device:TPU:0, one launch (start us, length us, event | category | flops | bytes accessed | tf_op | source)
XLA Modules:
  0.0 402.0 jit_solution(10641258969547491614)
XLA Ops:
  7.1 394.9 %conditional.1 = (bf16[32,40,2,1280]{3,2,1,0:T(2,128)(2,1)}) conditional(s32[]{:T(128)} %bitcast.40, (s32[320]{0:T(512)}, s32[]{:T(128)}, s32[640]{0:T(1024)}, s32[640]{0:T(1024)}, s32[]{:T(128)}, /*index=5*/s32[8,128]{1,0:T(8,128)S(1)}, bf16[32,40,2,1280]{3,2,1,0:T(2,128)(2,1)}, f32[768,1]{1,0:T(8,128)S(1)}, bf16[80,640,320]{1,2,0:T(8,128)(2,1)}, ...), branch_computations={%region_0.5_spmd, %region_5.10_spmd} | conditional | flops 646018 | bytes 73922640 | solution.py:548
  7.4 15.3 %dft.7 = bf16[16,80,8,128]{3,2,1,0:T(8,128)(2,1)} custom-call(s32[8,128]{1,0:T(8,128)S(1)} %get-tuple-element.110.lats_ref, bf16[32,40,2,1280]{3,2,1,0:T(2,128)(2,1)} %get-tuple-element.176.refs_0_.refs_1_.refs_2_.refs_3_, bf16[32,40,2,1280]{3,2,1,0:T(2,128)(2,1)} %get-tuple-element.176.refs_0_.refs_1_.refs_2_.refs_3_, ...), custom_call_target="tpu_custom_call" | custom-call | tf_op jit(solution)/shard_map/cond/branch_1_fun/dft/pallas_call | solution.py:94
  22.6 7.6 %all-to-all-start.2 = ((bf16[16,80,8,128]{3,2,1,0:T(8,128)(2,1)}), bf16[16,80,8,128]{3,2,1,0:T(8,128)(2,1)S(1)}, u32[]{:S(2)}, u32[]{:S(2)}) async-start(bf16[16,80,8,128]{3,2,1,0:T(8,128)(2,1)} %dft.7), calls=%async_computation.2 | async-start | bytes 5242880 | tf_op jit(solution)/shard_map/cond/branch_1_fun/all_to_all | solution.py:506
  40.3 40.0 %all-to-all-done.2.refs_0_ = bf16[16,80,8,128]{3,2,1,0:T(8,128)(2,1)S(1)} async-done(((bf16[16,80,8,128]{3,2,1,0:T(8,128)(2,1)}), bf16[16,80,8,128]{3,2,1,0:T(8,128)(2,1)S(1)}, u32[]{:S(2)}, u32[]{:S(2)}) %all-to-all-start.2) | async-done | bytes 2621472 | tf_op jit(solution)/shard_map/cond/branch_1_fun/all_to_all | solution.py:506
  81.8 31.1 %middle.7 = bf16[16,80,8,128]{3,2,1,0:T(8,128)(2,1)} custom-call(s32[3,16]{1,0:T(4,128)} %bitcast.148, s32[2,16]{1,0:T(2,128)} %pad_add_fusion.5.peers, bf16[16,80,8,128]{3,2,1,0:T(8,128)(2,1)} %copy-done.3, bf16[80,320,640]{2,1,0:T(8,128)(2,1)} %bitcast.125, bf16[2,160,320]{2,1,0:T(8,128)(2,1)} %fusion.29.refs_17_.refs_2_, ...), custom_call_target="tpu_custom_call" | custom-call | tf_op jit(solution)/shard_map/cond/branch_1_fun/middle/pallas_call | solution.py:274
  113.0 13.3 %all-to-all-start.3 = ((bf16[16,80,8,128]{3,2,1,0:T(8,128)(2,1)}), bf16[16,80,8,128]{3,2,1,0:T(8,128)(2,1)S(1)}, u32[]{:S(2)}, u32[]{:S(2)}) async-start(bf16[16,80,8,128]{3,2,1,0:T(8,128)(2,1)} %middle.7), calls=%async_computation.3 | async-start | bytes 5242880 | tf_op jit(solution)/shard_map/cond/branch_1_fun/all_to_all | solution.py:506
  126.3 18.5 %dft.6 = (bf16[1,94,8,128]{3,2,1,0:T(8,128)(2,1)}, bf16[1,94,8,128]{3,2,1,0:T(8,128)(2,1)}, bf16[1,94,8,128]{3,2,1,0:T(8,128)(2,1)}, bf16[1,94,8,128]{3,2,1,0:T(...) custom-call(s32[8,128]{1,0:T(8,128)S(1)} %get-tuple-element.110.lats, ...), custom_call_target="tpu_custom_call" | custom-call | tf_op jit(solution)/shard_map/cond/branch_1_fun/dft/pallas_call | solution.py:94
  153.0 5.7 %collective-permute-done.31.refs_2_ = bf16[1,94,8,128]{3,2,1,0:T(8,128)(2,1)S(1)} collective-permute-done((bf16[1,94,8,128]{3,2,1,0:T(8,128)(2,1)}, bf16[1,94,8,128]{3,2,1,0:T(8,128)(2,1)S(1)}, u32[]{:S(2)}, u32[]{:S(2)}) %collective-permute-start.31) | collective-permute-done | bytes 192544 | tf_op jit(solution)/shard_map/cond/branch_1_fun/ppermute | solution.py:419
  158.7 7.2 %collective-permute-done.32.refs_3_ = bf16[1,94,8,128]{3,2,1,0:T(8,128)(2,1)S(1)} collective-permute-done((bf16[1,94,8,128]{3,2,1,0:T(8,128)(2,1)}, bf16[1,94,8,128]{3,2,1,0:T(8,128)(2,1)S(1)}, u32[]{:S(2)}, u32[]{:S(2)}) %collective-permute-start.32) | collective-permute-done | bytes 192544 | tf_op jit(solution)/shard_map/cond/branch_1_fun/ppermute | solution.py:419
  165.9 12.4 %collective-permute-done.33.refs_4_ = bf16[1,94,8,128]{3,2,1,0:T(8,128)(2,1)S(1)} collective-permute-done((bf16[1,94,8,128]{3,2,1,0:T(8,128)(2,1)}, bf16[1,94,8,128]{3,2,1,0:T(8,128)(2,1)S(1)}, u32[]{:S(2)}, u32[]{:S(2)}) %collective-permute-start.33) | collective-permute-done | bytes 192544 | tf_op jit(solution)/shard_map/cond/branch_1_fun/ppermute | solution.py:419
  178.3 16.3 %collective-permute-start.38 = (bf16[1,94,8,128]{3,2,1,0:T(8,128)(2,1)}, bf16[1,94,8,128]{3,2,1,0:T(8,128)(2,1)}, u32[]{:S(2)}, u32[]{:S(2)}) collective-permute-start(bf16[1,94,8,128]{3,2,1,0:T(8,128)(2,1)} %get-tuple-element.122), channel_id=1, source_target_pairs={{0,9},{1,8},{2,11},{3,10},{4,13},{5,12},{6,15},{7,14},{8,1},{9,0},... | collective-permute-start | bytes 577544 | tf_op jit(solution)/shard_map/cond/branch_1_fun/ppermute | solution.py:419
  194.6 5.3 %collective-permute-start.39 = (bf16[1,94,8,128]{3,2,1,0:T(8,128)(2,1)}, bf16[1,94,8,128]{3,2,1,0:T(8,128)(2,1)}, u32[]{:S(2)}, u32[]{:S(2)}) collective-permute-start(bf16[1,94,8,128]{3,2,1,0:T(8,128)(2,1)} %get-tuple-element.123), channel_id=1, source_target_pairs={{0,10},{1,11},{2,8},{3,9},{4,14},{5,15},{6,12},{7,13},{8,2},{9,3},... | collective-permute-start | bytes 577544 | tf_op jit(solution)/shard_map/cond/branch_1_fun/ppermute | solution.py:419
  200.2 9.9 %collective-permute-start.40 = (bf16[1,94,8,128]{3,2,1,0:T(8,128)(2,1)}, bf16[1,94,8,128]{3,2,1,0:T(8,128)(2,1)}, u32[]{:S(2)}, u32[]{:S(2)}) collective-permute-start(bf16[1,94,8,128]{3,2,1,0:T(8,128)(2,1)} %get-tuple-element.124), channel_id=1, source_target_pairs={{0,11},{1,10},{2,9},{3,8},{4,15},{5,14},{6,13},{7,12},{8,3},{9,2},... | collective-permute-start | bytes 577544 | tf_op jit(solution)/shard_map/cond/branch_1_fun/ppermute | solution.py:419
  212.5 12.1 %collective-permute-done.37.refs_8_ = bf16[1,94,8,128]{3,2,1,0:T(8,128)(2,1)} collective-permute-done((bf16[1,94,8,128]{3,2,1,0:T(8,128)(2,1)}, bf16[1,94,8,128]{3,2,1,0:T(8,128)(2,1)}, u32[]{:S(2)}, u32[]{:S(2)}) %collective-permute-start.37) | collective-permute-done | bytes 192544 | tf_op jit(solution)/shard_map/cond/branch_1_fun/ppermute | solution.py:419
  224.6 4.0 %collective-permute-start.42 = (bf16[1,94,8,128]{3,2,1,0:T(8,128)(2,1)}, bf16[1,94,8,128]{3,2,1,0:T(8,128)(2,1)}, u32[]{:S(2)}, u32[]{:S(2)}) collective-permute-start(bf16[1,94,8,128]{3,2,1,0:T(8,128)(2,1)} %get-tuple-element.126), channel_id=1, source_target_pairs={{0,13},{1,12},{2,15},{3,14},{4,1},{5,0},{6,3},{7,2},{8,5},{9,4},{1... | collective-permute-start | bytes 577544 | tf_op jit(solution)/shard_map/cond/branch_1_fun/ppermute | solution.py:419
  228.6 5.2 %collective-permute-start.43 = (bf16[1,94,8,128]{3,2,1,0:T(8,128)(2,1)}, bf16[1,94,8,128]{3,2,1,0:T(8,128)(2,1)}, u32[]{:S(2)}, u32[]{:S(2)}) collective-permute-start(bf16[1,94,8,128]{3,2,1,0:T(8,128)(2,1)} %get-tuple-element.127), channel_id=1, source_target_pairs={{0,14},{1,15},{2,12},{3,13},{4,2},{5,3},{6,0},{7,1},{8,6},{9,7},{1... | collective-permute-start | bytes 577544 | tf_op jit(solution)/shard_map/cond/branch_1_fun/ppermute | solution.py:419
  233.8 12.2 %collective-permute-start.44 = (bf16[1,94,8,128]{3,2,1,0:T(8,128)(2,1)}, bf16[1,94,8,128]{3,2,1,0:T(8,128)(2,1)}, u32[]{:S(2)}, u32[]{:S(2)}) collective-permute-start(bf16[1,94,8,128]{3,2,1,0:T(8,128)(2,1)} %get-tuple-element.128), channel_id=1, source_target_pairs={{0,15},{1,14},{2,13},{3,12},{4,3},{5,2},{6,1},{7,0},{8,7},{9,6},{1... | collective-permute-start | bytes 577544 | tf_op jit(solution)/shard_map/cond/branch_1_fun/ppermute | solution.py:419
  250.7 46.6 %middle.6 = (bf16[1,94,8,128]{3,2,1,0:T(8,128)(2,1)}, bf16[1,94,8,128]{3,2,1,0:T(8,128)(2,1)}, bf16[1,94,8,128]{3,2,1,0:T(8,128)(2,1)}, bf16[1,94,8,128]{3,2,1,0...) custom-call(s32[3,24]{1,0:T(4,128)} %slice.36.meta, ...), custom_call_target="tpu_custom_call" | custom-call | tf_op jit(solution)/shard_map/cond/branch_1_fun/middle/pallas_call | solution.py:274
  315.5 4.7 %collective-permute-done.54.refs_6_ = bf16[1,94,8,128]{3,2,1,0:T(8,128)(2,1)S(1)} collective-permute-done((bf16[1,94,8,128]{3,2,1,0:T(8,128)(2,1)}, bf16[1,94,8,128]{3,2,1,0:T(8,128)(2,1)S(1)}, u32[]{:S(2)}, u32[]{:S(2)}) %collective-permute-start.54) | collective-permute-done | bytes 192544 | tf_op jit(solution)/shard_map/cond/branch_1_fun/ppermute | solution.py:419
  325.6 18.2 %collective-permute-done.56.refs_8_ = bf16[1,94,8,128]{3,2,1,0:T(8,128)(2,1)S(1)} collective-permute-done((bf16[1,94,8,128]{3,2,1,0:T(8,128)(2,1)}, bf16[1,94,8,128]{3,2,1,0:T(8,128)(2,1)S(1)}, u32[]{:S(2)}, u32[]{:S(2)}) %collective-permute-start.56) | collective-permute-done | bytes 192544 | tf_op jit(solution)/shard_map/cond/branch_1_fun/ppermute | solution.py:419
  352.6 12.1 %collective-permute-start.48 = (bf16[1,94,8,128]{3,2,1,0:T(8,128)(2,1)}, bf16[1,94,8,128]{3,2,1,0:T(8,128)(2,1)S(1)}, u32[]{:S(2)}, u32[]{:S(2)}) collective-permute-start(bf16[1,94,8,128]{3,2,1,0:T(8,128)(2,1)} %get-tuple-element.136), channel_id=1, source_target_pairs={{0,15},{1,14},{2,13},{3,12},{4,3},{5,2},{6,1},{7,0},{8,7},{9,6},{1... | collective-permute-start | bytes 577544 | tf_op jit(solution)/shard_map/cond/branch_1_fun/ppermute | solution.py:419
  369.3 8.8 %place.9.refs_13_ = bf16[2560,1280]{1,0:T(8,128)(2,1)} custom-call(s32[40]{0:T(128)} %dynamic-slice_bitcast_fusion.1.rank, bf16[16,80,8,128]{3,2,1,0:T(8,128)(2,1)} %copy-done.5, s32[512,1]{1,0:T(8,128)} %add.578.refs_1_), custom_call_target="tpu_custom_call" | custom-call | tf_op jit(solution)/shard_map/cond/branch_1_fun/place/pallas_call | solution.py:370
  378.1 12.7 %place.10.refs_5_ = bf16[2560,1280]{1,0:T(8,128)(2,1)} custom-call(s32[40]{0:T(128)} %dynamic-slice_bitcast_fusion.1.rank, bf16[1,94,8,128]{3,2,1,0:T(8,128)(2,1)} %get-tuple-element.137.refs_0_, bf16[1,94,8,128]{3,2,1,0:T(8,128)(2,1)} %copy-done.20, bf16[1,94,8,128]{3,2,1,0:T(8,128)(2,1)} %copy-done.21, bf16[1,94,8,128]{3,2,1,0:T(8,128)(2,1)} %copy-done.22, ...), custom_call_target="tpu_custom_call" | custom-call | tf_op jit(solution)/shard_map/cond/branch_1_fun/place/pallas_call | solution.py:370
  392.3 9.7 %place.11 = bf16[32,40,2,1280]{3,2,1,0:T(2,128)(2,1)} custom-call(s32[40]{0:T(128)} %dynamic-slice_bitcast_fusion.1.rank, bf16[1,94,8,128]{3,2,1,0:T(8,128)(2,1)} %copy-done.16, bf16[1,94,8,128]{3,2,1,0:T(8,128)(2,1)} %copy-done.17, bf16[1,94,8,128]{3,2,1,0:T(8,128)(2,1)} %copy-done.18, bf16[1,94,8,128]{3,2,1,0:T(8,128)(2,1)} %copy-done.19, ...), custom_call_target="tpu_custom_call" | custom-call | tf_op jit(solution)/shard_map/cond/branch_1_fun/place/pallas_call | solution.py:370
  (173 shorter events, 71.9 us)
Async XLA Ops:
  22.6 57.7 %all-to-all-start.2 = ((bf16[16,80,8,128]{3,2,1,0:T(8,128)(2,1)}), bf16[16,80,8,128]{3,2,1,0:T(8,128)(2,1)S(1)}, u32[]{:S(2)}, u32[]{:S(2)}) async-start(bf16[16,80,8,128]{3,2,1,0:T(8,128)(2,1)} %dft.7), calls=%async_computation.2 | async-start | bytes 5242880 | tf_op jit(solution)/shard_map/cond/branch_1_fun/all_to_all | solution.py:506
  113.0 254.9 %all-to-all-start.3 = ((bf16[16,80,8,128]{3,2,1,0:T(8,128)(2,1)}), bf16[16,80,8,128]{3,2,1,0:T(8,128)(2,1)S(1)}, u32[]{:S(2)}, u32[]{:S(2)}) async-start(bf16[16,80,8,128]{3,2,1,0:T(8,128)(2,1)} %middle.7), calls=%async_computation.3 | async-start | bytes 5242880 | tf_op jit(solution)/shard_map/cond/branch_1_fun/all_to_all | solution.py:506
  146.9 19.0 %collective-permute-start.32 = (bf16[1,94,8,128]{3,2,1,0:T(8,128)(2,1)}, bf16[1,94,8,128]{3,2,1,0:T(8,128)(2,1)S(1)}, u32[]{:S(2)}, u32[]{:S(2)}) collective-permute-start(bf16[1,94,8,128]{3,2,1,0:T(8,128)(2,1)} %get-tuple-element.116), channel_id=1, source_target_pairs={{0,3},{1,2},{2,1},{3,0},{4,7},{5,6},{6,5},{7,4},{8,11},{9,10},{10,... | collective-permute-start | bytes 577544 | tf_op jit(solution)/shard_map/cond/branch_1_fun/ppermute | solution.py:419
  146.9 31.4 %collective-permute-start.33 = (bf16[1,94,8,128]{3,2,1,0:T(8,128)(2,1)}, bf16[1,94,8,128]{3,2,1,0:T(8,128)(2,1)S(1)}, u32[]{:S(2)}, u32[]{:S(2)}) collective-permute-start(bf16[1,94,8,128]{3,2,1,0:T(8,128)(2,1)} %get-tuple-element.117), channel_id=1, source_target_pairs={{0,4},{1,5},{2,6},{3,7},{4,8},{5,9},{6,10},{7,11},{8,12},{9,13},{1... | collective-permute-start | bytes 577544 | tf_op jit(solution)/shard_map/cond/branch_1_fun/ppermute | solution.py:419
  148.6 46.0 %collective-permute-start.34 = (bf16[1,94,8,128]{3,2,1,0:T(8,128)(2,1)}, bf16[1,94,8,128]{3,2,1,0:T(8,128)(2,1)}, u32[]{:S(2)}, u32[]{:S(2)}) collective-permute-start(bf16[1,94,8,128]{3,2,1,0:T(8,128)(2,1)} %get-tuple-element.118), channel_id=1, source_target_pairs={{0,5},{1,4},{2,7},{3,6},{4,9},{5,8},{6,11},{7,10},{8,13},{9,12},{1... | collective-permute-start | bytes 577544 | tf_op jit(solution)/shard_map/cond/branch_1_fun/ppermute | solution.py:419
  150.6 49.6 %collective-permute-start.35 = (bf16[1,94,8,128]{3,2,1,0:T(8,128)(2,1)}, bf16[1,94,8,128]{3,2,1,0:T(8,128)(2,1)}, u32[]{:S(2)}, u32[]{:S(2)}) collective-permute-start(bf16[1,94,8,128]{3,2,1,0:T(8,128)(2,1)} %get-tuple-element.119), channel_id=1, source_target_pairs={{0,6},{1,7},{2,4},{3,5},{4,10},{5,11},{6,8},{7,9},{8,14},{9,15},{1... | collective-permute-start | bytes 577544 | tf_op jit(solution)/shard_map/cond/branch_1_fun/ppermute | solution.py:419
  158.7 51.4 %collective-permute-start.36 = (bf16[1,94,8,128]{3,2,1,0:T(8,128)(2,1)}, bf16[1,94,8,128]{3,2,1,0:T(8,128)(2,1)}, u32[]{:S(2)}, u32[]{:S(2)}) collective-permute-start(bf16[1,94,8,128]{3,2,1,0:T(8,128)(2,1)} %get-tuple-element.120), channel_id=1, source_target_pairs={{0,7},{1,6},{2,5},{3,4},{4,11},{5,10},{6,9},{7,8},{8,15},{9,14},{1... | collective-permute-start | bytes 577544 | tf_op jit(solution)/shard_map/cond/branch_1_fun/ppermute | solution.py:419
  165.9 58.6 %collective-permute-start.37 = (bf16[1,94,8,128]{3,2,1,0:T(8,128)(2,1)}, bf16[1,94,8,128]{3,2,1,0:T(8,128)(2,1)}, u32[]{:S(2)}, u32[]{:S(2)}) collective-permute-start(bf16[1,94,8,128]{3,2,1,0:T(8,128)(2,1)} %get-tuple-element.121), channel_id=1, source_target_pairs={{0,8},{1,9},{2,10},{3,11},{4,12},{5,13},{6,14},{7,15},{8,0},{9,1},... | collective-permute-start | bytes 577544 | tf_op jit(solution)/shard_map/cond/branch_1_fun/ppermute | solution.py:419
  178.3 50.3 %collective-permute-start.38 = (bf16[1,94,8,128]{3,2,1,0:T(8,128)(2,1)}, bf16[1,94,8,128]{3,2,1,0:T(8,128)(2,1)}, u32[]{:S(2)}, u32[]{:S(2)}) collective-permute-start(bf16[1,94,8,128]{3,2,1,0:T(8,128)(2,1)} %get-tuple-element.122), channel_id=1, source_target_pairs={{0,9},{1,8},{2,11},{3,10},{4,13},{5,12},{6,15},{7,14},{8,1},{9,0},... | collective-permute-start | bytes 577544 | tf_op jit(solution)/shard_map/cond/branch_1_fun/ppermute | solution.py:419
  194.6 39.2 %collective-permute-start.39 = (bf16[1,94,8,128]{3,2,1,0:T(8,128)(2,1)}, bf16[1,94,8,128]{3,2,1,0:T(8,128)(2,1)}, u32[]{:S(2)}, u32[]{:S(2)}) collective-permute-start(bf16[1,94,8,128]{3,2,1,0:T(8,128)(2,1)} %get-tuple-element.123), channel_id=1, source_target_pairs={{0,10},{1,11},{2,8},{3,9},{4,14},{5,15},{6,12},{7,13},{8,2},{9,3},... | collective-permute-start | bytes 577544 | tf_op jit(solution)/shard_map/cond/branch_1_fun/ppermute | solution.py:419
  200.2 46.5 %collective-permute-start.40 = (bf16[1,94,8,128]{3,2,1,0:T(8,128)(2,1)}, bf16[1,94,8,128]{3,2,1,0:T(8,128)(2,1)}, u32[]{:S(2)}, u32[]{:S(2)}) collective-permute-start(bf16[1,94,8,128]{3,2,1,0:T(8,128)(2,1)} %get-tuple-element.124), channel_id=1, source_target_pairs={{0,11},{1,10},{2,9},{3,8},{4,15},{5,14},{6,13},{7,12},{8,3},{9,2},... | collective-permute-start | bytes 577544 | tf_op jit(solution)/shard_map/cond/branch_1_fun/ppermute | solution.py:419
  210.1 36.6 %collective-permute-start.41 = (bf16[1,94,8,128]{3,2,1,0:T(8,128)(2,1)}, bf16[1,94,8,128]{3,2,1,0:T(8,128)(2,1)}, u32[]{:S(2)}, u32[]{:S(2)}) collective-permute-start(bf16[1,94,8,128]{3,2,1,0:T(8,128)(2,1)} %get-tuple-element.125), channel_id=1, source_target_pairs={{0,12},{1,13},{2,14},{3,15},{4,0},{5,1},{6,2},{7,3},{8,4},{9,5},{1... | collective-permute-start | bytes 577544 | tf_op jit(solution)/shard_map/cond/branch_1_fun/ppermute | solution.py:419
  224.6 22.1 %collective-permute-start.42 = (bf16[1,94,8,128]{3,2,1,0:T(8,128)(2,1)}, bf16[1,94,8,128]{3,2,1,0:T(8,128)(2,1)}, u32[]{:S(2)}, u32[]{:S(2)}) collective-permute-start(bf16[1,94,8,128]{3,2,1,0:T(8,128)(2,1)} %get-tuple-element.126), channel_id=1, source_target_pairs={{0,13},{1,12},{2,15},{3,14},{4,1},{5,0},{6,3},{7,2},{8,5},{9,4},{1... | collective-permute-start | bytes 577544 | tf_op jit(solution)/shard_map/cond/branch_1_fun/ppermute | solution.py:419
  228.6 18.0 %collective-permute-start.43 = (bf16[1,94,8,128]{3,2,1,0:T(8,128)(2,1)}, bf16[1,94,8,128]{3,2,1,0:T(8,128)(2,1)}, u32[]{:S(2)}, u32[]{:S(2)}) collective-permute-start(bf16[1,94,8,128]{3,2,1,0:T(8,128)(2,1)} %get-tuple-element.127), channel_id=1, source_target_pairs={{0,14},{1,15},{2,12},{3,13},{4,2},{5,3},{6,0},{7,1},{8,6},{9,7},{1... | collective-permute-start | bytes 577544 | tf_op jit(solution)/shard_map/cond/branch_1_fun/ppermute | solution.py:419
  233.8 16.8 %collective-permute-start.44 = (bf16[1,94,8,128]{3,2,1,0:T(8,128)(2,1)}, bf16[1,94,8,128]{3,2,1,0:T(8,128)(2,1)}, u32[]{:S(2)}, u32[]{:S(2)}) collective-permute-start(bf16[1,94,8,128]{3,2,1,0:T(8,128)(2,1)} %get-tuple-element.128), channel_id=1, source_target_pairs={{0,15},{1,14},{2,13},{3,12},{4,3},{5,2},{6,1},{7,0},{8,7},{9,6},{1... | collective-permute-start | bytes 577544 | tf_op jit(solution)/shard_map/cond/branch_1_fun/ppermute | solution.py:419
  303.4 16.7 %collective-permute-start.54 = (bf16[1,94,8,128]{3,2,1,0:T(8,128)(2,1)}, bf16[1,94,8,128]{3,2,1,0:T(8,128)(2,1)S(1)}, u32[]{:S(2)}, u32[]{:S(2)}) collective-permute-start(bf16[1,94,8,128]{3,2,1,0:T(8,128)(2,1)} %get-tuple-element.143), channel_id=1, source_target_pairs={{0,6},{1,7},{2,4},{3,5},{4,10},{5,11},{6,8},{7,9},{8,14},{9,15},{1... | collective-permute-start | bytes 577544 | tf_op jit(solution)/shard_map/cond/branch_1_fun/ppermute | solution.py:419
  310.3 33.4 %collective-permute-start.56 = (bf16[1,94,8,128]{3,2,1,0:T(8,128)(2,1)}, bf16[1,94,8,128]{3,2,1,0:T(8,128)(2,1)S(1)}, u32[]{:S(2)}, u32[]{:S(2)}) collective-permute-start(bf16[1,94,8,128]{3,2,1,0:T(8,128)(2,1)} %get-tuple-element.145), channel_id=1, source_target_pairs={{0,8},{1,9},{2,10},{3,11},{4,12},{5,13},{6,14},{7,15},{8,0},{9,1},... | collective-permute-start | bytes 577544 | tf_op jit(solution)/shard_map/cond/branch_1_fun/ppermute | solution.py:419
  311.0 36.8 %collective-permute-start.57 = (bf16[1,94,8,128]{3,2,1,0:T(8,128)(2,1)}, bf16[1,94,8,128]{3,2,1,0:T(8,128)(2,1)S(1)}, u32[]{:S(2)}, u32[]{:S(2)}) collective-permute-start(bf16[1,94,8,128]{3,2,1,0:T(8,128)(2,1)} %get-tuple-element.146), channel_id=1, source_target_pairs={{0,9},{1,8},{2,11},{3,10},{4,13},{5,12},{6,15},{7,14},{8,1},{9,0},... | collective-permute-start | bytes 577544 | tf_op jit(solution)/shard_map/cond/branch_1_fun/ppermute | solution.py:419
  314.6 38.0 %collective-permute-start.58 = (bf16[1,94,8,128]{3,2,1,0:T(8,128)(2,1)}, bf16[1,94,8,128]{3,2,1,0:T(8,128)(2,1)S(1)}, u32[]{:S(2)}, u32[]{:S(2)}) collective-permute-start(bf16[1,94,8,128]{3,2,1,0:T(8,128)(2,1)} %get-tuple-element.147), channel_id=1, source_target_pairs={{0,10},{1,11},{2,8},{3,9},{4,14},{5,15},{6,12},{7,13},{8,2},{9,3},... | collective-permute-start | bytes 577544 | tf_op jit(solution)/shard_map/cond/branch_1_fun/ppermute | solution.py:419
  320.1 58.0 %collective-permute-start.59 = (bf16[1,94,8,128]{3,2,1,0:T(8,128)(2,1)}, bf16[1,94,8,128]{3,2,1,0:T(8,128)(2,1)}, u32[]{:S(2)}, u32[]{:S(2)}) collective-permute-start(bf16[1,94,8,128]{3,2,1,0:T(8,128)(2,1)} %get-tuple-element.148), channel_id=1, source_target_pairs={{0,11},{1,10},{2,9},{3,8},{4,15},{5,14},{6,13},{7,12},{8,3},{9,2},... | collective-permute-start | bytes 577544 | tf_op jit(solution)/shard_map/cond/branch_1_fun/ppermute | solution.py:419
  323.1 67.7 %collective-permute-start.45 = (bf16[1,94,8,128]{3,2,1,0:T(8,128)(2,1)}, bf16[1,94,8,128]{3,2,1,0:T(8,128)(2,1)S(1)}, u32[]{:S(2)}, u32[]{:S(2)}) collective-permute-start(bf16[1,94,8,128]{3,2,1,0:T(8,128)(2,1)} %get-tuple-element.133), channel_id=1, source_target_pairs={{0,12},{1,13},{2,14},{3,15},{4,0},{5,1},{6,2},{7,3},{8,4},{9,5},{1... | collective-permute-start | bytes 577544 | tf_op jit(solution)/shard_map/cond/branch_1_fun/ppermute | solution.py:419
  343.7 47.1 %collective-permute-start.46 = (bf16[1,94,8,128]{3,2,1,0:T(8,128)(2,1)}, bf16[1,94,8,128]{3,2,1,0:T(8,128)(2,1)S(1)}, u32[]{:S(2)}, u32[]{:S(2)}) collective-permute-start(bf16[1,94,8,128]{3,2,1,0:T(8,128)(2,1)} %get-tuple-element.134), channel_id=1, source_target_pairs={{0,13},{1,12},{2,15},{3,14},{4,1},{5,0},{6,3},{7,2},{8,5},{9,4},{1... | collective-permute-start | bytes 577544 | tf_op jit(solution)/shard_map/cond/branch_1_fun/ppermute | solution.py:419
  347.9 43.0 %collective-permute-start.47 = (bf16[1,94,8,128]{3,2,1,0:T(8,128)(2,1)}, bf16[1,94,8,128]{3,2,1,0:T(8,128)(2,1)S(1)}, u32[]{:S(2)}, u32[]{:S(2)}) collective-permute-start(bf16[1,94,8,128]{3,2,1,0:T(8,128)(2,1)} %get-tuple-element.135), channel_id=1, source_target_pairs={{0,14},{1,15},{2,12},{3,13},{4,2},{5,3},{6,0},{7,1},{8,6},{9,7},{1... | collective-permute-start | bytes 577544 | tf_op jit(solution)/shard_map/cond/branch_1_fun/ppermute | solution.py:419
  352.6 38.3 %collective-permute-start.48 = (bf16[1,94,8,128]{3,2,1,0:T(8,128)(2,1)}, bf16[1,94,8,128]{3,2,1,0:T(8,128)(2,1)S(1)}, u32[]{:S(2)}, u32[]{:S(2)}) collective-permute-start(bf16[1,94,8,128]{3,2,1,0:T(8,128)(2,1)} %get-tuple-element.136), channel_id=1, source_target_pairs={{0,15},{1,14},{2,13},{3,12},{4,3},{5,2},{6,1},{7,0},{8,7},{9,6},{1... | collective-permute-start | bytes 577544 | tf_op jit(solution)/shard_map/cond/branch_1_fun/ppermute | solution.py:419
  (34 other events, 814.7 us)

commit v5 on v4

--- a/solution.py
+++ b/solution.py
@@ -46,9 +46,17 @@
 
 
 def dft_kernel(lats_ref, *refs, depths, pairs, slots):
-    views, freq, outs, table = refs[:slots], refs[slots], refs[slots + 1 : -1], refs[-1]
+    views, freq, outs = refs[:slots], refs[slots], refs[slots + 1 : -3]
+    table, halves = refs[-3], refs[-2:]
     fields, lon_count = views[0].shape[0], views[0].shape[3]
     step = pl.program_id(0)
+    starts, _ = units(depths)
+    each = outs[0].shape[0]
+
+    def fill(half):
+        for slot, view in enumerate(views):
+            rows = slice(slot * 2 * fields, (slot + 1) * 2 * fields)
+            half[rows, :] = view[:, 0].reshape(2 * fields, lon_count)
 
     @pl.when(step == 0)
     def _():
@@ -59,23 +67,28 @@
             first = pl.multiple_of(i * rows, rows)
             table[pl.ds(first, rows), :] = cosine_rows(freq, first, rows, lon_count)
 
-    values = [view[:, 0].reshape(2 * fields, lon_count) for view in views]
-    spectra = dot(table[...], jnp.concatenate(values, 0), NT)
-    spectra = spectra.reshape(-1, len(depths), 2, TILE, pairs * LANES)
-    starts, _ = units(depths)
-    each = outs[0].shape[0]
-
-    def store(tile, pair, where):
+        fill(halves[0])
+
+    def store(spectra, tile, pair, where):
         for part in range(2):
             block = spectra[:, tile, part, :, pair * LANES : (pair + 1) * LANES]
             block = block.astype(jnp.bfloat16)
             for piece, out in enumerate(outs):
                 out[:, starts[tile][part] + where] = block[piece * each : (piece + 1) * each]
 
-    for pair in range(pairs):
-        where = step * pairs + pair
-        for tile, depth in enumerate(depths):
-            pl.when(where < depth)(functools.partial(store, tile, pair, where))
+    def advance(ready, later):
+        spectra = dot(table[...], ready[...], NT)
+        fill(later)
+        spectra = spectra.reshape(-1, len(depths), 2, TILE, pairs * LANES)
+        for pair in range(pairs):
+            where = (step - 1) * pairs + pair
+            for tile, depth in enumerate(depths):
+                pl.when(where < depth)(functools.partial(store, spectra, tile, pair, where))
+
+    odd = step % 2 == 1
+    pl.when(odd)(functools.partial(advance, halves[0], halves[1]))
+    even = (step > 0) & (step % 2 == 0)
+    pl.when(even)(functools.partial(advance, halves[1], halves[0]))
 
 
 def dft(grid, order, freq, depths, owners, lats, low, separate):
@@ -83,23 +96,26 @@
     count = lats // low
     pairs = 2 if count % 2 == 0 else 1
     slots = pairs * low
+    steps = count // pairs
     pieces, each = (owners, 1) if separate else (1, owners)
     shape = (each, units(depths)[1], TILE, LANES)
 
     def view(slot):
         return pl.BlockSpec(
-            (fields, 1, 2, lon_count), lambda i, order: (0, order[0, i * slots + slot], 0, 0)
+            (fields, 1, 2, lon_count),
+            lambda i, order: (0, order[0, jnp.minimum(i, steps - 1) * slots + slot], 0, 0),
         )
 
     return pl.pallas_call(
         functools.partial(dft_kernel, depths=depths, pairs=pairs, slots=slots),
         grid_spec=pltpu.PrefetchScalarGridSpec(
             num_scalar_prefetch=1,
-            grid=(count // pairs,),
+            grid=(steps + 1,),
             in_specs=[view(slot) for slot in range(slots)]
             + [pl.BlockSpec(freq.shape, lambda i, _: (0, 0))],
             out_specs=[pl.BlockSpec(shape, lambda i, _: (0, 0, 0, 0))] * pieces,
-            scratch_shapes=[pltpu.VMEM((freq.shape[0], lon_count), jnp.bfloat16)],
+            scratch_shapes=[pltpu.VMEM((freq.shape[0], lon_count), jnp.bfloat16)]
+            + [pltpu.VMEM((pairs * LANES, lon_count), jnp.bfloat16)] * 2,
         ),
         out_shape=[jax.ShapeDtypeStruct(shape, jnp.bfloat16)] * pieces,
         name="dft",
@@ -114,12 +130,12 @@
     waves_ref, trim_ref, lats_ref, *outs, groups, levels, share, low, small, sizes, axes
 ):
     freqs, notes = outs[:-1], outs[-1]
-    total = waves_ref.shape[1]
+    total = waves_ref.shape[0]
     near_count = total // groups
-    waves = waves_ref[...].astype(jnp.float32)
+    waves = waves_ref[...].reshape(1, -1).astype(jnp.float32)
     lane = lax.broadcasted_iota(jnp.int32, (1, total), 1).astype(jnp.float32)
     number = lax.broadcasted_iota(jnp.int32, (total, 1), 0).astype(jnp.float32)
-    trim_column = as_column(trim_ref[...].astype(jnp.float32))
+    trim_column = as_column(trim_ref[...].reshape(1, -1).astype(jnp.float32))
     trims = jnp.sum(jnp.where(number == waves, trim_column, 0.0), 0, keepdims=True)
     base = jnp.floor((lane + 0.5) * (1.0 / near_count)) * near_count
     keys = (base * 8.0 + trims * near_count) + (lane - base)
@@ -143,29 +159,32 @@
             freq[piece * rows : (piece + 1) * rows, :] = jnp.sum(chosen, 1, keepdims=True)
         first += size
 
-    lats = lats_ref[...]
+    lats = lats_ref[...].reshape(1, -1).astype(jnp.float32)
+    lat_count = lats.shape[1]
+    slots = lat_count // groups
+    lane = lax.broadcasted_iota(jnp.int32, (1, lat_count), 1).astype(jnp.float32)
+    origin = jnp.floor((lane + 0.5) * (1.0 / slots)) * slots
+    owner = lax.broadcasted_iota(jnp.int32, (groups, 1), 0).astype(jnp.float32) * slots == origin
     fits = jnp.full((1, 1), 1, jnp.int32)
     for tile, depth in enumerate(small):
         spot = (rank - base) == float(min(tile * TILE, share - 1) * levels)
-        least = jnp.min(jnp.where(spot, trims, 8.0), 1, keepdims=True).astype(jnp.int32)
-        needed = jnp.where(lats >= LBLK * least, 1.0, 0.0)
+        least = jnp.min(jnp.where(spot, trims, 8.0), 1, keepdims=True)
+        needed = jnp.where(owner & (lats >= LBLK * least), 1.0, 0.0)
         needed = jnp.max(jnp.sum(needed, 1, keepdims=True), 0, keepdims=True)
         fits = fits * jnp.where(needed <= float(low * depth), 1, 0)
 
-    count = lats.shape[1]
-    mine = lats_ref[pl.ds(group, 1), :].astype(jnp.float32)
-    mine = jnp.concatenate([mine, jnp.full((1, LANES - count), -1.0, jnp.float32)], 1)
+    keys = (origin + slots) * lat_count - lats
+    place_of = jnp.sum(jnp.where(as_column(keys) < keys, 1.0, 0.0), 0, keepdims=True)
     spot = lax.broadcasted_iota(jnp.int32, (1, LANES), 1).astype(jnp.float32)
-    mine = mine * LANES - spot
-    place_of = jnp.sum(jnp.where(as_column(mine) > mine, 1.0, 0.0), 0, keepdims=True)
-    index = lax.broadcasted_iota(jnp.int32, (LANES, 1), 0).astype(jnp.float32)
-    order = jnp.sum(jnp.where(as_column(place_of) == spot, index, 0.0), 0, keepdims=True)
+    start = (group * slots).astype(jnp.float32)
+    index = lax.broadcasted_iota(jnp.int32, (lat_count, 1), 0).astype(jnp.float32) - start
+    chosen = jnp.where(as_column(place_of) - start == spot, index, 0.0)
+    order = jnp.sum(chosen, 0, keepdims=True)
     notes[0:1, :] = order.astype(jnp.int32)
     notes[1:2, :] = jnp.broadcast_to(fits, (1, LANES))
 
 
 def plan(wave_order, trim, lat_order, groups, levels, share, low, small, sizes):
-    total = wave_order.shape[0]
     owners = groups * levels
     return pl.pallas_call(
         functools.partial(
@@ -177,7 +196,7 @@
         ]
         + [jax.ShapeDtypeStruct((TILE, LANES), jnp.int32)],
         name="plan",
-    )(wave_order.reshape(1, total), trim.reshape(1, total), lat_order.reshape(groups, -1))
+    )(wave_order, trim, lat_order)
 
 
 def middle_kernel(meta, peers, *refs, levels, pieces, depths, count):
@@ -293,7 +312,7 @@
     blocks, refs = refs[:pieces], refs[pieces:]
     target, refs = refs[0], refs[1:]
     start = refs[0] if with_start else None
-    out, table, gathered = refs[-3:]
+    out, table, gathered, held = refs[-4:]
     per = table.shape[0] // split
     each = blocks[0].shape[0]
     span_rows = 2 * TILE * len(depths)
@@ -311,8 +330,8 @@
             table[rows, :] = jnp.where(column[rows] == wanted, 1.0, 0.0).astype(jnp.bfloat16)
 
     lane = lax.broadcasted_iota(jnp.int32, (1, LANES), 1) // span
-    turned = []
-    for item in range(batch):
+
+    def turn(item):
         merged = None
         for slot in range(low):
             index = rank[(step * batch + item) * low + slot]
@@ -329,8 +348,17 @@
                         gathered[slot, first : first + TILE, :] = block
             values = pltpu.roll(gathered[slot], ((slot - side) % low) * span, 1)
             merged = values if merged is None else jnp.where(lane == slot, values, merged)
-        turned.append(merged.T.astype(jnp.bfloat16))
-    rows = jnp.concatenate(turned, 0)
+        return merged.T.astype(jnp.bfloat16)
+
+    if final:
+        rows = jnp.concatenate([turn(item) for item in range(batch)], 0)
+    else:
+
+        @pl.loop(0, batch)
+        def _(item):
+            held[pl.ds(pl.multiple_of(item * LANES, LANES), LANES), :] = turn(item)
+
+        rows = held[...]
     placed = []
     for piece in range(split):
         part = slice(piece * per, (piece + 1) * per)
@@ -386,6 +414,7 @@
             scratch_shapes=[
                 pltpu.VMEM((rows, columns // split), jnp.bfloat16),
                 pltpu.VMEM((low, rows, LANES), jnp.float32),
+                pltpu.VMEM((batch * LANES, rows), jnp.bfloat16),
             ],
         ),
         out_shape=out_shape,
@@ -409,6 +438,12 @@
     else:
         low = (near + (fast - piece % fast if back else piece % fast)) % fast
     return high * fast + low
+
+
+def late_pieces(groups, levels):
+    fast = 2 * levels if groups % 2 == 0 else levels
+    half = groups * levels // fast // 2
+    return [p for p in range(1, groups * levels) if p // fast == half]
 
 
 def shift(pieces, groups, levels):
@@ -524,12 +559,16 @@
         result = None
         for which, blocks in enumerate(returned):
             last = which == len(returned) - 1
-            kept = len(blocks) * 3 // 4
-            parts = [slice(0, kept), slice(kept, None)] if kept else [slice(0, None)]
+            late = late_pieces(groups, levels) if len(blocks) > 1 else []
+            parts = [[p for p in range(len(blocks)) if p not in late], late]
+            parts = [part for part in parts if part]
+            rows = targets[which].reshape(len(blocks), -1)
             for part in parts:
-                target = targets[which].reshape(len(blocks), -1)[part].reshape(-1, 1)
+                target = jnp.concatenate([rows[p] for p in part]).reshape(-1, 1)
+                if len(part) == len(blocks):
+                    target = targets[which]
                 result = place(
-                    blocks[part], rank, target, result, lon_count, fields, low,
+                    [blocks[p] for p in part], rank, target, result, lon_count, fields, low,
                     last and part is parts[-1], depths[which],
                 )
         return result

time: 403 us -> 382 us (0.948)
  waiting for transfers between devices: 114 us -> 88.4 us
  Pallas kernels: 145 us -> 151 us
    ppermute x30, waiting for transfers between devices: 73.6 us -> 48.4 us  [shift(): moved.append(lax.ppermute(pieces[piece], AXES, pairs))]
    pallas_call x3, Pallas kernels: 31.1 us -> 36.7 us  [place(): pl.pallas_call(functools.partial(place_kernel, pieces=len(blocks), final=...]
  transfers between devices with their start and end apart: 32 -> 32, of which waited for: 14 -> 10; matrix products, arithmetic and copies ran while one was open for 4% -> 4% of each run, Pallas kernels for 22% -> 24%
where the time goes in v5:
time: 382 us; the launch traced here: 381 us
  Pallas kernels  151 us (40%)
  starting transfers between devices  118 us (31%)
  waiting for transfers between devices  88.4 us (23%)
  local copies, waits for them, and re-layouts  17.9 us (5%)
  other arithmetic  4.67 us (1%)
    ppermute x30, starting transfers between devices, shift(): moved.append(lax.ppermute(pieces[piece], AXES, pairs))  97.1 us
    pallas_call x2, Pallas kernels, middle(): pl.pallas_call(functools.partial(middle_kernel, levels=levels, pieces=len...  77.8 us
    ppermute x30, waiting for transfers between devices, shift(): moved.append(lax.ppermute(pieces[piece], AXES, pairs))  48.4 us
    all_to_all x2, waiting for transfers between devices, exchange(): lax.all_to_all(blocks[0], AXES, split_axis=0, concat_axis=0, tiled=True)  40 us
    pallas_call x3, Pallas kernels, place(): pl.pallas_call(functools.partial(place_kernel, pieces=len(blocks), final=...  36.7 us
    pallas_call x2, Pallas kernels, dft(): pl.pallas_call(functools.partial(dft_kernel, depths=depths, pairs=pairs,...  34.4 us
    all_to_all x2, starting transfers between devices, exchange(): lax.all_to_all(blocks[0], AXES, split_axis=0, concat_axis=0, tiled=True)  20.9 us
  transfers between devices with their start and end apart: 32, of which 10 were waited for; matrix products, arithmetic and copies ran while one was open for 4% of the time, Pallas kernels for 24%

profile of v5, /device:TPU:0, one launch (start us, length us, event | category | flops | bytes accessed | tf_op | source)
XLA Modules:
  0.0 381.4 jit_solution(12459531532774568448)
XLA Ops:
  3.3 378.1 %conditional.1 = (bf16[32,40,2,1280]{3,2,1,0:T(2,128)(2,1)}) conditional(s32[]{:T(128)} %bitcast.42, (s32[320]{0:T(512)}, s32[]{:T(128)}, s32[640]{0:T(1024)}, s32[640]{0:T(1024)}, s32[]{:T(128)}, /*index=5*/s32[8,128]{1,0:T(8,128)S(1)}, bf16[32,40,2,1280]{3,2,1,0:T(2,128)(2,1)}, f32[768,1]{1,0:T(8,128)S(1)}, bf16[80,640,320]{1,2,0:T(8,128)(2,1)}, ...), branch_computations={%region_0.5_spmd, %region_5.10_spmd} | conditional | flops 646594 | bytes 73934928 | solution.py:587
  3.6 15.6 %dft.7 = bf16[16,80,8,128]{3,2,1,0:T(8,128)(2,1)} custom-call(s32[8,128]{1,0:T(8,128)S(1)} %get-tuple-element.110.lats_ref, bf16[32,40,2,1280]{3,2,1,0:T(2,128)(2,1)} %get-tuple-element.176.refs_0_.refs_1_.refs_2_.refs_3_, bf16[32,40,2,1280]{3,2,1,0:T(2,128)(2,1)} %get-tuple-element.176.refs_0_.refs_1_.refs_2_.refs_3_, ...), custom_call_target="tpu_custom_call" | custom-call | tf_op jit(solution)/shard_map/cond/branch_1_fun/dft/pallas_call | solution.py:109
  19.2 7.6 %all-to-all-start.2 = ((bf16[16,80,8,128]{3,2,1,0:T(8,128)(2,1)}), bf16[16,80,8,128]{3,2,1,0:T(8,128)(2,1)S(1)}, u32[]{:S(2)}, u32[]{:S(2)}) async-start(bf16[16,80,8,128]{3,2,1,0:T(8,128)(2,1)} %dft.7), calls=%async_computation.2 | async-start | bytes 5242880 | tf_op jit(solution)/shard_map/cond/branch_1_fun/all_to_all | solution.py:541
  36.8 40.0 %all-to-all-done.2.refs_0_ = bf16[16,80,8,128]{3,2,1,0:T(8,128)(2,1)S(1)} async-done(((bf16[16,80,8,128]{3,2,1,0:T(8,128)(2,1)}), bf16[16,80,8,128]{3,2,1,0:T(8,128)(2,1)S(1)}, u32[]{:S(2)}, u32[]{:S(2)}) %all-to-all-start.2) | async-done | bytes 2621472 | tf_op jit(solution)/shard_map/cond/branch_1_fun/all_to_all | solution.py:541
  78.4 31.1 %middle.7 = bf16[16,80,8,128]{3,2,1,0:T(8,128)(2,1)} custom-call(s32[3,16]{1,0:T(4,128)} %bitcast.150, s32[2,16]{1,0:T(2,128)} %pad_add_fusion.7.peers, bf16[16,80,8,128]{3,2,1,0:T(8,128)(2,1)} %copy-done.3, bf16[80,320,640]{2,1,0:T(8,128)(2,1)} %bitcast.127, bf16[2,160,320]{2,1,0:T(8,128)(2,1)} %fusion.29.refs_17_.refs_2_, ...), custom_call_target="tpu_custom_call" | custom-call | tf_op jit(solution)/shard_map/cond/branch_1_fun/middle/pallas_call | solution.py:293
  109.5 13.3 %all-to-all-start.3 = ((bf16[16,80,8,128]{3,2,1,0:T(8,128)(2,1)}), bf16[16,80,8,128]{3,2,1,0:T(8,128)(2,1)S(1)}, u32[]{:S(2)}, u32[]{:S(2)}) async-start(bf16[16,80,8,128]{3,2,1,0:T(8,128)(2,1)} %middle.7), calls=%async_computation.3 | async-start | bytes 5242880 | tf_op jit(solution)/shard_map/cond/branch_1_fun/all_to_all | solution.py:541
  122.9 18.8 %dft.6 = (bf16[1,94,8,128]{3,2,1,0:T(8,128)(2,1)}, bf16[1,94,8,128]{3,2,1,0:T(8,128)(2,1)}, bf16[1,94,8,128]{3,2,1,0:T(8,128)(2,1)}, bf16[1,94,8,128]{3,2,1,0:T(...) custom-call(s32[8,128]{1,0:T(8,128)S(1)} %get-tuple-element.110.lats, ...), custom_call_target="tpu_custom_call" | custom-call | tf_op jit(solution)/shard_map/cond/branch_1_fun/dft/pallas_call | solution.py:109
  150.9 4.7 %collective-permute-done.31.refs_2_ = bf16[1,94,8,128]{3,2,1,0:T(8,128)(2,1)S(1)} collective-permute-done((bf16[1,94,8,128]{3,2,1,0:T(8,128)(2,1)}, bf16[1,94,8,128]{3,2,1,0:T(8,128)(2,1)S(1)}, u32[]{:S(2)}, u32[]{:S(2)}) %collective-permute-start.31) | collective-permute-done | bytes 192544 | tf_op jit(solution)/shard_map/cond/branch_1_fun/ppermute | solution.py:454
  155.7 6.8 %collective-permute-done.32.refs_3_ = bf16[1,94,8,128]{3,2,1,0:T(8,128)(2,1)S(1)} collective-permute-done((bf16[1,94,8,128]{3,2,1,0:T(8,128)(2,1)}, bf16[1,94,8,128]{3,2,1,0:T(8,128)(2,1)S(1)}, u32[]{:S(2)}, u32[]{:S(2)}) %collective-permute-start.32) | collective-permute-done | bytes 192544 | tf_op jit(solution)/shard_map/cond/branch_1_fun/ppermute | solution.py:454
  162.5 12.4 %collective-permute-done.33.refs_4_ = bf16[1,94,8,128]{3,2,1,0:T(8,128)(2,1)S(1)} collective-permute-done((bf16[1,94,8,128]{3,2,1,0:T(8,128)(2,1)}, bf16[1,94,8,128]{3,2,1,0:T(8,128)(2,1)S(1)}, u32[]{:S(2)}, u32[]{:S(2)}) %collective-permute-start.33) | collective-permute-done | bytes 192544 | tf_op jit(solution)/shard_map/cond/branch_1_fun/ppermute | solution.py:454
  174.9 16.3 %collective-permute-start.38 = (bf16[1,94,8,128]{3,2,1,0:T(8,128)(2,1)}, bf16[1,94,8,128]{3,2,1,0:T(8,128)(2,1)}, u32[]{:S(2)}, u32[]{:S(2)}) collective-permute-start(bf16[1,94,8,128]{3,2,1,0:T(8,128)(2,1)} %get-tuple-element.122), channel_id=1, source_target_pairs={{0,9},{1,8},{2,11},{3,10},{4,13},{5,12},{6,15},{7,14},{8,1},{9,0},... | collective-permute-start | bytes 577544 | tf_op jit(solution)/shard_map/cond/branch_1_fun/ppermute | solution.py:454
  191.2 5.3 %collective-permute-start.39 = (bf16[1,94,8,128]{3,2,1,0:T(8,128)(2,1)}, bf16[1,94,8,128]{3,2,1,0:T(8,128)(2,1)}, u32[]{:S(2)}, u32[]{:S(2)}) collective-permute-start(bf16[1,94,8,128]{3,2,1,0:T(8,128)(2,1)} %get-tuple-element.123), channel_id=1, source_target_pairs={{0,10},{1,11},{2,8},{3,9},{4,14},{5,15},{6,12},{7,13},{8,2},{9,3},... | collective-permute-start | bytes 577544 | tf_op jit(solution)/shard_map/cond/branch_1_fun/ppermute | solution.py:454
  197.3 9.3 %collective-permute-start.40 = (bf16[1,94,8,128]{3,2,1,0:T(8,128)(2,1)}, bf16[1,94,8,128]{3,2,1,0:T(8,128)(2,1)}, u32[]{:S(2)}, u32[]{:S(2)}) collective-permute-start(bf16[1,94,8,128]{3,2,1,0:T(8,128)(2,1)} %get-tuple-element.124), channel_id=1, source_target_pairs={{0,11},{1,10},{2,9},{3,8},{4,15},{5,14},{6,13},{7,12},{8,3},{9,2},... | collective-permute-start | bytes 577544 | tf_op jit(solution)/shard_map/cond/branch_1_fun/ppermute | solution.py:454
  209.0 12.0 %collective-permute-done.37.refs_8_ = bf16[1,94,8,128]{3,2,1,0:T(8,128)(2,1)} collective-permute-done((bf16[1,94,8,128]{3,2,1,0:T(8,128)(2,1)}, bf16[1,94,8,128]{3,2,1,0:T(8,128)(2,1)}, u32[]{:S(2)}, u32[]{:S(2)}) %collective-permute-start.37) | collective-permute-done | bytes 192544 | tf_op jit(solution)/shard_map/cond/branch_1_fun/ppermute | solution.py:454
  221.1 4.1 %collective-permute-start.42 = (bf16[1,94,8,128]{3,2,1,0:T(8,128)(2,1)}, bf16[1,94,8,128]{3,2,1,0:T(8,128)(2,1)}, u32[]{:S(2)}, u32[]{:S(2)}) collective-permute-start(bf16[1,94,8,128]{3,2,1,0:T(8,128)(2,1)} %get-tuple-element.126), channel_id=1, source_target_pairs={{0,13},{1,12},{2,15},{3,14},{4,1},{5,0},{6,3},{7,2},{8,5},{9,4},{1... | collective-permute-start | bytes 577544 | tf_op jit(solution)/shard_map/cond/branch_1_fun/ppermute | solution.py:454
  225.2 5.2 %collective-permute-start.43 = (bf16[1,94,8,128]{3,2,1,0:T(8,128)(2,1)}, bf16[1,94,8,128]{3,2,1,0:T(8,128)(2,1)}, u32[]{:S(2)}, u32[]{:S(2)}) collective-permute-start(bf16[1,94,8,128]{3,2,1,0:T(8,128)(2,1)} %get-tuple-element.127), channel_id=1, source_target_pairs={{0,14},{1,15},{2,12},{3,13},{4,2},{5,3},{6,0},{7,1},{8,6},{9,7},{1... | collective-permute-start | bytes 577544 | tf_op jit(solution)/shard_map/cond/branch_1_fun/ppermute | solution.py:454
  230.4 12.2 %collective-permute-start.44 = (bf16[1,94,8,128]{3,2,1,0:T(8,128)(2,1)}, bf16[1,94,8,128]{3,2,1,0:T(8,128)(2,1)}, u32[]{:S(2)}, u32[]{:S(2)}) collective-permute-start(bf16[1,94,8,128]{3,2,1,0:T(8,128)(2,1)} %get-tuple-element.128), channel_id=1, source_target_pairs={{0,15},{1,14},{2,13},{3,12},{4,3},{5,2},{6,1},{7,0},{8,7},{9,6},{1... | collective-permute-start | bytes 577544 | tf_op jit(solution)/shard_map/cond/branch_1_fun/ppermute | solution.py:454
  243.2 4.1 %collective-permute-done.44.refs_15_ = bf16[1,94,8,128]{3,2,1,0:T(8,128)(2,1)} collective-permute-done((bf16[1,94,8,128]{3,2,1,0:T(8,128)(2,1)}, bf16[1,94,8,128]{3,2,1,0:T(8,128)(2,1)}, u32[]{:S(2)}, u32[]{:S(2)}) %collective-permute-start.44) | collective-permute-done | bytes 192544 | tf_op jit(solution)/shard_map/cond/branch_1_fun/ppermute | solution.py:454
  247.3 46.6 %middle.6 = (bf16[1,94,8,128]{3,2,1,0:T(8,128)(2,1)}, bf16[1,94,8,128]{3,2,1,0:T(8,128)(2,1)}, bf16[1,94,8,128]{3,2,1,0:T(8,128)(2,1)}, bf16[1,94,8,128]{3,2,1,0...) custom-call(s32[3,24]{1,0:T(4,128)} %slice.134.meta, ...), custom_call_target="tpu_custom_call" | custom-call | tf_op jit(solution)/shard_map/cond/branch_1_fun/middle/pallas_call | solution.py:293
  306.9 4.0 %collective-permute-start.56 = (bf16[1,94,8,128]{3,2,1,0:T(8,128)(2,1)}, bf16[1,94,8,128]{3,2,1,0:T(8,128)(2,1)S(1)}, u32[]{:S(2)}, u32[]{:S(2)}) collective-permute-start(bf16[1,94,8,128]{3,2,1,0:T(8,128)(2,1)} %get-tuple-element.145), channel_id=1, source_target_pairs={{0,12},{1,13},{2,14},{3,15},{4,0},{5,1},{6,2},{7,3},{8,4},{9,5},{1... | collective-permute-start | bytes 577544 | tf_op jit(solution)/shard_map/cond/branch_1_fun/ppermute | solution.py:454
  319.7 16.4 %collective-permute-start.45 = (bf16[1,94,8,128]{3,2,1,0:T(8,128)(2,1)}, bf16[1,94,8,128]{3,2,1,0:T(8,128)(2,1)S(1)}, u32[]{:S(2)}, u32[]{:S(2)}) collective-permute-start(bf16[1,94,8,128]{3,2,1,0:T(8,128)(2,1)} %get-tuple-element.133), channel_id=1, source_target_pairs={{0,8},{1,9},{2,10},{3,11},{4,12},{5,13},{6,14},{7,15},{8,0},{9,1},... | collective-permute-start | bytes 577544 | tf_op jit(solution)/shard_map/cond/branch_1_fun/ppermute | solution.py:454
  343.1 11.4 %place.9.refs_13_ = bf16[2560,1280]{1,0:T(8,128)(2,1)} custom-call(s32[40]{0:T(128)} %dynamic-slice_bitcast_fusion.1.rank, bf16[16,80,8,128]{3,2,1,0:T(8,128)(2,1)} %copy-done.5, s32[512,1]{1,0:T(8,128)} %add.578.refs_1_), custom_call_target="tpu_custom_call" | custom-call | tf_op jit(solution)/shard_map/cond/branch_1_fun/place/pallas_call | solution.py:398
  354.5 15.7 %place.10.refs_5_ = bf16[2560,1280]{1,0:T(8,128)(2,1)} custom-call(s32[40]{0:T(128)} %dynamic-slice_bitcast_fusion.1.rank, bf16[1,94,8,128]{3,2,1,0:T(8,128)(2,1)} %get-tuple-element.137.refs_0_, bf16[1,94,8,128]{3,2,1,0:T(8,128)(2,1)} %copy-done.20, bf16[1,94,8,128]{3,2,1,0:T(8,128)(2,1)} %copy-done.21, bf16[1,94,8,128]{3,2,1,0:T(8,128)(2,1)} %copy-done.22, ...), custom_call_target="tpu_custom_call" | custom-call | tf_op jit(solution)/shard_map/cond/branch_1_fun/place/pallas_call | solution.py:398
  371.7 9.7 %place.11 = bf16[32,40,2,1280]{3,2,1,0:T(2,128)(2,1)} custom-call(s32[40]{0:T(128)} %dynamic-slice_bitcast_fusion.1.rank, bf16[1,94,8,128]{3,2,1,0:T(8,128)(2,1)} %copy-done.16, bf16[1,94,8,128]{3,2,1,0:T(8,128)(2,1)} %copy-done.17, bf16[1,94,8,128]{3,2,1,0:T(8,128)(2,1)} %copy-done.18, bf16[1,94,8,128]{3,2,1,0:T(8,128)(2,1)} %copy-done.19, ...), custom_call_target="tpu_custom_call" | custom-call | tf_op jit(solution)/shard_map/cond/branch_1_fun/place/pallas_call | solution.py:398
  (187 shorter events, 57.3 us)
Async XLA Ops:
  19.2 57.7 %all-to-all-start.2 = ((bf16[16,80,8,128]{3,2,1,0:T(8,128)(2,1)}), bf16[16,80,8,128]{3,2,1,0:T(8,128)(2,1)S(1)}, u32[]{:S(2)}, u32[]{:S(2)}) async-start(bf16[16,80,8,128]{3,2,1,0:T(8,128)(2,1)} %dft.7), calls=%async_computation.2 | async-start | bytes 5242880 | tf_op jit(solution)/shard_map/cond/branch_1_fun/all_to_all | solution.py:541
  109.5 232.1 %all-to-all-start.3 = ((bf16[16,80,8,128]{3,2,1,0:T(8,128)(2,1)}), bf16[16,80,8,128]{3,2,1,0:T(8,128)(2,1)S(1)}, u32[]{:S(2)}, u32[]{:S(2)}) async-start(bf16[16,80,8,128]{3,2,1,0:T(8,128)(2,1)} %middle.7), calls=%async_computation.3 | async-start | bytes 5242880 | tf_op jit(solution)/shard_map/cond/branch_1_fun/all_to_all | solution.py:541
  143.8 18.7 %collective-permute-start.32 = (bf16[1,94,8,128]{3,2,1,0:T(8,128)(2,1)}, bf16[1,94,8,128]{3,2,1,0:T(8,128)(2,1)S(1)}, u32[]{:S(2)}, u32[]{:S(2)}) collective-permute-start(bf16[1,94,8,128]{3,2,1,0:T(8,128)(2,1)} %get-tuple-element.116), channel_id=1, source_target_pairs={{0,3},{1,2},{2,1},{3,0},{4,7},{5,6},{6,5},{7,4},{8,11},{9,10},{10,... | collective-permute-start | bytes 577544 | tf_op jit(solution)/shard_map/cond/branch_1_fun/ppermute | solution.py:454
  143.8 31.1 %collective-permute-start.33 = (bf16[1,94,8,128]{3,2,1,0:T(8,128)(2,1)}, bf16[1,94,8,128]{3,2,1,0:T(8,128)(2,1)S(1)}, u32[]{:S(2)}, u32[]{:S(2)}) collective-permute-start(bf16[1,94,8,128]{3,2,1,0:T(8,128)(2,1)} %get-tuple-element.117), channel_id=1, source_target_pairs={{0,4},{1,5},{2,6},{3,7},{4,8},{5,9},{6,10},{7,11},{8,12},{9,13},{1... | collective-permute-start | bytes 577544 | tf_op jit(solution)/shard_map/cond/branch_1_fun/ppermute | solution.py:454
  145.6 45.6 %collective-permute-start.34 = (bf16[1,94,8,128]{3,2,1,0:T(8,128)(2,1)}, bf16[1,94,8,128]{3,2,1,0:T(8,128)(2,1)}, u32[]{:S(2)}, u32[]{:S(2)}) collective-permute-start(bf16[1,94,8,128]{3,2,1,0:T(8,128)(2,1)} %get-tuple-element.118), channel_id=1, source_target_pairs={{0,5},{1,4},{2,7},{3,6},{4,9},{5,8},{6,11},{7,10},{8,13},{9,12},{1... | collective-permute-start | bytes 577544 | tf_op jit(solution)/shard_map/cond/branch_1_fun/ppermute | solution.py:454
  148.6 48.7 %collective-permute-start.35 = (bf16[1,94,8,128]{3,2,1,0:T(8,128)(2,1)}, bf16[1,94,8,128]{3,2,1,0:T(8,128)(2,1)}, u32[]{:S(2)}, u32[]{:S(2)}) collective-permute-start(bf16[1,94,8,128]{3,2,1,0:T(8,128)(2,1)} %get-tuple-element.119), channel_id=1, source_target_pairs={{0,6},{1,7},{2,4},{3,5},{4,10},{5,11},{6,8},{7,9},{8,14},{9,15},{1... | collective-permute-start | bytes 577544 | tf_op jit(solution)/shard_map/cond/branch_1_fun/ppermute | solution.py:454
  155.7 51.0 %collective-permute-start.36 = (bf16[1,94,8,128]{3,2,1,0:T(8,128)(2,1)}, bf16[1,94,8,128]{3,2,1,0:T(8,128)(2,1)}, u32[]{:S(2)}, u32[]{:S(2)}) collective-permute-start(bf16[1,94,8,128]{3,2,1,0:T(8,128)(2,1)} %get-tuple-element.120), channel_id=1, source_target_pairs={{0,7},{1,6},{2,5},{3,4},{4,11},{5,10},{6,9},{7,8},{8,15},{9,14},{1... | collective-permute-start | bytes 577544 | tf_op jit(solution)/shard_map/cond/branch_1_fun/ppermute | solution.py:454
  162.5 58.6 %collective-permute-start.37 = (bf16[1,94,8,128]{3,2,1,0:T(8,128)(2,1)}, bf16[1,94,8,128]{3,2,1,0:T(8,128)(2,1)}, u32[]{:S(2)}, u32[]{:S(2)}) collective-permute-start(bf16[1,94,8,128]{3,2,1,0:T(8,128)(2,1)} %get-tuple-element.121), channel_id=1, source_target_pairs={{0,8},{1,9},{2,10},{3,11},{4,12},{5,13},{6,14},{7,15},{8,0},{9,1},... | collective-permute-start | bytes 577544 | tf_op jit(solution)/shard_map/cond/branch_1_fun/ppermute | solution.py:454
  174.9 50.3 %collective-permute-start.38 = (bf16[1,94,8,128]{3,2,1,0:T(8,128)(2,1)}, bf16[1,94,8,128]{3,2,1,0:T(8,128)(2,1)}, u32[]{:S(2)}, u32[]{:S(2)}) collective-permute-start(bf16[1,94,8,128]{3,2,1,0:T(8,128)(2,1)} %get-tuple-element.122), channel_id=1, source_target_pairs={{0,9},{1,8},{2,11},{3,10},{4,13},{5,12},{6,15},{7,14},{8,1},{9,0},... | collective-permute-start | bytes 577544 | tf_op jit(solution)/shard_map/cond/branch_1_fun/ppermute | solution.py:454
  191.2 39.2 %collective-permute-start.39 = (bf16[1,94,8,128]{3,2,1,0:T(8,128)(2,1)}, bf16[1,94,8,128]{3,2,1,0:T(8,128)(2,1)}, u32[]{:S(2)}, u32[]{:S(2)}) collective-permute-start(bf16[1,94,8,128]{3,2,1,0:T(8,128)(2,1)} %get-tuple-element.123), channel_id=1, source_target_pairs={{0,10},{1,11},{2,8},{3,9},{4,14},{5,15},{6,12},{7,13},{8,2},{9,3},... | collective-permute-start | bytes 577544 | tf_op jit(solution)/shard_map/cond/branch_1_fun/ppermute | solution.py:454
  197.3 45.8 %collective-permute-start.40 = (bf16[1,94,8,128]{3,2,1,0:T(8,128)(2,1)}, bf16[1,94,8,128]{3,2,1,0:T(8,128)(2,1)}, u32[]{:S(2)}, u32[]{:S(2)}) collective-permute-start(bf16[1,94,8,128]{3,2,1,0:T(8,128)(2,1)} %get-tuple-element.124), channel_id=1, source_target_pairs={{0,11},{1,10},{2,9},{3,8},{4,15},{5,14},{6,13},{7,12},{8,3},{9,2},... | collective-permute-start | bytes 577544 | tf_op jit(solution)/shard_map/cond/branch_1_fun/ppermute | solution.py:454
  206.6 36.6 %collective-permute-start.41 = (bf16[1,94,8,128]{3,2,1,0:T(8,128)(2,1)}, bf16[1,94,8,128]{3,2,1,0:T(8,128)(2,1)}, u32[]{:S(2)}, u32[]{:S(2)}) collective-permute-start(bf16[1,94,8,128]{3,2,1,0:T(8,128)(2,1)} %get-tuple-element.125), channel_id=1, source_target_pairs={{0,12},{1,13},{2,14},{3,15},{4,0},{5,1},{6,2},{7,3},{8,4},{9,5},{1... | collective-permute-start | bytes 577544 | tf_op jit(solution)/shard_map/cond/branch_1_fun/ppermute | solution.py:454
  221.1 22.1 %collective-permute-start.42 = (bf16[1,94,8,128]{3,2,1,0:T(8,128)(2,1)}, bf16[1,94,8,128]{3,2,1,0:T(8,128)(2,1)}, u32[]{:S(2)}, u32[]{:S(2)}) collective-permute-start(bf16[1,94,8,128]{3,2,1,0:T(8,128)(2,1)} %get-tuple-element.126), channel_id=1, source_target_pairs={{0,13},{1,12},{2,15},{3,14},{4,1},{5,0},{6,3},{7,2},{8,5},{9,4},{1... | collective-permute-start | bytes 577544 | tf_op jit(solution)/shard_map/cond/branch_1_fun/ppermute | solution.py:454
  225.2 18.0 %collective-permute-start.43 = (bf16[1,94,8,128]{3,2,1,0:T(8,128)(2,1)}, bf16[1,94,8,128]{3,2,1,0:T(8,128)(2,1)}, u32[]{:S(2)}, u32[]{:S(2)}) collective-permute-start(bf16[1,94,8,128]{3,2,1,0:T(8,128)(2,1)} %get-tuple-element.127), channel_id=1, source_target_pairs={{0,14},{1,15},{2,12},{3,13},{4,2},{5,3},{6,0},{7,1},{8,6},{9,7},{1... | collective-permute-start | bytes 577544 | tf_op jit(solution)/shard_map/cond/branch_1_fun/ppermute | solution.py:454
  230.4 16.8 %collective-permute-start.44 = (bf16[1,94,8,128]{3,2,1,0:T(8,128)(2,1)}, bf16[1,94,8,128]{3,2,1,0:T(8,128)(2,1)}, u32[]{:S(2)}, u32[]{:S(2)}) collective-permute-start(bf16[1,94,8,128]{3,2,1,0:T(8,128)(2,1)} %get-tuple-element.128), channel_id=1, source_target_pairs={{0,15},{1,14},{2,13},{3,12},{4,3},{5,2},{6,1},{7,0},{8,7},{9,6},{1... | collective-permute-start | bytes 577544 | tf_op jit(solution)/shard_map/cond/branch_1_fun/ppermute | solution.py:454
  299.2 17.5 %collective-permute-start.54 = (bf16[1,94,8,128]{3,2,1,0:T(8,128)(2,1)}, bf16[1,94,8,128]{3,2,1,0:T(8,128)(2,1)S(1)}, u32[]{:S(2)}, u32[]{:S(2)}) collective-permute-start(bf16[1,94,8,128]{3,2,1,0:T(8,128)(2,1)} %get-tuple-element.143), channel_id=1, source_target_pairs={{0,6},{1,7},{2,4},{3,5},{4,10},{5,11},{6,8},{7,9},{8,14},{9,15},{1... | collective-permute-start | bytes 577544 | tf_op jit(solution)/shard_map/cond/branch_1_fun/ppermute | solution.py:454
  306.9 29.3 %collective-permute-start.56 = (bf16[1,94,8,128]{3,2,1,0:T(8,128)(2,1)}, bf16[1,94,8,128]{3,2,1,0:T(8,128)(2,1)S(1)}, u32[]{:S(2)}, u32[]{:S(2)}) collective-permute-start(bf16[1,94,8,128]{3,2,1,0:T(8,128)(2,1)} %get-tuple-element.145), channel_id=1, source_target_pairs={{0,12},{1,13},{2,14},{3,15},{4,0},{5,1},{6,2},{7,3},{8,4},{9,5},{1... | collective-permute-start | bytes 577544 | tf_op jit(solution)/shard_map/cond/branch_1_fun/ppermute | solution.py:454
  310.9 25.3 %collective-permute-start.57 = (bf16[1,94,8,128]{3,2,1,0:T(8,128)(2,1)}, bf16[1,94,8,128]{3,2,1,0:T(8,128)(2,1)S(1)}, u32[]{:S(2)}, u32[]{:S(2)}) collective-permute-start(bf16[1,94,8,128]{3,2,1,0:T(8,128)(2,1)} %get-tuple-element.146), channel_id=1, source_target_pairs={{0,13},{1,12},{2,15},{3,14},{4,1},{5,0},{6,3},{7,2},{8,5},{9,4},{1... | collective-permute-start | bytes 577544 | tf_op jit(solution)/shard_map/cond/branch_1_fun/ppermute | solution.py:454
  311.3 26.4 %collective-permute-start.58 = (bf16[1,94,8,128]{3,2,1,0:T(8,128)(2,1)}, bf16[1,94,8,128]{3,2,1,0:T(8,128)(2,1)}, u32[]{:S(2)}, u32[]{:S(2)}) collective-permute-start(bf16[1,94,8,128]{3,2,1,0:T(8,128)(2,1)} %get-tuple-element.147), channel_id=1, source_target_pairs={{0,14},{1,15},{2,12},{3,13},{4,2},{5,3},{6,0},{7,1},{8,6},{9,7},{1... | collective-permute-start | bytes 577544 | tf_op jit(solution)/shard_map/cond/branch_1_fun/ppermute | solution.py:454
  316.8 37.8 %collective-permute-start.59 = (bf16[1,94,8,128]{3,2,1,0:T(8,128)(2,1)}, bf16[1,94,8,128]{3,2,1,0:T(8,128)(2,1)}, u32[]{:S(2)}, u32[]{:S(2)}) collective-permute-start(bf16[1,94,8,128]{3,2,1,0:T(8,128)(2,1)} %get-tuple-element.148), channel_id=1, source_target_pairs={{0,15},{1,14},{2,13},{3,12},{4,3},{5,2},{6,1},{7,0},{8,7},{9,6},{1... | collective-permute-start | bytes 577544 | tf_op jit(solution)/shard_map/cond/branch_1_fun/ppermute | solution.py:454
  319.7 50.5 %collective-permute-start.45 = (bf16[1,94,8,128]{3,2,1,0:T(8,128)(2,1)}, bf16[1,94,8,128]{3,2,1,0:T(8,128)(2,1)S(1)}, u32[]{:S(2)}, u32[]{:S(2)}) collective-permute-start(bf16[1,94,8,128]{3,2,1,0:T(8,128)(2,1)} %get-tuple-element.133), channel_id=1, source_target_pairs={{0,8},{1,9},{2,10},{3,11},{4,12},{5,13},{6,14},{7,15},{8,0},{9,1},... | collective-permute-start | bytes 577544 | tf_op jit(solution)/shard_map/cond/branch_1_fun/ppermute | solution.py:454
  336.2 34.0 %collective-permute-start.46 = (bf16[1,94,8,128]{3,2,1,0:T(8,128)(2,1)}, bf16[1,94,8,128]{3,2,1,0:T(8,128)(2,1)S(1)}, u32[]{:S(2)}, u32[]{:S(2)}) collective-permute-start(bf16[1,94,8,128]{3,2,1,0:T(8,128)(2,1)} %get-tuple-element.134), channel_id=1, source_target_pairs={{0,9},{1,8},{2,11},{3,10},{4,13},{5,12},{6,15},{7,14},{8,1},{9,0},... | collective-permute-start | bytes 577544 | tf_op jit(solution)/shard_map/cond/branch_1_fun/ppermute | solution.py:454
  336.9 33.4 %collective-permute-start.47 = (bf16[1,94,8,128]{3,2,1,0:T(8,128)(2,1)}, bf16[1,94,8,128]{3,2,1,0:T(8,128)(2,1)S(1)}, u32[]{:S(2)}, u32[]{:S(2)}) collective-permute-start(bf16[1,94,8,128]{3,2,1,0:T(8,128)(2,1)} %get-tuple-element.135), channel_id=1, source_target_pairs={{0,10},{1,11},{2,8},{3,9},{4,14},{5,15},{6,12},{7,13},{8,2},{9,3},... | collective-permute-start | bytes 577544 | tf_op jit(solution)/shard_map/cond/branch_1_fun/ppermute | solution.py:454
  337.6 32.6 %collective-permute-start.48 = (bf16[1,94,8,128]{3,2,1,0:T(8,128)(2,1)}, bf16[1,94,8,128]{3,2,1,0:T(8,128)(2,1)S(1)}, u32[]{:S(2)}, u32[]{:S(2)}) collective-permute-start(bf16[1,94,8,128]{3,2,1,0:T(8,128)(2,1)} %get-tuple-element.136), channel_id=1, source_target_pairs={{0,11},{1,10},{2,9},{3,8},{4,15},{5,14},{6,13},{7,12},{8,3},{9,2},... | collective-permute-start | bytes 577544 | tf_op jit(solution)/shard_map/cond/branch_1_fun/ppermute | solution.py:454
  (34 other events, 597.8 us)
